TPU v7x, 128 devices: a whole 4x4x4 slice. The times are simulated.
128 devices in a mesh: ctx: 16 (over z, y), exp: 8 (over x, core).
Axes of the slice: x: 4, y: 4, z: 4, core: 2. Of those that a mesh axis runs over, the one named last changes fastest.
Arguments:
- queries: bfloat16 [16384, 16, 128], P('ctx', 'exp'), may hold values from -6 to 6
- key_vectors: bfloat16 [16384, 16, 128], P('ctx', 'exp'), may hold values from -6 to 6
- values: bfloat16 [16384, 32, 128], P('ctx', 'exp'), may hold values from -6 to 6
- out_gate: bfloat16 [16384, 32, 128], P('ctx', 'exp'), may hold values from -6 to 6
- write_strength: float32 [32, 16384], P('exp', 'ctx'), may hold values from 0.001 to 0.9
- decay_logarithm: float32 [32, 16384], P('exp', 'ctx'), may hold values from -0.75 to 0
- residual: bfloat16 [16384, 2048], P(('ctx', 'exp')), may hold values from -6 to 6
- out_weight: bfloat16 [4096, 2048], P('exp'), may hold values from -0.09375 to 0.09375
- head_gain: float32 [128], replicated, may hold values from 0.1 to 1.9
- post_gain: float32 [2048], replicated, may hold values from 0.1 to 1.9
- gate_proj: bfloat16 [256, 2048, 512], P(('ctx', 'exp')), may hold values from -0.125 to 0.125
- up_proj: bfloat16 [256, 2048, 512], P(('ctx', 'exp')), may hold values from -0.125 to 0.125
- down_proj: bfloat16 [256, 512, 2048], P(('ctx', 'exp')), may hold values from -0.25 to 0.25
- expert_ids: int32 [16384, 10], P(('ctx', 'exp')), may hold values from 0 to 255, all different within a row; in each aligned block of 128 rows (0 to 127, 128 to 255, ...) at most 10 rows name the same one
- route_gates: float32 [16384, 10], P(('ctx', 'exp')), may hold values from 0.02 to 0.3
Outputs:
- attended: bfloat16 [16384, 2048], P(('ctx', 'exp'))
- expert_mix: bfloat16 [16384, 2048], P(('ctx', 'exp'))
Inputs may be any that keep to these rules, and one draw needn't show every extreme that they name: `expert_ids`: the 10 ids of a row differ. Among the rows of one device no id appears more than 10 times, and some id appears exactly 10 times.
All inputs are finite; a program needn't handle non-finite values.
Results may differ from a plain program's by a relative error of at most 0.025.
Values may be sent and summed in bfloat16 or wider, within the bound.
No kernel may reach another device: no remote copies, remote signals or barrier semaphores. Data moves between devices by JAX's collectives and lax.ppermute only.
A program may use at most 192 MiB of HBM per device.

v0:
```python
import jax
import jax.numpy as jnp
from jax import lax
from jax.sharding import PartitionSpec as P

SPAN = 64


highest = lax.Precision.HIGHEST


def prefix(part, axis, combine, identity):
    place = lax.axis_index(axis)
    gathered = jax.tree.map(lambda a: lax.all_gather(a, axis), part)
    state = jax.tree.map(lambda a, e: jnp.zeros_like(a) + jnp.asarray(e, a.dtype), part, identity)

    def one(step, state):
        return combine(
            state, jax.tree.map(lambda a: lax.dynamic_index_in_dim(a, step, 0, False), gathered)
        )

    return lax.fori_loop(0, place, one, state)


def unit_rows(tensor, multiplier):
    return tensor * multiplier / jnp.sqrt(jnp.sum(tensor * tensor, axis=-1, keepdims=True) + 1e-06)


def solve_span(key_rows, strength, cumulative):
    span_len = key_rows.shape[-2]
    gram = jnp.einsum("...id,...jd->...ij", key_rows, key_rows, precision=highest)
    strict = jnp.tril(jnp.ones((span_len, span_len), jnp.bool_), -1)
    lower = jnp.where(
        strict,
        strength[..., :, None]
        * gram
        * jnp.exp(jnp.where(strict, cumulative[..., :, None] - cumulative[..., None, :], 0.0)),
        0.0,
    )
    eye_span = jnp.eye(span_len, dtype=jnp.float32)
    power = -lower
    inverse = eye_span + power
    reach = 2
    while reach < span_len:
        power = jnp.einsum("...ij,...jk->...ik", power, power, precision=highest)
        inverse = jnp.einsum("...ij,...jk->...ik", inverse, eye_span + power, precision=highest)
        reach = reach * 2
    return inverse


def by_blocks(tensor, block_len):
    seq_length, head_count, feature_len = tensor.shape
    return tensor.reshape(seq_length // block_len, block_len, head_count, feature_len).transpose(
        2, 0, 1, 3
    )


def chain(earlier, latter):
    joined_map = jnp.einsum("hde,hef->hdf", latter[0], earlier[0], precision=highest)
    joined_state = jnp.einsum("hde,hef->hdf", latter[0], earlier[1], precision=highest) + latter[1]
    return (joined_map, joined_state)


def compose(running, member):
    acc_map, acc_state = running
    step_map, step_state = member
    new_map = jnp.einsum("hde,hef->hdf", step_map, acc_map, precision=highest)
    new_state = jnp.einsum("hde,hef->hdf", step_map, acc_state, precision=highest) + step_state
    return ((new_map, new_state), (acc_map, acc_state))


def advance(state_now, member):
    decayed_query, mixing_n, weight_rows, write_rows, tail_keys, closing_n = member
    fresh_rows = write_rows - jnp.einsum("hid,hde->hie", weight_rows, state_now, precision=highest)
    output = jnp.einsum("hid,hde->hie", decayed_query, state_now, precision=highest)
    output = output + jnp.einsum("hij,hje->hie", mixing_n, fresh_rows, precision=highest)
    state_now = jnp.exp(closing_n)[..., None] * state_now + jnp.einsum(
        "hjd,hje->hde", tail_keys, fresh_rows, precision=highest
    )
    return (state_now, output)


def shards(
    queries,
    key_vectors,
    values,
    out_gate,
    write_strength,
    decay_logarithm,
    residual,
    out_weight,
    head_gain,
    post_gain,
    gate_proj,
    up_proj,
    down_proj,
    expert_ids,
    route_gates,
):
    block_len = SPAN
    seq_length = queries.shape[0]
    head_count = values.shape[1]
    head_group = head_count // queries.shape[1]
    key_dim = queries.shape[2]
    value_dim = values.shape[2]
    block_number = seq_length // block_len
    query_rows = jnp.repeat(
        unit_rows(queries.astype(jnp.float32), key_dim ** (-0.5)), head_group, axis=1
    )
    key_rows = jnp.repeat(unit_rows(key_vectors.astype(jnp.float32), 1.0), head_group, axis=1)
    query_blocks = by_blocks(query_rows, block_len)
    key_blocks = by_blocks(key_rows, block_len)
    value_blocks = by_blocks(values.astype(jnp.float32), block_len)
    strength = write_strength.reshape(head_count, block_number, block_len)
    cumulative = jnp.cumsum(decay_logarithm.reshape(head_count, block_number, block_len), axis=-1)
    inverse = solve_span(key_blocks, strength, cumulative)
    weighted = jnp.einsum(
        "hnij,hnjd->hnid",
        inverse,
        (strength * jnp.exp(cumulative))[..., None] * key_blocks,
        precision=highest,
    )
    written = jnp.einsum(
        "hnij,hnjd->hnid", inverse, strength[..., None] * value_blocks, precision=highest
    )
    closing = cumulative[..., -1:]
    tail_keys = key_blocks * jnp.exp(closing - cumulative)[..., None]
    causal = jnp.tril(jnp.ones((block_len, block_len), jnp.bool_))
    spread_mat = jnp.where(
        causal,
        jnp.exp(jnp.where(causal, cumulative[..., :, None] - cumulative[..., None, :], 0.0)),
        0.0,
    )
    mixing = jnp.einsum("hnid,hnjd->hnij", query_blocks, key_blocks, precision=highest) * spread_mat
    query_decayed = query_blocks * jnp.exp(cumulative)[..., None]
    eye_map = jnp.eye(key_dim, dtype=jnp.float32)
    transit = jnp.exp(closing)[..., None] * eye_map - jnp.einsum(
        "hncd,hnce->hnde", tail_keys, weighted, precision=highest
    )
    deposit = jnp.einsum("hncd,hnce->hnde", tail_keys, written, precision=highest)
    initial = (
        jnp.broadcast_to(eye_map, (head_count, key_dim, key_dim)),
        jnp.zeros((head_count, key_dim, value_dim), jnp.float32),
    )
    (device_map, device_state), (before_map, before_state) = lax.scan(
        compose, initial, (jnp.moveaxis(transit, 1, 0), jnp.moveaxis(deposit, 1, 0))
    )
    carried_map, carried_state = prefix((device_map, device_state), "ctx", chain, initial)
    scan_items = (
        jnp.moveaxis(query_decayed, 1, 0),
        jnp.moveaxis(mixing, 1, 0),
        jnp.moveaxis(weighted, 1, 0),
        jnp.moveaxis(written, 1, 0),
        jnp.moveaxis(tail_keys, 1, 0),
        jnp.moveaxis(closing, 1, 0),
    )
    final_state, outputs = lax.scan(advance, carried_state, scan_items)
    core_out = jnp.moveaxis(outputs, 0, 1)
    core_out = core_out.reshape(head_count, seq_length, value_dim).transpose(1, 0, 2)
    root_mean = jnp.sqrt(jnp.mean(core_out * core_out, axis=-1, keepdims=True) + 1e-06)
    gated = (core_out / root_mean * head_gain * jax.nn.silu(out_gate.astype(jnp.float32))).astype(
        jnp.bfloat16
    )
    gated = gated.reshape(seq_length, head_count * value_dim)
    tok_count = residual.shape[0]
    attn_out = lax.psum_scatter(
        jnp.dot(gated, out_weight, preferred_element_type=jnp.float32).astype(jnp.bfloat16),
        "exp",
        scatter_dimension=0,
        tiled=True,
    ).astype(jnp.float32)
    attended = (residual.astype(jnp.float32) + attn_out).astype(jnp.bfloat16)
    settled = lax.optimization_barrier(attended).astype(jnp.float32)
    normed = (
        settled / jnp.sqrt(jnp.mean(settled * settled, axis=-1, keepdims=True) + 1e-06) * post_gain
    ).astype(jnp.bfloat16)
    ctx_count = lax.axis_size("ctx")
    exp_count = lax.axis_size("exp")
    dev_count = ctx_count * exp_count
    local_experts = gate_proj.shape[0]
    expert_count = local_experts * dev_count
    top_count = expert_ids.shape[1]
    model_width = normed.shape[1]
    capacity = max(2, (2 * tok_count * top_count + expert_count - 1) // expert_count)
    expert_hits = jnp.zeros((tok_count, expert_count), jnp.int32)
    expert_iota = lax.iota(jnp.int32, expert_count)
    for which_pick in range(top_count):
        expert_hits = expert_hits + (
            expert_ids[:, which_pick, None] == expert_iota[None, :]
        ).astype(jnp.int32)
    earlier_hits = jnp.cumsum(expert_hits, axis=0, dtype=jnp.int32) - expert_hits
    slot_rank = jnp.take_along_axis(earlier_hits, expert_ids, axis=1)
    slot_index = expert_ids * capacity + slot_rank
    token_index = jnp.repeat(lax.iota(jnp.int32, tok_count), top_count)
    owner_rows = (
        jnp.full((expert_count * capacity,), tok_count, jnp.int32)
        .at[slot_index.reshape(-1)]
        .set(token_index)
    )
    padded = jnp.concatenate([normed, jnp.zeros((1, model_width), jnp.bfloat16)], axis=0)
    outgoing = padded[owner_rows]
    shaped = outgoing.reshape(dev_count, local_experts, capacity, model_width)
    slot_block = lax.all_to_all(shaped, ("ctx", "exp"), split_axis=0, concat_axis=0, tiled=True)
    gate_part = jnp.einsum(
        "sxcd,xdf->sxcf", slot_block, gate_proj, preferred_element_type=jnp.float32
    )
    up_part = jnp.einsum("sxcd,xdf->sxcf", slot_block, up_proj, preferred_element_type=jnp.float32)
    inner_act = (jax.nn.silu(gate_part) * up_part).astype(jnp.bfloat16)
    returned = lax.all_to_all(
        jnp.einsum(
            "sxcf,xfd->sxcd", inner_act, down_proj, preferred_element_type=jnp.float32
        ).astype(jnp.bfloat16),
        ("ctx", "exp"),
        split_axis=0,
        concat_axis=0,
        tiled=True,
    )
    picked = returned.reshape(expert_count * capacity, model_width)[slot_index]
    mixture = jnp.sum(route_gates[:, :, None] * picked.astype(jnp.float32), axis=1)
    return (attended, mixture.astype(jnp.bfloat16))


def solution(mesh):
    in_specs = (
        P("ctx", "exp", None),
        P("ctx", "exp", None),
        P("ctx", "exp", None),
        P("ctx", "exp", None),
        P("exp", "ctx"),
        P("exp", "ctx"),
        P(("ctx", "exp"), None),
        P("exp", None),
        P(),
        P(),
        P(("ctx", "exp"), None, None),
        P(("ctx", "exp"), None, None),
        P(("ctx", "exp"), None, None),
        P(("ctx", "exp"), None),
        P(("ctx", "exp"), None),
    )
    out_specs = (P(("ctx", "exp"), None), P(("ctx", "exp"), None))
    return jax.shard_map(shards, mesh=mesh, in_specs=in_specs, out_specs=out_specs, check_vma=False)
```

profile of v0, /device:TPU:1, one launch (start us, length us, event | category | flops | bytes accessed | tf_op | source)
XLA Modules:
  0.0 848.5 jit_solution(12639324011751579820)
XLA Ops:
  7.3 2.4 fusion.68
  9.9 2.5 convert_divide_fusion.1
  16.3 3.6 select_negate_fusion
  19.9 2.2 fusion.90
  22.1 2.3 fusion.91
  24.4 2.3 fusion.62
  26.7 2.8 fusion.92
  29.5 2.3 fusion.60
  31.8 2.3 fusion.93
  34.1 2.2 fusion.58
  36.3 2.3 fusion.94
  38.7 2.4 fusion.56
  41.4 2.2 fusion.54
  43.7 3.6 fusion.52
  47.2 3.5 fusion.50
  50.8 12.0 %convolution_bitcast_fusion = f32[16,4,128,128]{3,2,0,1:T(8,128)} fusion(f32[4,16,64,128]{3,2,1,0:T(8,128)} %fusion.50, f32[4,16,64,128]{3,2,1,0:T(8,128)} %bitcast.224, f32[4,16,64]{2,1,0:T(8,128)S(1)} %get-tuple-element.272), kind=kOutput, calls=%fused_computation.62 | convolution fusion | flops 805830656 | bytes 8404992 | tf_op jit(solution)/shard_map/hncd,hnce->hnde/dot_general | solution.py:140
  62.8 9.2 %bitcast_subtract_fusion = f32[16,4,128,128]{3,2,0,1:T(8,128)} fusion(f32[4,16,64,128]{3,2,1,0:T(8,128)S(1)} %copy-done.6, f32[128,128]{1,0:T(8,128)S(1)} %fusion.83, f32[16,4]{0,1:T(4,128)S(1)} %bitcast.238, f32[4,16,64,128]{3,2,1,0:T(8,128)S(1)} %bitcast.225, f32[4,16,64]{2,1,0:T(8,128)S(1)} %get-tuple-element.272), kind=kOutput, calls=%fused_computation.57 | convolution fusion | flops 807927808 | bytes 8470784 | tf_op jit(solution)/shard_map/hncd,hnce->hnde/dot_general | solution.py:137
  72.0 46.0 %while.39 = (s32[]{:T(128)}, f32[4,128,128]{2,1,0:T(8,128)S(1)}, f32[4,128,128]{2,1,0:T(8,128)S(1)}, f32[16,4,128,128]{3,2,0,1:T(8,128)}, f32[16,4,128,128]{3,2,0,1:T(8,128)}, /*index=5*/s32[]{:T(128)}, s32[]{:T(128)}) while((s32[]{:T(128)}, f32[4,128,128]{2,1,0:T(8,128)S(1)}, f32[4,128,128]{2,1,0:T(8,128)S(1)}, ...), condition=%wide.region_3.4_spmd.clone, body=%wide.region_2.0_spmd.clone.sunk | while | flops 201457664 | bytes 2885207 | solution.py:145
  120.8 2.5 fusion.69
  125.2 4.8 bitcast_multiply_fusion.3
  130.0 2.6 broadcast_multiply_fusion
  132.6 41.1 %all-gather.5.cloned.1.call-done = f32[64,128,128]{2,1,0:T(8,128)} async-done(((f32[4,128,128]{2,1,0:T(8,128)}), f32[64,128,128]{2,1,0:T(8,128)}) %all-gather.5.cloned.1.call-update) | async-done | bytes 4194320 | tf_op jit(solution)/shard_map/all_gather | solution.py:14
  173.7 54.0 %all-gather.7.cloned.1.call-done = f32[64,128,128]{2,1,0:T(8,128)} async-done(((f32[4,128,128]{2,1,0:T(8,128)}), f32[64,128,128]{2,1,0:T(8,128)}) %all-gather.7.cloned.1.call-update) | async-done | bytes 4194320 | tf_op jit(solution)/shard_map/all_gather | solution.py:14
  227.8 96.4 %while.38 = (s32[]{:T(128)}, f32[4,128,128]{2,1,0:T(8,128)S(1)}, f32[16,4,64,128]{3,2,0,1:T(8,128)}, f32[16,4,1]{1,2,0:T(1,128)S(1)}, f32[16,4,64,128]{3,2,0,1:T...) while((s32[]{:T(128)}, f32[4,128,128]{2,1,0:T(8,128)S(1)}, ...), condition=%wide.region_8.9_spmd, body=%wide.region_7.8_spmd.sunk | while | flops 176357376 | bytes 2493593 | solution.py:157
  230.5 1.9 fusion.155
  232.4 1.5 convolution_add_fusion.8
  236.5 1.9 fusion.155
  242.5 1.9 fusion.155
  244.4 1.5 convolution_add_fusion.8
  248.5 1.9 fusion.155
  254.5 1.9 fusion.155
  256.4 1.5 convolution_add_fusion.8
  260.5 2.0 fusion.155
  266.5 1.9 fusion.155
  272.6 1.9 fusion.155
  278.6 1.9 fusion.155
  284.6 2.0 fusion.155
  290.6 2.0 fusion.155
  296.7 1.9 fusion.155
  302.7 2.0 fusion.155
  308.7 1.9 fusion.155
  314.7 1.9 fusion.155
  320.7 1.9 fusion.155
  324.2 2.4 fusion.48
  326.6 2.1 fusion.65
  330.0 5.5 convolution_convert_fusion
  337.2 10.1 %gather_fusion.2 = s32[1280]{0:T(1024)S(1)} fusion(s32[128,256]{1,0:T(8,128)S(1)} %fusion.89, s32[1280]{0:T(1024)S(1)} %reshape.169), kind=kCustom, calls=%fused_computation.2 | custom fusion | bytes 20480 | tf_op jit(solution)/shard_map/jit(take_along_axis)/gather | solution.py:192
  348.1 5.3 scatter_custom_fusion
  353.3 38.3 %reduce-scatter.2.cloned.1.call-done = bf16[128,2048]{1,0:T(8,128)(2,1)} async-done(((bf16[1024,2048]{1,0:T(8,128)(2,1)}), bf16[128,2048]{1,0:T(8,128)(2,1)}) %reduce-scatter.2.cloned.1.call-update) | async-done | bytes 524304 | tf_op jit(solution)/shard_map/reduce_scatter | solution.py:166
  393.3 10.8 %gather_fusion = bf16[2560,2048]{1,0:T(8,128)(2,1)} fusion(bf16[129,2048]{1,0:T(8,128)(2,1)S(1)} %concatenate.3, s32[3072]{0:T(1024)S(1)} %pad_clamp_fusion), kind=kCustom, calls=%fused_computation | custom fusion | bytes 20981760 | tf_op jit(solution)/shard_map/gather | solution.py:201
  404.0 17.6 %reshape.150 = bf16[128,2,10,2048]{3,2,1,0:T(8,128)(2,1)} reshape(bf16[2560,2048]{1,0:T(8,128)(2,1)} %gather_fusion) | data formatting | bytes 20971520 | tf_op jit(solution)/shard_map/reshape | solution.py:202
  421.7 19.3 %copy.153 = bf16[128,2,10,2048]{3,1,2,0:T(2,128)(2,1)S(1)} copy(bf16[128,2,10,2048]{3,2,1,0:T(8,128)(2,1)} %reshape.150) | data formatting | bytes 20971520 | tf_op jit(solution)/shard_map/reshape | solution.py:202
  440.9 130.7 %all_to_all.10 = bf16[128,2,10,2048]{3,1,2,0:T(2,128)(2,1)S(1)} all-to-all(bf16[128,2,10,2048]{3,1,2,0:T(2,128)(2,1)S(1)} %copy.153), channel_id=1, replica_groups=mesh['ctx'=16,'exp'=8] {'ctx','exp'}, dimensions={0} | all-to-all | bytes 20971520 | tf_op jit(solution)/shard_map/all_to_all | solution.py:203
  571.6 14.6 %fusion.31 = f32[2,128,10,512]{3,1,2,0:T(8,128)} fusion(bf16[128,2,10,2048]{3,1,2,0:T(2,128)(2,1)S(1)} %all_to_all.10, bf16[2,2048,512]{2,1,0:T(8,128)(2,1)S(1)} %copy-done.20), kind=kOutput, calls=%fused_computation.43 | convolution fusion | flops 5368709120 | bytes 19922944 | tf_op jit(solution)/shard_map/sxcd,xdf->sxcf/dot_general | solution.py:207
  586.2 15.2 %fusion.33 = f32[2,128,10,512]{3,1,2,0:T(8,128)} fusion(bf16[128,2,10,2048]{3,1,2,0:T(2,128)(2,1)S(1)} %all_to_all.10, bf16[2,2048,512]{2,1,0:T(8,128)(2,1)S(1)} %copy-done.21), kind=kOutput, calls=%fused_computation.45 | convolution fusion | flops 5368709120 | bytes 19922944 | tf_op jit(solution)/shard_map/sxcd,xdf->sxcf/dot_general | solution.py:204
  601.4 10.0 %convert_bitcast_fusion = bf16[128,2,10,2048]{3,0,2,1:T(8,128)(2,1)S(1)} fusion(bf16[2,512,2048]{2,1,0:T(8,128)(2,1)S(1)} %copy-done.22, f32[2,128,10,512]{3,1,2,0:T(8,128)} %fusion.31, f32[2,128,10,512]{3,1,2,0:T(8,128)} %fusion.33), kind=kOutput, calls=%fused_computation.42 | convolution fusion | flops 5381816320 | bytes 25165824 | tf_op jit(solution)/shard_map/sxcf,xfd->sxcd/dot_general | solution.py:210
  611.4 29.6 %copy.156 = bf16[128,2,10,2048]{3,1,2,0:T(2,128)(2,1)} copy(bf16[128,2,10,2048]{3,0,2,1:T(8,128)(2,1)S(1)} %convert_bitcast_fusion) | data formatting | bytes 20971520 | tf_op jit(solution)/shard_map/convert_element_type | solution.py:212
  641.0 6.1 all-to-all-start.1
  647.5 125.0 %all-to-all-done.1 = bf16[128,2,10,2048]{3,1,2,0:T(2,128)(2,1)} async-done(((bf16[128,2,10,2048]{3,1,2,0:T(2,128)(2,1)}), bf16[128,2,10,2048]{3,1,2,0:T(2,128)(2,1)}, u32[]{:S(2)}, u32[]{:S(2)}) %all-to-all-start.1) | async-done | bytes 10485792 | tf_op jit(solution)/shard_map/all_to_all | solution.py:209
  772.5 14.1 %copy.157 = bf16[128,2,10,2048]{3,2,1,0:T(8,128)(2,1)} copy(bf16[128,2,10,2048]{3,1,2,0:T(2,128)(2,1)} %all-to-all-done.1) | data formatting | bytes 20971520 | tf_op jit(solution)/shard_map/all_to_all | solution.py:209
  786.6 18.1 %reshape.151 = bf16[2560,2048]{1,0:T(8,128)(2,1)} reshape(bf16[128,2,10,2048]{3,2,1,0:T(8,128)(2,1)} %copy.157) | data formatting | bytes 20971520 | tf_op jit(solution)/shard_map/reshape | solution.py:218
  804.7 16.1 %gather_fusion.1 = bf16[1280,2048]{1,0:T(8,128)(2,1)} fusion(bf16[2560,2048]{1,0:T(8,128)(2,1)} %reshape.151, s32[2048]{0:T(1024)S(1)} %pad_clamp_fusion.1), kind=kCustom, calls=%fused_computation.1 | custom fusion | bytes 10490880 | tf_op jit(solution)/shard_map/gather | solution.py:218
  820.9 10.4 %reshape.188 = f32[128,10,2048]{2,1,0:T(8,128)} reshape(bf16[1280,2048]{1,0:T(8,128)(2,1)} %gather_fusion.1) | data formatting | bytes 15728640 | tf_op jit(solution)/shard_map/convert_element_type | solution.py:219
  831.2 10.5 %multiply_reduce_fusion = bf16[128,2048]{1,0:T(8,128)(2,1)} fusion(f32[128,10,2048]{2,1,0:T(8,128)} %reshape.188, f32[128,10]{1,0:T(8,128)S(1)} %copy.149), kind=kLoop, calls=%fused_computation.41 | loop fusion | flops 4980736 | bytes 11015168 | tf_op jit(solution)/shard_map/reduce_sum | solution.py:219
  (230 shorter events, 120.1 us)
Async XLA Ops:
  7.2 322.9 %copy-start = (bf16[512,2048]{1,0:T(8,128)(2,1)S(1)}, bf16[512,2048]{1,0:T(8,128)(2,1)}, u32[]{:S(2)}) copy-start(bf16[512,2048]{1,0:T(8,128)(2,1)} %param.28) | copy-start | bytes 6291460
  7.2 2.7 copy-start.10
  7.2 166.5 %all-gather.5.cloned.1.call-start = ((), (), s32[]{:S(2)}) async-start(), calls=%async_computation.4 | async-start | bytes 4456448 | tf_op jit(solution)/shard_map/all_gather | solution.py:14
  9.8 3.5 copy-start.15
  9.9 3.6 copy-start.16
  16.3 27.3 %copy-start.2 = (f32[1024,2,2,128]{3,0,2,1:T(8,128)}, f32[1024,2,2,128]{3,0,2,1:T(8,128)S(1)}, u32[]{:S(2)}) copy-start(f32[1024,2,2,128]{3,0,2,1:T(8,128)S(1)} %broadcast_in_dim.55) | copy-start | bytes 6291460
  38.6 2.5 copy-start.12
  50.8 12.0 %copy-start.3 = (f32[1024,2,2,128]{3,0,2,1:T(8,128)S(1)}, f32[1024,2,2,128]{3,0,2,1:T(8,128)}, u32[]{:S(2)}) copy-start(f32[1024,2,2,128]{3,0,2,1:T(8,128)} %copy-done.2) | copy-start | bytes 6291460
  50.8 12.0 %copy-start.6 = (f32[4,16,64,128]{3,2,1,0:T(8,128)S(1)}, f32[4,16,64,128]{3,2,1,0:T(8,128)}, u32[]{:S(2)}) copy-start(f32[4,16,64,128]{3,2,1,0:T(8,128)} %fusion.52) | copy-start | bytes 6291460
  72.0 47.5 %copy-start.11 = (bf16[1024,2,128]{2,1,0:T(2,128)(2,1)S(1)}, bf16[1024,2,128]{2,1,0:T(2,128)(2,1)}, u32[]{:S(2)}) copy-start(bf16[1024,2,128]{2,1,0:T(2,128)(2,1)} %param.21) | copy-start | bytes 1572868
  118.0 0.7 copy-start.5
  118.0 0.8 copy-start.7
  118.7 109.0 %all-gather.7.cloned.1.call-start = ((), (), s32[]{:S(2)}) async-start(), calls=%async_computation.5 | async-start | bytes 4456448 | tf_op jit(solution)/shard_map/all_gather | solution.py:14
  119.5 272.1 %reduce-scatter.2.cloned.1.call-start = ((), (), s32[]{:S(2)}) async-start(), calls=%async_computation.3 | async-start | bytes 4718592 | tf_op jit(solution)/shard_map/reduce_scatter | solution.py:166
  123.6 1.6 copy-start.4
  324.2 2.4 copy-start.8
  324.2 2.4 copy-start.19
  335.6 0.7 copy-start.14
  337.2 54.4 %copy-start.13 = (bf16[128,2048]{1,0:T(8,128)(2,1)S(1)}, bf16[128,2048]{1,0:T(8,128)(2,1)}, u32[]{:S(2)}) copy-start(bf16[128,2048]{1,0:T(8,128)(2,1)} %param.27) | copy-start | bytes 1572868
  347.4 45.6 %copy-start.17 = (f32[2048]{0:T(1024)S(1)}, f32[2048]{0:T(1024)}, u32[]{:S(2)}) copy-start(f32[2048]{0:T(1024)} %param.30) | copy-start | bytes 24580
  392.8 11.3 %copy-start.9 = (bf16[128,2048]{1,0:T(8,128)(2,1)}, bf16[128,2048]{1,0:T(8,128)(2,1)S(1)}, u32[]{:S(2)}) copy-start(bf16[128,2048]{1,0:T(8,128)(2,1)S(1)} %add_convert_fusion) | copy-start | bytes 1572868
  440.9 130.7 %copy-start.20 = (bf16[2,2048,512]{2,1,0:T(8,128)(2,1)S(1)}, bf16[2,2048,512]{2,1,0:T(8,128)(2,1)}, u32[]{:S(2)}) copy-start(bf16[2,2048,512]{2,1,0:T(8,128)(2,1)} %param.32) | copy-start | bytes 12582916
  571.6 14.6 %copy-start.21 = (bf16[2,2048,512]{2,1,0:T(8,128)(2,1)S(1)}, bf16[2,2048,512]{2,1,0:T(8,128)(2,1)}, u32[]{:S(2)}) copy-start(bf16[2,2048,512]{2,1,0:T(8,128)(2,1)} %param.31) | copy-start | bytes 12582916
  586.2 15.2 %copy-start.22 = (bf16[2,512,2048]{2,1,0:T(8,128)(2,1)S(1)}, bf16[2,512,2048]{2,1,0:T(8,128)(2,1)}, u32[]{:S(2)}) copy-start(bf16[2,512,2048]{2,1,0:T(8,128)(2,1)} %param.33) | copy-start | bytes 12582916
  641.0 6.4 copy-start.18
  641.0 131.5 %all-to-all-start.1 = ((bf16[128,2,10,2048]{3,1,2,0:T(2,128)(2,1)}), bf16[128,2,10,2048]{3,1,2,0:T(2,128)(2,1)}, u32[]{:S(2)}, u32[]{:S(2)}) async-start(bf16[128,2,10,2048]{3,1,2,0:T(2,128)(2,1)} %copy.156), calls=%async_computation.2 | async-start | bytes 20971520 | tf_op jit(solution)/shard_map/all_to_all | solution.py:209
  831.2 10.5 %copy-start.1 = (bf16[512,2048]{1,0:T(8,128)(2,1)S(1)}, bf16[512,2048]{1,0:T(8,128)(2,1)}, u32[]{:S(2)}) copy-start(bf16[512,2048]{1,0:T(8,128)(2,1)} %param.28) | copy-start | bytes 6291460
Sparse Core Ops, SparseCore 0:
  118.8 54.8 all-gather.4
  176.5 51.2 all-gather.6
  335.7 55.8 reduce-scatter.1
where the time goes:
time: 859 us; the launch traced here: 848 us
  waiting for transfers between devices  259 us (30%)
  matrix products  246 us (29%)
  local copies, waits for them, and re-layouts  161 us (19%)
  blocking collectives  131 us (15%)
  other arithmetic  30.3 us (4%)
  between operations  14.6 us (2%)
    all_to_all x1, blocking collectives, shards(): lax.all_to_all(shaped, ('ctx', 'exp'), split_axis=0, concat_axis=0, tiled...  131 us
    all_to_all x1, waiting for transfers between devices, shards(): lax.all_to_all(jnp.einsum('sxcf,xfd->sxcd', inner_act, down_proj, preferr...  125 us
    all_gather x2, waiting for transfers between devices, prefix(): gathered = jax.tree.map(lambda a: lax.all_gather(a, axis), part)  95.1 us
    reduce_scatter x1, waiting for transfers between devices, shards(): lax.psum_scatter(jnp.dot(gated, out_weight, preferred_element_type=jnp.fl...  38.3 us
    reshape x2, local copies, waits for them, and re-layouts, shards(): shaped = outgoing.reshape(dev_count, local_experts, capacity, model_width)  36.9 us
    dot_general x16, matrix products, advance(): jnp.einsum('hid,hde->hie', decayed_query, state_now, precision=highest)  31 us
    convert_element_type x1, local copies, waits for them, and re-layouts, shards(): returned = lax.all_to_all(jnp.einsum('sxcf,xfd->sxcd', inner_act, down_pr...  29.6 us
    dot_general x16, matrix products, advance(): jnp.einsum('hjd,hje->hde', tail_keys, fresh_rows, precision=highest)  24.6 us
  transfers between devices with their start and end apart: 4, of which 4 were waited for; matrix products, arithmetic and copies ran while one was open for 3% of the time, Pallas kernels for 0%

commit v1 on v0

v1 whole, which is shorter than its diff:
```python
import functools

import jax
import jax.numpy as jnp
from jax import lax
from jax.experimental import pallas as pl
from jax.experimental.pallas import tpu as pltpu
from jax.sharding import PartitionSpec as P

CHUNK = 128
CAP = 10
F32 = jnp.float32
BF16 = jnp.bfloat16
VMEM = pltpu.VMEM
MIB = 1024 * 1024


def mxu(a, b, dims=((1,), (0,))):
    return lax.dot_general(a, b, (dims, ((), ())), preferred_element_type=F32)


def halves(a):
    high = a.astype(BF16)
    return high, (a - high.astype(F32)).astype(BF16)


def product(a, b):
    width = b[0].shape[1]
    left = jnp.concatenate([a[0], a[1]], axis=1)
    right = jnp.concatenate(
        [
            jnp.concatenate([b[0], b[1]], axis=1),
            jnp.concatenate([b[0], jnp.zeros_like(b[0])], axis=1),
        ],
        axis=0,
    )
    both = mxu(left, right)
    return both[:, :width] + both[:, width:]


def unit_lower_inverse(lower, row, col):
    eye = (row == col).astype(F32)
    diag = jnp.where(row // 16 == col // 16, lower, 0.0)
    inverse = eye - diag
    power = halves(-diag)
    for step in range(3):
        power = halves(product(power, power))
        inverse = inverse + product(halves(inverse), power)
    size = 16
    while size < lower.shape[0]:
        below = jnp.where((row // (2 * size) == col // (2 * size)) & (row // size != col // size), lower, 0.0)
        inv = halves(inverse)
        inverse = inverse - product(halves(product(inv, halves(below))), inv)
        size = size * 2
    return inverse


def delta_kernel(ds_ref, q_ref, k_ref, v_ref, r_ref, o_ref, msg_ref, state_ref):
    step = pl.program_id(0)
    heads = v_ref.shape[0]
    group = heads // q_ref.shape[0]
    c, d = q_ref.shape[1], q_ref.shape[2]
    row = lax.broadcasted_iota(jnp.int32, (c, c), 0)
    col = lax.broadcasted_iota(jnp.int32, (c, c), 1)
    causal = row >= col
    strict = row > col

    @pl.when(step == 0)
    def _():
        eye = (row == col).astype(F32)
        for h in range(heads):
            state_ref[h] = jnp.concatenate([eye, jnp.zeros_like(eye)], axis=1)

    ds = ds_ref[0]
    upto = (row <= col).astype(BF16)
    d0 = ds.astype(BF16)
    rest = ds - d0.astype(F32)
    d1 = rest.astype(BF16)
    d2 = (rest - d1.astype(F32)).astype(BF16)
    cum = mxu(d0, upto) + mxu(d1, upto) + mxu(d2, upto)
    half = jnp.where(lax.broadcasted_iota(jnp.int32, ds.shape, 0) < heads, cum, ds)
    columns = jnp.transpose(half, (1, 0))

    keyed = []
    for g in range(q_ref.shape[0]):
        q, k = q_ref[g], k_ref[g]
        qf, kf = q.astype(F32), k.astype(F32)
        q_col = (d ** -0.5) / jnp.sqrt(jnp.sum(qf * qf, axis=1, keepdims=True) + 1e-06)
        k_col = 1.0 / jnp.sqrt(jnp.sum(kf * kf, axis=1, keepdims=True) + 1e-06)
        gram = mxu(k, k, ((1,), (1,)))
        k_row = 1.0 / jnp.sqrt(jnp.sum(jnp.where(row == col, gram, 0.0), axis=0, keepdims=True) + 1e-06)
        gram = gram * (k_col * k_row)
        cross = mxu(q, k, ((1,), (1,))) * (q_col * k_row)
        keyed.append((qf, k, kf, q_col, k_col, k_row, gram, cross, jnp.transpose(kf, (1, 0)).astype(BF16)))

    for h in range(heads):
        qf, k, kf, q_col, k_col, k_row, gram, cross, k_t = keyed[h // group]
        cum_col, beta_col = columns[:, h : h + 1], columns[:, heads + h : heads + h + 1]
        cum_row, beta_row = half[h : h + 1, :], half[heads + h : heads + h + 1, :]
        closing = cum_row[:, c - 1 : c]
        spread = jnp.where(causal, jnp.exp(jnp.where(causal, cum_col - cum_row, 0.0)), 0.0)
        lower = jnp.where(strict, beta_col * gram * spread, 0.0)
        mixing = cross * spread
        inverse = unit_lower_inverse(lower, row, col)
        t_k = halves(inverse * (beta_row * jnp.exp(cum_row) * k_row))
        t_v = halves(inverse * beta_row)
        v = v_ref[h]
        weighted = mxu(jnp.concatenate(t_k, axis=1), jnp.concatenate([k, k], axis=0))
        written = mxu(jnp.concatenate(t_v, axis=1), jnp.concatenate([v, v], axis=0))
        state = state_ref[h]
        state_b = state.astype(BF16)
        fresh = jnp.concatenate([jnp.zeros_like(written), written], axis=1) - mxu(weighted.astype(BF16), state_b)
        reads = jnp.concatenate([qf * (q_col * jnp.exp(cum_col)), mixing], axis=1).astype(BF16)
        out = mxu(reads, jnp.concatenate([state_b, fresh.astype(BF16)], axis=0))
        r_ref[h] = out[:, :d].astype(BF16)
        o_ref[h] = out[:, d:]
        tail = (fresh * (k_col * jnp.exp(closing - cum_col))).astype(BF16)
        state_ref[h] = jnp.exp(closing) * state + mxu(k_t, tail)

    @pl.when(step == pl.num_programs(0) - 1)
    def _():
        parts = msg_ref.shape[1]
        wide = d // parts
        for h in range(heads):
            state = state_ref[h]
            moved = state[:, :d].astype(msg_ref.dtype)
            added = jnp.transpose(state[:, d:], (1, 0)).astype(msg_ref.dtype)
            for p in range(parts):
                msg_ref[h, p, :d, :] = moved
                msg_ref[h, p, d:, :] = added[p * wide : (p + 1) * wide]


def local_delta(ds, q, k, v, parts):
    heads, seq, dv = v.shape
    kh, _, dk = q.shape
    wide = dv // parts
    return pl.pallas_call(
        delta_kernel,
        grid=(seq // CHUNK,),
        in_specs=[
            pl.BlockSpec((1, 2 * heads, CHUNK), lambda i: (i, 0, 0)),
            pl.BlockSpec((kh, CHUNK, dk), lambda i: (0, i, 0)),
            pl.BlockSpec((kh, CHUNK, dk), lambda i: (0, i, 0)),
            pl.BlockSpec((heads, CHUNK, dv), lambda i: (0, i, 0)),
        ],
        out_specs=[
            pl.BlockSpec((heads, CHUNK, dk), lambda i: (0, i, 0)),
            pl.BlockSpec((heads, CHUNK, dv), lambda i: (0, i, 0)),
            pl.BlockSpec((heads, parts, dk + wide, dk), lambda i: (0, 0, 0, 0)),
        ],
        out_shape=[
            jax.ShapeDtypeStruct((heads, seq, dk), BF16),
            jax.ShapeDtypeStruct((heads, seq, dv), F32),
            jax.ShapeDtypeStruct((heads, parts, dk + wide, dk), BF16),
        ],
        scratch_shapes=[VMEM((heads, dk, dk + dv), F32)],
        compiler_params=pltpu.CompilerParams(
            dimension_semantics=("arbitrary",), vmem_limit_bytes=40 * MIB
        ),
        name="delta_local",
    )(ds, q, k, v)


def prefix_kernel(msg_ref, out_ref):
    count, tall, dk = msg_ref.shape
    wide = tall - dk
    state = jnp.zeros((wide, dk), F32)
    for i in range(count):
        out_ref[i] = state.astype(out_ref.dtype)
        if i < count - 1:
            both = jnp.concatenate(halves(state), axis=0)
            moved = mxu(both, msg_ref[i, :dk, :], ((1,), (1,)))
            state = moved[:wide] + moved[wide:] + msg_ref[i, dk:, :].astype(F32)


def prefix_states(msg, wide):
    count, tall, dk = msg.shape
    return pl.pallas_call(
        prefix_kernel,
        out_shape=jax.ShapeDtypeStruct((count, wide, dk), BF16),
        compiler_params=pltpu.CompilerParams(vmem_limit_bytes=16 * MIB),
        name="prefix_states",
    )(msg)


def gate_kernel(r_ref, o_ref, s_ref, g_ref, gain_ref, w_ref, out_ref):
    parts = []
    for h in range(r_ref.shape[0]):
        core = o_ref[h] + mxu(r_ref[h], s_ref[h], ((1,), (1,)))
        root = jnp.sqrt(jnp.mean(core * core, axis=1, keepdims=True) + 1e-06)
        gate = g_ref[h].astype(F32)
        silu = gate / (1.0 + jnp.exp(-gate))
        parts.append((core / root * gain_ref[...] * silu).astype(BF16))
    out_ref[...] = mxu(jnp.concatenate(parts, axis=1), w_ref[...]).astype(BF16)


def gate_project(r, o, states, gate, gain, weight):
    heads, seq, d = r.shape
    rows = 256
    width = weight.shape[1]
    by_rows = pl.BlockSpec((heads, rows, d), lambda i: (0, i, 0))
    return pl.pallas_call(
        gate_kernel,
        grid=(seq // rows,),
        in_specs=[
            by_rows,
            by_rows,
            pl.BlockSpec((heads, d, d), lambda i: (0, 0, 0)),
            by_rows,
            pl.BlockSpec((1, d), lambda i: (0, 0)),
            pl.BlockSpec(weight.shape, lambda i: (0, 0)),
        ],
        out_specs=pl.BlockSpec((rows, width), lambda i: (i, 0)),
        out_shape=jax.ShapeDtypeStruct((seq, width), BF16),
        compiler_params=pltpu.CompilerParams(
            dimension_semantics=("arbitrary",), vmem_limit_bytes=40 * MIB
        ),
        name="gate_project",
    )(r, o, states, gate, gain, weight)


def slot_kernel(experts, ids_ref, out_ref):
    top, toks = ids_ref.shape
    expert = lax.broadcasted_iota(jnp.int32, (experts, toks), 0)
    hits = jnp.zeros((experts, toks), F32)
    for k in range(top):
        hits = hits + (expert == ids_ref[k : k + 1, :]).astype(F32)
    before = (
        lax.broadcasted_iota(jnp.int32, (toks, toks), 0) < lax.broadcasted_iota(jnp.int32, (toks, toks), 1)
    ).astype(BF16)
    earlier = mxu(hits.astype(BF16), before)
    for k in range(top):
        ids = ids_ref[k : k + 1, :]
        rank = jnp.sum(jnp.where(expert == ids, earlier, 0.0), axis=0, keepdims=True)
        out_ref[k : k + 1, :] = ids * CAP + rank.astype(jnp.int32)


def slots_of(ids, experts):
    return pl.pallas_call(
        functools.partial(slot_kernel, experts),
        out_shape=jax.ShapeDtypeStruct(ids.shape, jnp.int32),
        compiler_params=pltpu.CompilerParams(vmem_limit_bytes=16 * MIB),
        name="slots",
    )(ids)


def dispatch_kernel(part_ref, res_ref, gain_ref, slot_ref, att_ref, send_ref, flat_ref):
    toks, width = part_ref.shape
    pieces = width // 128
    attended = (res_ref[...].astype(F32) + part_ref[...].astype(F32)).astype(BF16)
    att_ref[...] = attended
    settled = attended.astype(F32)
    root = jnp.sqrt(jnp.mean(settled * settled, axis=1, keepdims=True) + 1e-06)
    normed = settled / root * gain_ref[...]
    for j in range(pieces):
        flat_ref[pl.ds(j, toks, stride=pieces), :] = normed[:, j * 128 : (j + 1) * 128]

    @pl.loop(0, toks)
    def _(t):
        tile = flat_ref[pl.ds(pl.multiple_of(t * pieces, pieces), pieces), :].astype(BF16)
        for k in range(slot_ref.shape[0]):
            send_ref[slot_ref[k, t]] = tile


def dispatch(part, residual, gain, slots, count):
    toks, width = part.shape
    pieces = width // 128
    whole = pl.BlockSpec(memory_space=VMEM)
    return pl.pallas_call(
        dispatch_kernel,
        in_specs=[whole, whole, whole, pl.BlockSpec(memory_space=pltpu.SMEM)],
        out_specs=[whole, whole],
        out_shape=[
            jax.ShapeDtypeStruct((toks, width), BF16),
            jax.ShapeDtypeStruct((count, pieces, 128), BF16),
        ],
        scratch_shapes=[VMEM((toks * pieces, 128), F32)],
        compiler_params=pltpu.CompilerParams(vmem_limit_bytes=40 * MIB),
        name="dispatch",
    )(part, residual, gain, slots)


def expert_kernel(x_ref, wg_ref, wu_ref, wd_ref, out_ref, flat_ref):
    sources, _, tall, lanes = x_ref.shape
    rows = flat_ref.shape[0] // 16
    pieces = 16
    flat_ref[...] = x_ref[...].reshape(sources * tall, lanes).astype(F32)
    x = jnp.concatenate(
        [flat_ref[pl.ds(j, rows, stride=pieces), :].astype(BF16) for j in range(pieces)], axis=1
    )
    gate = mxu(x, wg_ref[0])
    up = mxu(x, wu_ref[0])
    inner = (gate / (1.0 + jnp.exp(-gate)) * up).astype(BF16)
    y = mxu(inner, wd_ref[0])
    for j in range(pieces):
        flat_ref[pl.ds(j, rows, stride=pieces), :] = y[:, j * 128 : (j + 1) * 128]
    out_ref[...] = flat_ref[...].astype(BF16).reshape(sources, 1, tall, lanes)


def run_experts(x, gate_proj, up_proj, down_proj):
    count, local, tall, lanes = x.shape
    sources = 32
    rows = sources * tall // 16
    tokens = pl.BlockSpec((sources, 1, tall, lanes), lambda e, i: (i, e, 0, 0))
    return pl.pallas_call(
        expert_kernel,
        grid=(local, count // sources),
        in_specs=[
            tokens,
            pl.BlockSpec((1,) + gate_proj.shape[1:], lambda e, i: (e, 0, 0)),
            pl.BlockSpec((1,) + up_proj.shape[1:], lambda e, i: (e, 0, 0)),
            pl.BlockSpec((1,) + down_proj.shape[1:], lambda e, i: (e, 0, 0)),
        ],
        out_specs=tokens,
        out_shape=jax.ShapeDtypeStruct(x.shape, BF16),
        scratch_shapes=[VMEM((sources * tall, lanes), F32)],
        compiler_params=pltpu.CompilerParams(
            dimension_semantics=("arbitrary", "arbitrary"), vmem_limit_bytes=48 * MIB
        ),
        name="experts",
    )(x, gate_proj, up_proj, down_proj)


def combine_kernel(back_ref, slot_ref, gate_ref, out_ref, flat_ref):
    toks, width = out_ref.shape
    pieces = width // 128

    @pl.loop(0, toks)
    def _(t):
        total = jnp.zeros((pieces, 128), F32)
        for k in range(slot_ref.shape[0]):
            total = total + gate_ref[k, t] * back_ref[slot_ref[k, t]].astype(F32)
        flat_ref[pl.ds(pl.multiple_of(t * pieces, pieces), pieces), :] = total

    for j in range(pieces):
        out_ref[:, j * 128 : (j + 1) * 128] = flat_ref[pl.ds(j, toks, stride=pieces), :].astype(BF16)


def combine(back, slots, gates):
    count, pieces, lanes = back.shape
    toks = slots.shape[1]
    smem = pl.BlockSpec(memory_space=pltpu.SMEM)
    return pl.pallas_call(
        combine_kernel,
        in_specs=[pl.BlockSpec(memory_space=VMEM), smem, smem],
        out_specs=pl.BlockSpec(memory_space=VMEM),
        out_shape=jax.ShapeDtypeStruct((toks, pieces * lanes), BF16),
        scratch_shapes=[VMEM((toks * pieces, lanes), F32)],
        compiler_params=pltpu.CompilerParams(vmem_limit_bytes=40 * MIB),
        name="combine",
    )(back, slots, gates)


def shards(
    queries,
    key_vectors,
    values,
    out_gate,
    write_strength,
    decay_logarithm,
    residual,
    out_weight,
    head_gain,
    post_gain,
    gate_proj,
    up_proj,
    down_proj,
    expert_ids,
    route_gates,
):
    seq, heads, dv = values.shape
    dk = queries.shape[2]
    n_ctx = lax.axis_size("ctx")
    n_dev = n_ctx * lax.axis_size("exp")
    parts = n_ctx // heads
    wide = dv // parts
    local_experts = gate_proj.shape[0]
    toks, width = residual.shape

    slots = slots_of(expert_ids.T, local_experts * n_dev)
    gates = route_gates.T

    by_head = lambda a: jnp.transpose(a, (1, 0, 2))
    ds = jnp.transpose(
        jnp.concatenate([decay_logarithm, write_strength], axis=0).reshape(2 * heads, seq // CHUNK, CHUNK),
        (1, 0, 2),
    )
    reads, local_out, msg = local_delta(ds, by_head(queries), by_head(key_vectors), by_head(values), parts)
    msg = lax.all_to_all(msg.reshape(n_ctx, dk + wide, dk), "ctx", 0, 0, tiled=True)
    states = lax.all_to_all(prefix_states(msg, wide), "ctx", 0, 0, tiled=True).reshape(heads, dv, dk)
    share = gate_project(reads, local_out, states, by_head(out_gate), head_gain.reshape(1, dv), out_weight)
    summed = lax.psum_scatter(share, "exp", scatter_dimension=0, tiled=True)
    attended, send = dispatch(
        summed, residual, post_gain.reshape(1, width), slots, n_dev * local_experts * CAP
    )
    tall = CAP * width // 128
    held = lax.all_to_all(
        send.reshape(n_dev, local_experts, tall, 128), ("ctx", "exp"), 0, 0, tiled=True
    )
    done = run_experts(held, gate_proj, up_proj, down_proj)
    back = lax.all_to_all(done, ("ctx", "exp"), 0, 0, tiled=True)
    mixture = combine(back.reshape(n_dev * local_experts * CAP, width // 128, 128), slots, gates)
    return (attended, mixture)


def solution(mesh):
    in_specs = (
        P("ctx", "exp", None),
        P("ctx", "exp", None),
        P("ctx", "exp", None),
        P("ctx", "exp", None),
        P("exp", "ctx"),
        P("exp", "ctx"),
        P(("ctx", "exp"), None),
        P("exp", None),
        P(),
        P(),
        P(("ctx", "exp"), None, None),
        P(("ctx", "exp"), None, None),
        P(("ctx", "exp"), None, None),
        P(("ctx", "exp"), None),
        P(("ctx", "exp"), None),
    )
    out_specs = (P(("ctx", "exp"), None), P(("ctx", "exp"), None))
    return jax.shard_map(shards, mesh=mesh, in_specs=in_specs, out_specs=out_specs, check_vma=False)
```

time: 859 us -> 455 us (0.53); the launches traced: 848 us -> 454 us
  matrix products: 246 us -> 0 us
  waiting for transfers between devices: 259 us -> 39.6 us
  local copies, waits for them, and re-layouts: 161 us -> 13 us
  blocking collectives: 131 us -> 276 us
  Pallas kernels: 0 us -> 107 us
  other arithmetic: 30.3 us -> 0.75 us
    dot_general x116 -> x0, matrix products: 246 us -> none  [the longest x16 31 us: advance(): jnp.einsum('hid,hde->hie', decayed_query, state_now, precision=highest)]
    all_to_all x1 -> x3, blocking collectives: 131 us -> 276 us  [the longest x1 131 us: shards(): lax.all_to_all(send.reshape(n_dev, local_experts, tall, 128), ('ctx', 'ex...]
    all_to_all x1, waiting for transfers between devices: 125 us -> 5.39 us  [shards(): lax.all_to_all(prefix_states(msg, wide), 'ctx', 0, 0, tiled=True)]
    pallas_call x0 -> x7, Pallas kernels: none -> 107 us  [the longest x1 60.3 us: local_delta(): pl.pallas_call(delta_kernel, grid=(seq // CHUNK,), in_specs=[pl.BlockSpec...]
    all_gather x2 -> x0, waiting for transfers between devices: 95.1 us -> none  [prefix(): gathered = jax.tree.map(lambda a: lax.all_gather(a, axis), part)]
    reshape x6 -> x0, local copies, waits for them, and re-layouts: 55.3 us -> none  [the longest x2 36.9 us: shards(): shaped = outgoing.reshape(dev_count, local_experts, capacity, model_width)]
    convert_element_type x3 -> x0, local copies, waits for them, and re-layouts: 41.3 us -> none  [the longest x1 29.6 us: shards(): returned = lax.all_to_all(jnp.einsum('sxcf,xfd->sxcd', inner_act, down_pr...]
    gather x7 -> x0, local copies, waits for them, and re-layouts: 37.5 us -> none  [the longest x1 16.1 us: shards(): picked = returned.reshape(expert_count * capacity, model_width)[slot_index]]
  transfers between devices with their start and end apart: 4 -> 2, of which waited for: 4 -> 2; matrix products, arithmetic and copies ran while one was open for 3% -> 0% of each run, Pallas kernels for 0% -> 0%
where the time goes in v1:
time: 455 us; the launch traced here: 454 us
  blocking collectives  276 us (61%)
  Pallas kernels  107 us (24%)
  waiting for transfers between devices  39.6 us (9%)
  between operations  14.1 us (3%)
  local copies, waits for them, and re-layouts  13 us (3%)
    all_to_all x1, blocking collectives, shards(): lax.all_to_all(send.reshape(n_dev, local_experts, tall, 128), ('ctx', 'ex...  131 us
    all_to_all x1, blocking collectives, shards(): back = lax.all_to_all(done, ('ctx', 'exp'), 0, 0, tiled=True)  125 us
    pallas_call x1, Pallas kernels, local_delta(): pl.pallas_call(delta_kernel, grid=(seq // CHUNK,), in_specs=[pl.BlockSpec...  60.3 us
    reduce_scatter x1, waiting for transfers between devices, shards(): summed = lax.psum_scatter(share, 'exp', scatter_dimension=0, tiled=True)  34.2 us
    pallas_call x1, Pallas kernels, run_experts(): pl.pallas_call(expert_kernel, grid=(local, count // sources), in_specs=[t...  29.5 us
    all_to_all x1, blocking collectives, shards(): lax.all_to_all(msg.reshape(n_ctx, dk + wide, dk), 'ctx', 0, 0, tiled=True)  20.2 us
    unnamed x28, local copies, waits for them, and re-layouts  11.5 us
  transfers between devices with their start and end apart: 2, of which 2 were waited for; matrix products, arithmetic and copies ran while one was open for 0% of the time, Pallas kernels for 0%

profile of v1, /device:TPU:1, one launch (start us, length us, event | category | flops | bytes accessed | tf_op | source)
XLA Modules:
  0.0 454.3 jit_solution(11417876410892539794)
XLA Ops:
  7.2 1.4 copy.26
  8.5 0.7 maximum_bitcast_fusion.ds_ref
  9.3 0.0 copy-start.2
  9.3 0.0 copy-start.12
  9.3 1.5 copy_bitcast_fusion.2
  10.8 60.3 %delta_local.1 = (bf16[4,1024,128]{2,1,0:T(8,128)(2,1)S(1)}, f32[4,1024,128]{2,1,0:T(8,128)S(1)}, bf16[4,4,160,128]{3,2,1,0:T(8,128)(2,1)S(1)}) custom-call(f32[8,8,128]{2,1,0:T(8,128)S(1)} %maximum_bitcast_fusion.ds_ref, bf16[2,1024,128]{2,1,0:T(8,128)(2,1)S(1)} %get-tuple-element.13.q_ref, bf16[2,1024,128]{2,1,0:T(8,128)(2,1)S(1)} %get-tuple-element.12.k_ref, ...), custom_call_target="tpu_custom_call" | custom-call | tf_op jit(solution)/shard_map/delta_local/pallas_call | solution.py:137
  71.1 0.0 copy-start.3
  71.1 1.3 copy-done.3
  72.5 0.0 copy-start.5
  72.5 1.0 copy-done.5
  73.4 20.2 %all_to_all.20.msg_ref = bf16[16,160,128]{2,1,0:T(8,128)(2,1)S(1)} all-to-all(bf16[16,160,128]{2,1,0:T(8,128)(2,1)S(1)} %bitcast.26), channel_id=1, replica_groups=mesh['ctx'=16,'exp'=8] {'ctx'}, dimensions={0} | all-to-all | bytes 1310720 | tf_op jit(solution)/shard_map/all_to_all | solution.py:389
  93.6 2.5 prefix_states.1
  96.2 3.5 all-to-all-start.1
  99.7 0.0 reduce-scatter.2.cloned.1.call-start
  99.7 1.4 copy.25
  101.1 5.4 %all-to-all-done.1 = bf16[16,32,128]{2,1,0:T(8,128)(2,1)S(1)} async-done(((bf16[16,32,128]{2,1,0:T(8,128)(2,1)}), bf16[16,32,128]{2,1,0:T(8,128)(2,1)S(1)}, u32[]{:S(2)}, u32[]{:S(2)}) %all-to-all-start.1) | async-done | bytes 131104 | tf_op jit(solution)/shard_map/all_to_all | solution.py:390
  106.5 0.0 copy-done.2
  106.5 0.0 copy-done.12
  106.5 0.0 copy-start.4
  106.5 1.6 copy-done.4
  108.1 0.0 copy-start.6
  108.1 1.2 copy-done.6
  109.3 5.0 %gate_project.1 = bf16[1024,2048]{1,0:T(8,128)(2,1)S(1)} custom-call(bf16[4,1024,128]{2,1,0:T(8,128)(2,1)S(1)} %copy-done.6, f32[4,1024,128]{2,1,0:T(8,128)S(1)} %copy-done.4, bf16[4,128,128]{2,1,0:T(8,128)(2,1)S(1)} %bitcast.27, bf16[4,1024,128]{2,1,0:T(8,128)(2,1)S(1)} %bitcast.25, f32[1,128]{1,0:T(1,128)S(1)} %bitcast.31, bf16[512,2048]{1,0:T(8,128)(2,1)S(1)} %copy-done.2), custom_call_target="tpu_custom_call" | custom-call | tf_op jit(solution)/shard_map/gate_project/pallas_call | solution.py:202
  114.3 0.0 copy-start
  114.3 1.9 copy-done
  116.3 0.0 copy-start.10
  116.3 0.0 copy-start.7
  116.3 0.0 copy-start.9
  116.3 0.0 reduce-scatter.2.cloned.1.call-update
  116.3 0.7 copy-done.10
  117.0 0.4 slots.1.slot_ref
  117.3 34.2 %reduce-scatter.2.cloned.1.call-done.part_ref = bf16[128,2048]{1,0:T(8,128)(2,1)} async-done(((bf16[1024,2048]{1,0:T(8,128)(2,1)}), bf16[128,2048]{1,0:T(8,128)(2,1)}) %reduce-scatter.2.cloned.1.call-update) | async-done | bytes 524304 | tf_op jit(solution)/shard_map/reduce_scatter | solution.py:392
  151.5 0.0 copy-done.7
  151.5 0.0 copy-done.9
  151.5 0.0 copy-start.8
  151.5 1.0 copy-done.8
  152.6 4.3 dispatch.1
  156.9 0.0 copy-start.1
  156.9 130.5 %all_to_all.21.x_ref = bf16[128,2,160,128]{3,2,1,0:T(8,128)(2,1)} all-to-all(bf16[128,2,160,128]{3,2,1,0:T(8,128)(2,1)S(1)} %bitcast.23), channel_id=1, replica_groups=mesh['ctx'=16,'exp'=8] {'ctx','exp'}, dimensions={0} | all-to-all | bytes 20971520 | tf_op jit(solution)/shard_map/all_to_all | solution.py:397
  287.4 0.0 copy-done.1
  287.4 29.5 %experts.1 = bf16[128,2,160,128]{3,2,1,0:T(8,128)(2,1)} custom-call(bf16[128,2,160,128]{3,2,1,0:T(8,128)(2,1)} %all_to_all.21.x_ref, bf16[2,2048,512]{2,1,0:T(8,128)(2,1)S(1)} %copy-done.1, bf16[2,2048,512]{2,1,0:T(8,128)(2,1)} %wu_ref.1, bf16[2,512,2048]{2,1,0:T(8,128)(2,1)} %wd_ref.1), custom_call_target="tpu_custom_call" | custom-call | tf_op jit(solution)/shard_map/experts/pallas_call | solution.py:305
  317.0 0.0 copy-start.11
  317.0 125.5 %all_to_all.22 = bf16[128,2,160,128]{3,2,1,0:T(8,128)(2,1)S(1)} all-to-all(bf16[128,2,160,128]{3,2,1,0:T(8,128)(2,1)} %experts.1), channel_id=1, replica_groups=mesh['ctx'=16,'exp'=8] {'ctx','exp'}, dimensions={0} | all-to-all | bytes 20971520 | tf_op jit(solution)/shard_map/all_to_all | solution.py:401
  442.4 0.0 copy-done.11
  442.4 5.0 %combine.1 = bf16[128,2048]{1,0:T(8,128)(2,1)} custom-call(bf16[2560,16,128]{2,1,0:T(8,128)(2,1)S(1)} %bitcast.22, s32[10,128]{1,0:T(8,128)S(1)} %slots.1.slot_ref, f32[10,128]{1,0:T(8,128)S(1)} %bitcast.30), custom_call_target="tpu_custom_call" | custom-call | tf_op jit(solution)/shard_map/combine/pallas_call | solution.py:343
Async XLA Ops:
  9.3 97.2 %copy-start.2 = (bf16[512,2048]{1,0:T(8,128)(2,1)S(1)}, bf16[512,2048]{1,0:T(8,128)(2,1)}, u32[]{:S(2)}) copy-start(bf16[512,2048]{1,0:T(8,128)(2,1)} %w_ref.1) | copy-start | bytes 6291460
  9.3 97.2 %copy-start.12 = (f32[128]{0:T(128)S(1)}, f32[128]{0:T(128)}, u32[]{:S(2)}) copy-start(f32[128]{0:T(128)} %param.23) | copy-start | bytes 1540
  71.1 1.3 copy-start.3
  72.5 1.0 copy-start.5
  96.2 10.3 %all-to-all-start.1 = ((bf16[16,32,128]{2,1,0:T(8,128)(2,1)}), bf16[16,32,128]{2,1,0:T(8,128)(2,1)S(1)}, u32[]{:S(2)}, u32[]{:S(2)}) async-start(bf16[16,32,128]{2,1,0:T(8,128)(2,1)} %prefix_states.1), calls=%async_computation.1 | async-start | bytes 262144 | tf_op jit(solution)/shard_map/all_to_all | solution.py:390
  99.7 51.8 %reduce-scatter.2.cloned.1.call-start = ((), (), s32[]{:S(2)}) async-start(), calls=%async_computation.5 | async-start | bytes 4718592 | tf_op jit(solution)/shard_map/reduce_scatter | solution.py:392
  106.5 1.6 copy-start.4
  108.1 1.2 copy-start.6
  114.3 2.0 copy-start
  116.3 0.7 copy-start.10
  116.3 35.2 %copy-start.7 = (bf16[128,2048]{1,0:T(8,128)(2,1)S(1)}, bf16[128,2048]{1,0:T(8,128)(2,1)}, u32[]{:S(2)}) copy-start(bf16[128,2048]{1,0:T(8,128)(2,1)} %res_ref.1) | copy-start | bytes 1572868
  116.3 35.2 %copy-start.9 = (f32[2048]{0:T(1024)S(1)}, f32[2048]{0:T(1024)}, u32[]{:S(2)}) copy-start(f32[2048]{0:T(1024)} %param.24) | copy-start | bytes 24580
  151.5 1.0 copy-start.8
  156.9 130.5 %copy-start.1 = (bf16[2,2048,512]{2,1,0:T(8,128)(2,1)S(1)}, bf16[2,2048,512]{2,1,0:T(8,128)(2,1)}, u32[]{:S(2)}) copy-start(bf16[2,2048,512]{2,1,0:T(8,128)(2,1)} %wg_ref.1) | copy-start | bytes 12582916
  317.0 125.5 %copy-start.11 = (f32[128,10]{0,1:T(8,128)S(1)}, f32[128,10]{0,1:T(8,128)}, u32[]{:S(2)}) copy-start(f32[128,10]{0,1:T(8,128)} %param.29) | copy-start | bytes 15364
Sparse Core Ops, SparseCore 0:
  116.4 35.0 reduce-scatter.1

commit v2 on v1

--- a/solution.py
+++ b/solution.py
@@ -8,6 +8,7 @@
 from jax.sharding import PartitionSpec as P
 
 CHUNK = 128
+PER_STEP = 4
 CAP = 10
 F32 = jnp.float32
 BF16 = jnp.bfloat16
@@ -38,28 +39,32 @@
     return both[:, :width] + both[:, width:]
 
 
-def unit_lower_inverse(lower, row, col):
+def unit_lower_inverses(lowers, row, col):
     eye = (row == col).astype(F32)
-    diag = jnp.where(row // 16 == col // 16, lower, 0.0)
-    inverse = eye - diag
-    power = halves(-diag)
+    near = row // 16 == col // 16
+    diags = [jnp.where(near, low, 0.0) for low in lowers]
+    inverses = [eye - diag for diag in diags]
+    powers = [halves(-diag) for diag in diags]
     for step in range(3):
-        power = halves(product(power, power))
-        inverse = inverse + product(halves(inverse), power)
+        powers = [halves(product(power, power)) for power in powers]
+        inverses = [inv + product(halves(inv), power) for inv, power in zip(inverses, powers)]
     size = 16
-    while size < lower.shape[0]:
-        below = jnp.where((row // (2 * size) == col // (2 * size)) & (row // size != col // size), lower, 0.0)
-        inv = halves(inverse)
-        inverse = inverse - product(halves(product(inv, halves(below))), inv)
+    while size < row.shape[0]:
+        pick = (row // (2 * size) == col // (2 * size)) & (row // size != col // size)
+        invs = [halves(inv) for inv in inverses]
+        crossed = [halves(product(inv, halves(jnp.where(pick, low, 0.0)))) for inv, low in zip(invs, lowers)]
+        inverses = [full - product(cro, inv) for full, cro, inv in zip(inverses, crossed, invs)]
         size = size * 2
-    return inverse
+    return inverses
 
 
 def delta_kernel(ds_ref, q_ref, k_ref, v_ref, r_ref, o_ref, msg_ref, state_ref):
     step = pl.program_id(0)
     heads = v_ref.shape[0]
     group = heads // q_ref.shape[0]
-    c, d = q_ref.shape[1], q_ref.shape[2]
+    d = q_ref.shape[2]
+    c = CHUNK
+    per_step = q_ref.shape[1] // c
     row = lax.broadcasted_iota(jnp.int32, (c, c), 0)
     col = lax.broadcasted_iota(jnp.int32, (c, c), 1)
     causal = row >= col
@@ -71,51 +76,87 @@
         for h in range(heads):
             state_ref[h] = jnp.concatenate([eye, jnp.zeros_like(eye)], axis=1)
 
-    ds = ds_ref[0]
     upto = (row <= col).astype(BF16)
-    d0 = ds.astype(BF16)
-    rest = ds - d0.astype(F32)
-    d1 = rest.astype(BF16)
-    d2 = (rest - d1.astype(F32)).astype(BF16)
-    cum = mxu(d0, upto) + mxu(d1, upto) + mxu(d2, upto)
-    half = jnp.where(lax.broadcasted_iota(jnp.int32, ds.shape, 0) < heads, cum, ds)
-    columns = jnp.transpose(half, (1, 0))
+    rows_of, columns_of = [], []
+    for n in range(per_step):
+        ds = ds_ref[n]
+        d0 = ds.astype(BF16)
+        rest = ds - d0.astype(F32)
+        d1 = rest.astype(BF16)
+        d2 = (rest - d1.astype(F32)).astype(BF16)
+        cum = mxu(d0, upto) + mxu(d1, upto) + mxu(d2, upto)
+        half = jnp.where(lax.broadcasted_iota(jnp.int32, ds.shape, 0) < heads, cum, ds)
+        rows_of.append(half)
+        columns_of.append(jnp.transpose(half, (1, 0)))
 
     keyed = []
-    for g in range(q_ref.shape[0]):
-        q, k = q_ref[g], k_ref[g]
-        qf, kf = q.astype(F32), k.astype(F32)
-        q_col = (d ** -0.5) / jnp.sqrt(jnp.sum(qf * qf, axis=1, keepdims=True) + 1e-06)
-        k_col = 1.0 / jnp.sqrt(jnp.sum(kf * kf, axis=1, keepdims=True) + 1e-06)
-        gram = mxu(k, k, ((1,), (1,)))
-        k_row = 1.0 / jnp.sqrt(jnp.sum(jnp.where(row == col, gram, 0.0), axis=0, keepdims=True) + 1e-06)
-        gram = gram * (k_col * k_row)
-        cross = mxu(q, k, ((1,), (1,))) * (q_col * k_row)
-        keyed.append((qf, k, kf, q_col, k_col, k_row, gram, cross, jnp.transpose(kf, (1, 0)).astype(BF16)))
-
+    for n in range(per_step):
+        span = pl.ds(n * c, c)
+        for g in range(q_ref.shape[0]):
+            q, k = q_ref[g, span], k_ref[g, span]
+            qf, kf = q.astype(F32), k.astype(F32)
+            q_col = (d ** -0.5) / jnp.sqrt(jnp.sum(qf * qf, axis=1, keepdims=True) + 1e-06)
+            k_col = 1.0 / jnp.sqrt(jnp.sum(kf * kf, axis=1, keepdims=True) + 1e-06)
+            gram = mxu(k, k, ((1,), (1,)))
+            k_row = 1.0 / jnp.sqrt(jnp.sum(jnp.where(row == col, gram, 0.0), axis=0, keepdims=True) + 1e-06)
+            gram = gram * (k_col * k_row)
+            cross = mxu(q, k, ((1,), (1,))) * (q_col * k_row)
+            keyed.append((qf, k, q_col, k_col, k_row, gram, cross, jnp.transpose(kf, (1, 0)).astype(BF16)))
+
+    lowers, mixings = [], []
+    for n in range(per_step):
+        for h in range(heads):
+            gram, cross = keyed[n * q_ref.shape[0] + h // group][5:7]
+            cum_col, beta_col = columns_of[n][:, h : h + 1], columns_of[n][:, heads + h : heads + h + 1]
+            cum_row = rows_of[n][h : h + 1, :]
+            spread = jnp.where(causal, jnp.exp(jnp.where(causal, cum_col - cum_row, 0.0)), 0.0)
+            lowers.append(jnp.where(strict, beta_col * gram * spread, 0.0))
+            mixings.append((cross * spread).astype(BF16))
+    inverses = unit_lower_inverses(lowers, row, col)
+    weights, writes = [], []
+    for n in range(per_step):
+        for h in range(heads):
+            k, k_row = keyed[n * q_ref.shape[0] + h // group][1], keyed[n * q_ref.shape[0] + h // group][4]
+            cum_row, beta_row = rows_of[n][h : h + 1, :], rows_of[n][heads + h : heads + h + 1, :]
+            inverse = inverses[n * heads + h]
+            t_k = halves(inverse * (beta_row * jnp.exp(cum_row) * k_row))
+            t_v = halves(inverse * beta_row)
+            v = v_ref[h, pl.ds(n * c, c)]
+            weights.append(
+                mxu(jnp.concatenate(t_k, axis=1), jnp.concatenate([k, k], axis=0)).astype(BF16)
+            )
+            writes.append(mxu(jnp.concatenate(t_v, axis=1), jnp.concatenate([v, v], axis=0)))
+
+    states = [state_ref[h] for h in range(heads)]
+    for n in range(per_step):
+        span = pl.ds(n * c, c)
+        bases = [state.astype(BF16) for state in states]
+        reads = [mxu(weights[n * heads + h], bases[h]) for h in range(heads)]
+        freshes, tails = [], []
+        for h in range(heads):
+            k_col = keyed[n * q_ref.shape[0] + h // group][3]
+            cum_col = columns_of[n][:, h : h + 1]
+            closing = rows_of[n][h : h + 1, c - 1 : c]
+            written = writes[n * heads + h]
+            fresh = jnp.concatenate([-reads[h][:, :d], written - reads[h][:, d:]], axis=1)
+            freshes.append(fresh.astype(BF16))
+            tails.append((fresh * (k_col * jnp.exp(closing - cum_col))).astype(BF16))
+        for h in range(heads):
+            closing = rows_of[n][h : h + 1, c - 1 : c]
+            k_t = keyed[n * q_ref.shape[0] + h // group][7]
+            states[h] = jnp.exp(closing) * states[h] + mxu(k_t, tails[h])
+        for h in range(heads):
+            qf, q_col = keyed[n * q_ref.shape[0] + h // group][0], keyed[n * q_ref.shape[0] + h // group][2]
+            cum_col = columns_of[n][:, h : h + 1]
+            query = (qf * (q_col * jnp.exp(cum_col))).astype(BF16)
+            out = mxu(
+                jnp.concatenate([query, mixings[n * heads + h]], axis=1),
+                jnp.concatenate([bases[h], freshes[h]], axis=0),
+            )
+            r_ref[h, span] = out[:, :d].astype(BF16)
+            o_ref[h, span] = out[:, d:]
     for h in range(heads):
-        qf, k, kf, q_col, k_col, k_row, gram, cross, k_t = keyed[h // group]
-        cum_col, beta_col = columns[:, h : h + 1], columns[:, heads + h : heads + h + 1]
-        cum_row, beta_row = half[h : h + 1, :], half[heads + h : heads + h + 1, :]
-        closing = cum_row[:, c - 1 : c]
-        spread = jnp.where(causal, jnp.exp(jnp.where(causal, cum_col - cum_row, 0.0)), 0.0)
-        lower = jnp.where(strict, beta_col * gram * spread, 0.0)
-        mixing = cross * spread
-        inverse = unit_lower_inverse(lower, row, col)
-        t_k = halves(inverse * (beta_row * jnp.exp(cum_row) * k_row))
-        t_v = halves(inverse * beta_row)
-        v = v_ref[h]
-        weighted = mxu(jnp.concatenate(t_k, axis=1), jnp.concatenate([k, k], axis=0))
-        written = mxu(jnp.concatenate(t_v, axis=1), jnp.concatenate([v, v], axis=0))
-        state = state_ref[h]
-        state_b = state.astype(BF16)
-        fresh = jnp.concatenate([jnp.zeros_like(written), written], axis=1) - mxu(weighted.astype(BF16), state_b)
-        reads = jnp.concatenate([qf * (q_col * jnp.exp(cum_col)), mixing], axis=1).astype(BF16)
-        out = mxu(reads, jnp.concatenate([state_b, fresh.astype(BF16)], axis=0))
-        r_ref[h] = out[:, :d].astype(BF16)
-        o_ref[h] = out[:, d:]
-        tail = (fresh * (k_col * jnp.exp(closing - cum_col))).astype(BF16)
-        state_ref[h] = jnp.exp(closing) * state + mxu(k_t, tail)
+        state_ref[h] = states[h]
 
     @pl.when(step == pl.num_programs(0) - 1)
     def _():
@@ -134,18 +175,19 @@
     heads, seq, dv = v.shape
     kh, _, dk = q.shape
     wide = dv // parts
+    rows = PER_STEP * CHUNK
     return pl.pallas_call(
         delta_kernel,
-        grid=(seq // CHUNK,),
+        grid=(seq // rows,),
         in_specs=[
-            pl.BlockSpec((1, 2 * heads, CHUNK), lambda i: (i, 0, 0)),
-            pl.BlockSpec((kh, CHUNK, dk), lambda i: (0, i, 0)),
-            pl.BlockSpec((kh, CHUNK, dk), lambda i: (0, i, 0)),
-            pl.BlockSpec((heads, CHUNK, dv), lambda i: (0, i, 0)),
+            pl.BlockSpec((PER_STEP, 2 * heads, CHUNK), lambda i: (i, 0, 0)),
+            pl.BlockSpec((kh, rows, dk), lambda i: (0, i, 0)),
+            pl.BlockSpec((kh, rows, dk), lambda i: (0, i, 0)),
+            pl.BlockSpec((heads, rows, dv), lambda i: (0, i, 0)),
         ],
         out_specs=[
-            pl.BlockSpec((heads, CHUNK, dk), lambda i: (0, i, 0)),
-            pl.BlockSpec((heads, CHUNK, dv), lambda i: (0, i, 0)),
+            pl.BlockSpec((heads, rows, dk), lambda i: (0, i, 0)),
+            pl.BlockSpec((heads, rows, dv), lambda i: (0, i, 0)),
             pl.BlockSpec((heads, parts, dk + wide, dk), lambda i: (0, 0, 0, 0)),
         ],
         out_shape=[
@@ -155,7 +197,7 @@
         ],
         scratch_shapes=[VMEM((heads, dk, dk + dv), F32)],
         compiler_params=pltpu.CompilerParams(
-            dimension_semantics=("arbitrary",), vmem_limit_bytes=40 * MIB
+            dimension_semantics=("arbitrary",), vmem_limit_bytes=56 * MIB
         ),
         name="delta_local",
     )(ds, q, k, v)
@@ -183,21 +225,19 @@
     )(msg)
 
 
-def gate_kernel(r_ref, o_ref, s_ref, g_ref, gain_ref, w_ref, out_ref):
-    parts = []
+def gate_kernel(r_ref, o_ref, s_ref, g_ref, gain_ref, out_ref):
+    d = r_ref.shape[2]
     for h in range(r_ref.shape[0]):
         core = o_ref[h] + mxu(r_ref[h], s_ref[h], ((1,), (1,)))
         root = jnp.sqrt(jnp.mean(core * core, axis=1, keepdims=True) + 1e-06)
         gate = g_ref[h].astype(F32)
         silu = gate / (1.0 + jnp.exp(-gate))
-        parts.append((core / root * gain_ref[...] * silu).astype(BF16))
-    out_ref[...] = mxu(jnp.concatenate(parts, axis=1), w_ref[...]).astype(BF16)
-
-
-def gate_project(r, o, states, gate, gain, weight):
+        out_ref[:, h * d : (h + 1) * d] = (core / root * gain_ref[...] * silu).astype(BF16)
+
+
+def gated_rows(r, o, states, gate, gain):
     heads, seq, d = r.shape
     rows = 256
-    width = weight.shape[1]
     by_rows = pl.BlockSpec((heads, rows, d), lambda i: (0, i, 0))
     return pl.pallas_call(
         gate_kernel,
@@ -208,15 +248,41 @@
             pl.BlockSpec((heads, d, d), lambda i: (0, 0, 0)),
             by_rows,
             pl.BlockSpec((1, d), lambda i: (0, 0)),
-            pl.BlockSpec(weight.shape, lambda i: (0, 0)),
-        ],
-        out_specs=pl.BlockSpec((rows, width), lambda i: (i, 0)),
-        out_shape=jax.ShapeDtypeStruct((seq, width), BF16),
-        compiler_params=pltpu.CompilerParams(
-            dimension_semantics=("arbitrary",), vmem_limit_bytes=40 * MIB
-        ),
-        name="gate_project",
-    )(r, o, states, gate, gain, weight)
+        ],
+        out_specs=pl.BlockSpec((rows, heads * d), lambda i: (i, 0)),
+        out_shape=jax.ShapeDtypeStruct((seq, heads * d), BF16),
+        compiler_params=pltpu.CompilerParams(dimension_semantics=("arbitrary",), vmem_limit_bytes=56 * MIB),
+        name="gated_rows",
+    )(r, o, states, gate, gain)
+
+
+def project_kernel(g_ref, w_ref, out_ref):
+    part = mxu(g_ref[0], w_ref[...])
+
+    @pl.when(pl.program_id(0) == 0)
+    def _():
+        out_ref[...] = part
+
+    @pl.when(pl.program_id(0) > 0)
+    def _():
+        out_ref[...] += part
+
+
+def project(gated, weight):
+    count, toks, deep = gated.shape
+    width = weight.shape[1]
+    return pl.pallas_call(
+        project_kernel,
+        grid=(count,),
+        in_specs=[
+            pl.BlockSpec((1, toks, deep), lambda i: (i, 0, 0)),
+            pl.BlockSpec((deep, width), lambda i: (i, 0)),
+        ],
+        out_specs=pl.BlockSpec((toks, width), lambda i: (0, 0)),
+        out_shape=jax.ShapeDtypeStruct((toks, width), F32),
+        compiler_params=pltpu.CompilerParams(dimension_semantics=("arbitrary",), vmem_limit_bytes=46 * MIB),
+        name="project",
+    )(gated, weight)
 
 
 def slot_kernel(experts, ids_ref, out_ref):
@@ -247,7 +313,7 @@
 def dispatch_kernel(part_ref, res_ref, gain_ref, slot_ref, att_ref, send_ref, flat_ref):
     toks, width = part_ref.shape
     pieces = width // 128
-    attended = (res_ref[...].astype(F32) + part_ref[...].astype(F32)).astype(BF16)
+    attended = (res_ref[...].astype(F32) + part_ref[...]).astype(BF16)
     att_ref[...] = attended
     settled = attended.astype(F32)
     root = jnp.sqrt(jnp.mean(settled * settled, axis=1, keepdims=True) + 1e-06)
@@ -275,7 +341,7 @@
             jax.ShapeDtypeStruct((count, pieces, 128), BF16),
         ],
         scratch_shapes=[VMEM((toks * pieces, 128), F32)],
-        compiler_params=pltpu.CompilerParams(vmem_limit_bytes=40 * MIB),
+        compiler_params=pltpu.CompilerParams(vmem_limit_bytes=24 * MIB),
         name="dispatch",
     )(part, residual, gain, slots)
 
@@ -299,7 +365,7 @@
 
 def run_experts(x, gate_proj, up_proj, down_proj):
     count, local, tall, lanes = x.shape
-    sources = 32
+    sources = 64
     rows = sources * tall // 16
     tokens = pl.BlockSpec((sources, 1, tall, lanes), lambda e, i: (i, e, 0, 0))
     return pl.pallas_call(
@@ -315,7 +381,7 @@
         out_shape=jax.ShapeDtypeStruct(x.shape, BF16),
         scratch_shapes=[VMEM((sources * tall, lanes), F32)],
         compiler_params=pltpu.CompilerParams(
-            dimension_semantics=("arbitrary", "arbitrary"), vmem_limit_bytes=48 * MIB
+            dimension_semantics=("arbitrary", "arbitrary"), vmem_limit_bytes=56 * MIB
         ),
         name="experts",
     )(x, gate_proj, up_proj, down_proj)
@@ -346,7 +412,7 @@
         out_specs=pl.BlockSpec(memory_space=VMEM),
         out_shape=jax.ShapeDtypeStruct((toks, pieces * lanes), BF16),
         scratch_shapes=[VMEM((toks * pieces, lanes), F32)],
-        compiler_params=pltpu.CompilerParams(vmem_limit_bytes=40 * MIB),
+        compiler_params=pltpu.CompilerParams(vmem_limit_bytes=24 * MIB),
         name="combine",
     )(back, slots, gates)
 
@@ -371,12 +437,14 @@
     seq, heads, dv = values.shape
     dk = queries.shape[2]
     n_ctx = lax.axis_size("ctx")
-    n_dev = n_ctx * lax.axis_size("exp")
+    n_exp = lax.axis_size("exp")
+    n_dev = n_ctx * n_exp
     parts = n_ctx // heads
     wide = dv // parts
     local_experts = gate_proj.shape[0]
     toks, width = residual.shape
 
+    whole_weight = lax.all_gather(out_weight, "exp", axis=0, tiled=True)
     slots = slots_of(expert_ids.T, local_experts * n_dev)
     gates = route_gates.T
 
@@ -388,8 +456,9 @@
     reads, local_out, msg = local_delta(ds, by_head(queries), by_head(key_vectors), by_head(values), parts)
     msg = lax.all_to_all(msg.reshape(n_ctx, dk + wide, dk), "ctx", 0, 0, tiled=True)
     states = lax.all_to_all(prefix_states(msg, wide), "ctx", 0, 0, tiled=True).reshape(heads, dv, dk)
-    share = gate_project(reads, local_out, states, by_head(out_gate), head_gain.reshape(1, dv), out_weight)
-    summed = lax.psum_scatter(share, "exp", scatter_dimension=0, tiled=True)
+    gated = gated_rows(reads, local_out, states, by_head(out_gate), head_gain.reshape(1, dv))
+    gated = lax.all_to_all(gated.reshape(n_exp, toks, heads * dv), "exp", 0, 0, tiled=True)
+    summed = project(gated, whole_weight)
     attended, send = dispatch(
         summed, residual, post_gain.reshape(1, width), slots, n_dev * local_experts * CAP
     )

time: 455 us -> 420 us (0.923)
  Pallas kernels: 107 us -> 74.8 us
  starting transfers between devices: 3.55 us -> 11.1 us
  local copies, waits for them, and re-layouts: 13 us -> 6.49 us
    reduce_scatter x1 -> x0, waiting for transfers between devices: 34.2 us -> none  [shards(): summed = lax.psum_scatter(share, 'exp', scatter_dimension=0, tiled=True)]
    pallas_call x2 -> x3, Pallas kernels: 65.3 us -> 33.1 us  [the longest x1 18.1 us: local_delta(): pl.pallas_call(delta_kernel, grid=(seq // rows,), in_specs=[pl.BlockSpec(...]
    all_to_all x0 -> x1, waiting for transfers between devices: none -> 26.2 us  [shards(): lax.all_to_all(gated.reshape(n_exp, toks, heads * dv), 'exp', 0, 0, tiled...]
    all_to_all x0 -> x1, starting transfers between devices: none -> 7.58 us  [shards(): lax.all_to_all(gated.reshape(n_exp, toks, heads * dv), 'exp', 0, 0, tiled...]
    unnamed x28 -> x14, local copies, waits for them, and re-layouts: 11.5 us -> 4.19 us
  transfers between devices with their start and end apart: 2 -> 3, of which waited for: 2 -> 3; matrix products, arithmetic and copies ran while one was open for 0% -> 2% of each run, Pallas kernels for 0% -> 6%
where the time goes in v2:
time: 420 us; the launch traced here: 419 us
  blocking collectives  275 us (65%)
  Pallas kernels  74.8 us (18%)
  waiting for transfers between devices  36.8 us (9%)
  between operations  14.1 us (3%)
  starting transfers between devices  11.1 us (3%)
  local copies, waits for them, and re-layouts  6.49 us (2%)
    all_to_all x1, blocking collectives, shards(): lax.all_to_all(send.reshape(n_dev, local_experts, tall, 128), ('ctx', 'ex...  129 us
    all_to_all x1, blocking collectives, shards(): back = lax.all_to_all(done, ('ctx', 'exp'), 0, 0, tiled=True)  125 us
    pallas_call x1, Pallas kernels, run_experts(): pl.pallas_call(expert_kernel, grid=(local, count // sources), in_specs=[t...  29.5 us
    all_to_all x1, waiting for transfers between devices, shards(): lax.all_to_all(gated.reshape(n_exp, toks, heads * dv), 'exp', 0, 0, tiled...  26.2 us
    all_to_all x1, blocking collectives, shards(): lax.all_to_all(msg.reshape(n_ctx, dk + wide, dk), 'ctx', 0, 0, tiled=True)  20.4 us
    pallas_call x1, Pallas kernels, local_delta(): pl.pallas_call(delta_kernel, grid=(seq // rows,), in_specs=[pl.BlockSpec(...  18.1 us
    pallas_call x1, Pallas kernels, project(): pl.pallas_call(project_kernel, grid=(count,), in_specs=[pl.BlockSpec((1,...  9.78 us
  transfers between devices with their start and end apart: 3, of which 3 were waited for; matrix products, arithmetic and copies ran while one was open for 2% of the time, Pallas kernels for 6%

profile of v2, /device:TPU:1, one launch (start us, length us, event | category | flops | bytes accessed | tf_op | source)
XLA Modules:
  0.0 419.2 jit_solution(7800469442155616404)
XLA Ops:
  7.2 0.0 copy-start.4
  7.2 0.0 copy-start.2
  7.2 0.0 all-gather.2.cloned.1.call-start
  7.2 0.7 all-gather.2.cloned.1.call-update
  7.9 2.4 copy.26
  10.3 1.3 maximum_bitcast_fusion.ds_ref
  11.6 2.3 copy_bitcast_fusion.2
  13.9 18.1 %delta_local.1 = (bf16[4,1024,128]{2,1,0:T(8,128)(2,1)}, f32[4,1024,128]{2,1,0:T(8,128)}, bf16[4,4,160,128]{3,2,1,0:T(8,128)(2,1)}) custom-call(f32[8,8,128]{2,1,0:T(8,128)} %maximum_bitcast_fusion.ds_ref, bf16[2,1024,128]{2,1,0:T(8,128)(2,1)} %get-tuple-element.13.q_ref, bf16[2,1024,128]{2,1,0:T(8,128)(2,1)} %get-tuple-element.12.k_ref, ...), custom_call_target="tpu_custom_call" | custom-call | tf_op jit(solution)/shard_map/delta_local/pallas_call | solution.py:179
  32.0 20.4 %all_to_all.25.msg_ref = bf16[16,160,128]{2,1,0:T(8,128)(2,1)S(1)} all-to-all(bf16[16,160,128]{2,1,0:T(8,128)(2,1)} %bitcast.31), channel_id=1, replica_groups=mesh['ctx'=16,'exp'=8] {'ctx'}, dimensions={0} | all-to-all | bytes 1310720 | tf_op jit(solution)/shard_map/all_to_all | solution.py:457
  52.4 2.5 prefix_states.1
  55.0 3.5 all-to-all-start.1
  58.5 0.0 copy-done.4
  58.5 1.1 copy.25
  59.7 5.6 %all-to-all-done.1 = bf16[16,32,128]{2,1,0:T(8,128)(2,1)S(1)} async-done(((bf16[16,32,128]{2,1,0:T(8,128)(2,1)}), bf16[16,32,128]{2,1,0:T(8,128)(2,1)S(1)}, u32[]{:S(2)}, u32[]{:S(2)}) %all-to-all-start.1) | async-done | bytes 131104 | tf_op jit(solution)/shard_map/all_to_all | solution.py:458
  65.3 0.0 copy-start.5
  65.3 0.7 copy-done.5
  66.0 5.2 %gated_rows.1 = bf16[1024,512]{1,0:T(8,128)(2,1)} custom-call(bf16[4,1024,128]{2,1,0:T(8,128)(2,1)} %get-tuple-element.7.r_ref, f32[4,1024,128]{2,1,0:T(8,128)} %get-tuple-element.8.o_ref, bf16[4,128,128]{2,1,0:T(8,128)(2,1)} %bitcast.32, bf16[4,1024,128]{2,1,0:T(8,128)(2,1)} %bitcast.29, f32[1,128]{1,0:T(1,128)} %bitcast.33), custom_call_target="tpu_custom_call" | custom-call | tf_op jit(solution)/shard_map/gated_rows/pallas_call | solution.py:242
  71.2 0.0 copy-start
  71.2 0.0 copy-start.1
  71.2 7.6 %all-to-all-start.2 = ((bf16[8,128,512]{2,1,0:T(8,128)(2,1)}), bf16[8,128,512]{2,1,0:T(8,128)(2,1)S(1)}, u32[]{:S(2)}, u32[]{:S(2)}) async-start(bf16[8,128,512]{2,1,0:T(8,128)(2,1)} %bitcast.30), calls=%async_computation.2 | async-start | bytes 2097152 | tf_op jit(solution)/shard_map/all_to_all | solution.py:460
  78.8 0.0 copy-done.2
  78.8 0.4 slots.1.slot_ref
  79.1 26.2 %all-to-all-done.2.g_ref = bf16[8,128,512]{2,1,0:T(8,128)(2,1)S(1)} async-done(((bf16[8,128,512]{2,1,0:T(8,128)(2,1)}), bf16[8,128,512]{2,1,0:T(8,128)(2,1)S(1)}, u32[]{:S(2)}, u32[]{:S(2)}) %all-to-all-start.2) | async-done | bytes 1048608 | tf_op jit(solution)/shard_map/all_to_all | solution.py:460
  105.4 4.2 all-gather.2.cloned.1.call-done.w_ref
  109.6 9.8 %project.1.part_ref = f32[128,2048]{1,0:T(8,128)S(1)} custom-call(bf16[8,128,512]{2,1,0:T(8,128)(2,1)S(1)} %all-to-all-done.2.g_ref, bf16[4096,2048]{1,0:T(8,128)(2,1)} %all-gather.2.cloned.1.call-done.w_ref), custom_call_target="tpu_custom_call" | custom-call | tf_op jit(solution)/shard_map/project/pallas_call | solution.py:274
  119.4 0.0 copy-done
  119.4 0.0 copy-done.1
  119.4 4.3 %dispatch.1 = (bf16[128,2048]{1,0:T(8,128)(2,1)}, bf16[2560,16,128]{2,1,0:T(8,128)(2,1)S(1)}) custom-call(f32[128,2048]{1,0:T(8,128)S(1)} %project.1.part_ref, bf16[128,2048]{1,0:T(8,128)(2,1)S(1)} %copy-done, f32[1,2048]{1,0:T(1,128)S(1)} %bitcast.25, s32[10,128]{1,0:T(8,128)S(1)} %slots.1.slot_ref), custom_call_target="tpu_custom_call" | custom-call | tf_op jit(solution)/shard_map/dispatch/pallas_call | solution.py:335
  123.7 128.8 %all_to_all.26.x_ref = bf16[128,2,160,128]{3,2,1,0:T(8,128)(2,1)} all-to-all(bf16[128,2,160,128]{3,2,1,0:T(8,128)(2,1)S(1)} %bitcast.24), channel_id=1, replica_groups=mesh['ctx'=16,'exp'=8] {'ctx','exp'}, dimensions={0} | all-to-all | bytes 20971520 | tf_op jit(solution)/shard_map/all_to_all | solution.py:466
  252.5 29.5 %experts.1 = bf16[128,2,160,128]{3,2,1,0:T(8,128)(2,1)} custom-call(bf16[128,2,160,128]{3,2,1,0:T(8,128)(2,1)} %all_to_all.26.x_ref, bf16[2,2048,512]{2,1,0:T(8,128)(2,1)} %wg_ref.1, bf16[2,2048,512]{2,1,0:T(8,128)(2,1)} %wu_ref.1, bf16[2,512,2048]{2,1,0:T(8,128)(2,1)} %wd_ref.1), custom_call_target="tpu_custom_call" | custom-call | tf_op jit(solution)/shard_map/experts/pallas_call | solution.py:371
  282.0 0.0 copy-start.3
  282.0 125.4 %all_to_all.27 = bf16[128,2,160,128]{3,2,1,0:T(8,128)(2,1)S(1)} all-to-all(bf16[128,2,160,128]{3,2,1,0:T(8,128)(2,1)} %experts.1), channel_id=1, replica_groups=mesh['ctx'=16,'exp'=8] {'ctx','exp'}, dimensions={0} | all-to-all | bytes 20971520 | tf_op jit(solution)/shard_map/all_to_all | solution.py:470
  407.4 0.0 copy-done.3
  407.4 5.0 %combine.1 = bf16[128,2048]{1,0:T(8,128)(2,1)} custom-call(bf16[2560,16,128]{2,1,0:T(8,128)(2,1)S(1)} %bitcast.23, s32[10,128]{1,0:T(8,128)S(1)} %slots.1.slot_ref, f32[10,128]{1,0:T(8,128)S(1)} %bitcast.27), custom_call_target="tpu_custom_call" | custom-call | tf_op jit(solution)/shard_map/combine/pallas_call | solution.py:409
Async XLA Ops:
  7.2 51.4 %copy-start.4 = (bf16[1024,4,128]{2,1,0:T(4,128)(2,1)S(1)}, bf16[1024,4,128]{2,1,0:T(4,128)(2,1)}, u32[]{:S(2)}) copy-start(bf16[1024,4,128]{2,1,0:T(4,128)(2,1)} %param.18) | copy-start | bytes 3145732
  7.2 71.6 %copy-start.2 = (s32[128,10]{0,1:T(8,128)S(1)}, s32[128,10]{0,1:T(8,128)}, u32[]{:S(2)}) copy-start(s32[128,10]{0,1:T(8,128)} %param.28) | copy-start | bytes 15364
  7.2 102.4 %all-gather.2.cloned.1.call-start = ((), (), s32[]{:S(2)}) async-start(), calls=%async_computation.5 | async-start | bytes 18874368 | tf_op jit(solution)/shard_map/all_gather | solution.py:447
  55.0 10.3 %all-to-all-start.1 = ((bf16[16,32,128]{2,1,0:T(8,128)(2,1)}), bf16[16,32,128]{2,1,0:T(8,128)(2,1)S(1)}, u32[]{:S(2)}, u32[]{:S(2)}) async-start(bf16[16,32,128]{2,1,0:T(8,128)(2,1)} %prefix_states.1), calls=%async_computation.1 | async-start | bytes 262144 | tf_op jit(solution)/shard_map/all_to_all | solution.py:458
  65.3 0.7 copy-start.5
  71.2 48.2 %copy-start = (bf16[128,2048]{1,0:T(8,128)(2,1)S(1)}, bf16[128,2048]{1,0:T(8,128)(2,1)}, u32[]{:S(2)}) copy-start(bf16[128,2048]{1,0:T(8,128)(2,1)} %res_ref.1) | copy-start | bytes 1572868
  71.2 48.2 %copy-start.1 = (f32[2048]{0:T(1024)S(1)}, f32[2048]{0:T(1024)}, u32[]{:S(2)}) copy-start(f32[2048]{0:T(1024)} %param.24) | copy-start | bytes 24580
  71.2 34.2 %all-to-all-start.2 = ((bf16[8,128,512]{2,1,0:T(8,128)(2,1)}), bf16[8,128,512]{2,1,0:T(8,128)(2,1)S(1)}, u32[]{:S(2)}, u32[]{:S(2)}) async-start(bf16[8,128,512]{2,1,0:T(8,128)(2,1)} %bitcast.30), calls=%async_computation.2 | async-start | bytes 2097152 | tf_op jit(solution)/shard_map/all_to_all | solution.py:460
  282.0 125.4 %copy-start.3 = (f32[128,10]{0,1:T(8,128)S(1)}, f32[128,10]{0,1:T(8,128)}, u32[]{:S(2)}) copy-start(f32[128,10]{0,1:T(8,128)} %param.29) | copy-start | bytes 15364
Sparse Core Ops, SparseCore 0:
  9.7 99.7 all-gather.1

commit v3 on v2

--- a/solution.py
+++ b/solution.py
@@ -10,6 +10,7 @@
 CHUNK = 128
 PER_STEP = 4
 CAP = 10
+PITCH = 24
 F32 = jnp.float32
 BF16 = jnp.bfloat16
 VMEM = pltpu.VMEM
@@ -225,64 +226,102 @@
     )(msg)
 
 
-def gate_kernel(r_ref, o_ref, s_ref, g_ref, gain_ref, out_ref):
+def gate_kernel(place_ref, r_ref, o_ref, s_ref, g_ref, gain_ref, keep_ref, give_ref):
     d = r_ref.shape[2]
-    for h in range(r_ref.shape[0]):
-        core = o_ref[h] + mxu(r_ref[h], s_ref[h], ((1,), (1,)))
-        root = jnp.sqrt(jnp.mean(core * core, axis=1, keepdims=True) + 1e-06)
-        gate = g_ref[h].astype(F32)
-        silu = gate / (1.0 + jnp.exp(-gate))
-        out_ref[:, h * d : (h + 1) * d] = (core / root * gain_ref[...] * silu).astype(BF16)
-
-
-def gated_rows(r, o, states, gate, gain):
+    rows = keep_ref.shape[1]
+    core = place_ref[0]
+    for part, out_ref in ((core, keep_ref), (1 - core, give_ref)):
+        span = pl.ds(pl.multiple_of(part * rows, rows), rows)
+        for h in range(r_ref.shape[0]):
+            value = o_ref[h, span, :] + mxu(r_ref[h, span, :], s_ref[h], ((1,), (1,)))
+            root = jnp.sqrt(jnp.mean(value * value, axis=1, keepdims=True) + 1e-06)
+            gate = g_ref[h, span, :].astype(F32)
+            silu = gate / (1.0 + jnp.exp(-gate))
+            out_ref[0, :, h * d : (h + 1) * d] = (value / root * gain_ref[...] * silu).astype(BF16)
+
+
+def gated_rows(place, r, o, states, gate, gain, toks):
     heads, seq, d = r.shape
-    rows = 256
-    by_rows = pl.BlockSpec((heads, rows, d), lambda i: (0, i, 0))
+    rows = 2 * toks
+    by_rows = pl.BlockSpec((heads, rows, d), lambda i, p: (0, i, 0))
+    out = pl.BlockSpec((1, toks, heads * d), lambda i, p: (i, 0, 0))
+    shape = jax.ShapeDtypeStruct((seq // rows, toks, heads * d), BF16)
     return pl.pallas_call(
         gate_kernel,
-        grid=(seq // rows,),
-        in_specs=[
-            by_rows,
-            by_rows,
-            pl.BlockSpec((heads, d, d), lambda i: (0, 0, 0)),
-            by_rows,
-            pl.BlockSpec((1, d), lambda i: (0, 0)),
-        ],
-        out_specs=pl.BlockSpec((rows, heads * d), lambda i: (i, 0)),
-        out_shape=jax.ShapeDtypeStruct((seq, heads * d), BF16),
+        grid_spec=pltpu.PrefetchScalarGridSpec(
+            num_scalar_prefetch=1,
+            grid=(seq // rows,),
+            in_specs=[
+                by_rows,
+                by_rows,
+                pl.BlockSpec((heads, d, d), lambda i, p: (0, 0, 0)),
+                by_rows,
+                pl.BlockSpec((1, d), lambda i, p: (0, 0)),
+            ],
+            out_specs=[out, out],
+        ),
+        out_shape=[shape, shape],
         compiler_params=pltpu.CompilerParams(dimension_semantics=("arbitrary",), vmem_limit_bytes=56 * MIB),
         name="gated_rows",
-    )(r, o, states, gate, gain)
-
-
-def project_kernel(g_ref, w_ref, out_ref):
-    part = mxu(g_ref[0], w_ref[...])
-
-    @pl.when(pl.program_id(0) == 0)
-    def _():
-        out_ref[...] = part
-
-    @pl.when(pl.program_id(0) > 0)
-    def _():
-        out_ref[...] += part
-
-
-def project(gated, weight):
-    count, toks, deep = gated.shape
+    )(place, r, o, states, gate, gain)
+
+
+def far_kernel(place_ref, mine_ref, got_ref, w_ref, v_ref, a_ref, b_ref):
+    part = mxu(mine_ref[0], w_ref[...]) + mxu(got_ref[0], v_ref[...])
+    half = a_ref.shape[0]
+    a_ref[...] = part[:half].astype(BF16)
+    b_ref[...] = part[half:].astype(BF16)
+
+
+def near_kernel(place_ref, mine_ref, got_ref, w_ref, v_ref, out_ref):
+    out_ref[0] = mxu(mine_ref[0], w_ref[...]) + mxu(got_ref[0], v_ref[...])
+
+
+def project(place, mine, got, weight, other, near):
+    count, toks, deep = mine.shape
     width = weight.shape[1]
-    return pl.pallas_call(
-        project_kernel,
-        grid=(count,),
-        in_specs=[
-            pl.BlockSpec((1, toks, deep), lambda i: (i, 0, 0)),
-            pl.BlockSpec((deep, width), lambda i: (i, 0)),
-        ],
-        out_specs=pl.BlockSpec((toks, width), lambda i: (0, 0)),
-        out_shape=jax.ShapeDtypeStruct((toks, width), F32),
-        compiler_params=pltpu.CompilerParams(dimension_semantics=("arbitrary",), vmem_limit_bytes=46 * MIB),
-        name="project",
-    )(gated, weight)
+    step = (lambda i: lax.rem(1 + 2 * i, 4) * (1 - i // 2)) if near else (lambda i: i + 2)
+    chunk = pl.BlockSpec((1, toks, deep), lambda i, p: (lax.rem(p[1] + step(i), count), 0, 0))
+    whole = pl.BlockSpec(weight.shape, lambda i, p: (0, 0))
+    half = jax.ShapeDtypeStruct((toks // 2, width), BF16)
+    steps = 3 if near else 1
+    return pl.pallas_call(
+        near_kernel if near else far_kernel,
+        grid_spec=pltpu.PrefetchScalarGridSpec(
+            num_scalar_prefetch=1,
+            grid=(steps,),
+            in_specs=[chunk, chunk, whole, whole],
+            out_specs=pl.BlockSpec((1, toks, width), lambda i, p: (i, 0, 0))
+            if near
+            else [pl.BlockSpec((toks // 2, width), lambda i, p: (0, 0))] * 2,
+        ),
+        out_shape=jax.ShapeDtypeStruct((3, toks, width), F32) if near else [half, half],
+        cost_estimate=pl.CostEstimate(
+            flops=4 * steps * toks * deep * width,
+            bytes_accessed=4 * weight.size + 4 * steps * toks * width,
+            transcendentals=0,
+        ),
+        compiler_params=pltpu.CompilerParams(dimension_semantics=("arbitrary",), vmem_limit_bytes=24 * MIB),
+        name="project_near" if near else "project_far",
+    )(place, mine, got, weight, other)
+
+
+def relay_kernel(near_ref, a_ref, b_ref, right_ref, left_ref):
+    half = a_ref.shape[0]
+    right_ref[:half] = (near_ref[0, :half] + a_ref[...].astype(F32)).astype(BF16)
+    right_ref[half:] = near_ref[0, half:].astype(BF16)
+    left_ref[:half] = near_ref[1, :half].astype(BF16)
+    left_ref[half:] = (near_ref[1, half:] + b_ref[...].astype(F32)).astype(BF16)
+
+
+def relay(near, first, second):
+    shape = jax.ShapeDtypeStruct(near.shape[1:], BF16)
+    return pl.pallas_call(
+        relay_kernel,
+        out_shape=[shape, shape],
+        compiler_params=pltpu.CompilerParams(vmem_limit_bytes=16 * MIB),
+        name="relay",
+    )(near, first, second)
 
 
 def slot_kernel(experts, ids_ref, out_ref):
@@ -310,10 +349,11 @@
     )(ids)
 
 
-def dispatch_kernel(part_ref, res_ref, gain_ref, slot_ref, att_ref, send_ref, flat_ref):
-    toks, width = part_ref.shape
+def dispatch_kernel(near_ref, back_ref, ahead_ref, res_ref, gain_ref, slot_ref, att_ref, send_ref, flat_ref):
+    toks, width = res_ref.shape
     pieces = width // 128
-    attended = (res_ref[...].astype(F32) + part_ref[...]).astype(BF16)
+    total = near_ref[2] + back_ref[...].astype(F32) + ahead_ref[...].astype(F32)
+    attended = (res_ref[...].astype(F32) + total).astype(BF16)
     att_ref[...] = attended
     settled = attended.astype(F32)
     root = jnp.sqrt(jnp.mean(settled * settled, axis=1, keepdims=True) + 1e-06)
@@ -328,13 +368,13 @@
             send_ref[slot_ref[k, t]] = tile
 
 
-def dispatch(part, residual, gain, slots, count):
-    toks, width = part.shape
+def dispatch(near, back, ahead, residual, gain, slots, count):
+    toks, width = residual.shape
     pieces = width // 128
     whole = pl.BlockSpec(memory_space=VMEM)
     return pl.pallas_call(
         dispatch_kernel,
-        in_specs=[whole, whole, whole, pl.BlockSpec(memory_space=pltpu.SMEM)],
+        in_specs=[whole] * 5 + [pl.BlockSpec(memory_space=pltpu.SMEM)],
         out_specs=[whole, whole],
         out_shape=[
             jax.ShapeDtypeStruct((toks, width), BF16),
@@ -343,30 +383,31 @@
         scratch_shapes=[VMEM((toks * pieces, 128), F32)],
         compiler_params=pltpu.CompilerParams(vmem_limit_bytes=24 * MIB),
         name="dispatch",
-    )(part, residual, gain, slots)
+    )(near, back, ahead, residual, gain, slots)
 
 
 def expert_kernel(x_ref, wg_ref, wu_ref, wd_ref, out_ref, flat_ref):
     sources, _, tall, lanes = x_ref.shape
-    rows = flat_ref.shape[0] // 16
-    pieces = 16
-    flat_ref[...] = x_ref[...].reshape(sources * tall, lanes).astype(F32)
+    pieces = wg_ref.shape[1] // lanes
+    rows = flat_ref.shape[0] // PITCH
+    tiles_ref = flat_ref.reshape(rows, PITCH, lanes)
+    tiles_ref[:, :pieces, :] = x_ref[...].reshape(rows, pieces, lanes).astype(F32)
     x = jnp.concatenate(
-        [flat_ref[pl.ds(j, rows, stride=pieces), :].astype(BF16) for j in range(pieces)], axis=1
+        [flat_ref[pl.ds(j, rows, stride=PITCH), :].astype(BF16) for j in range(pieces)], axis=1
     )
     gate = mxu(x, wg_ref[0])
     up = mxu(x, wu_ref[0])
     inner = (gate / (1.0 + jnp.exp(-gate)) * up).astype(BF16)
     y = mxu(inner, wd_ref[0])
     for j in range(pieces):
-        flat_ref[pl.ds(j, rows, stride=pieces), :] = y[:, j * 128 : (j + 1) * 128]
-    out_ref[...] = flat_ref[...].astype(BF16).reshape(sources, 1, tall, lanes)
+        flat_ref[pl.ds(j, rows, stride=PITCH), :] = y[:, j * lanes : (j + 1) * lanes]
+    out_ref[...] = tiles_ref[:, :pieces, :].astype(BF16).reshape(sources, 1, tall, lanes)
 
 
 def run_experts(x, gate_proj, up_proj, down_proj):
     count, local, tall, lanes = x.shape
     sources = 64
-    rows = sources * tall // 16
+    rows = sources * tall * lanes // gate_proj.shape[1]
     tokens = pl.BlockSpec((sources, 1, tall, lanes), lambda e, i: (i, e, 0, 0))
     return pl.pallas_call(
         expert_kernel,
@@ -379,7 +420,7 @@
         ],
         out_specs=tokens,
         out_shape=jax.ShapeDtypeStruct(x.shape, BF16),
-        scratch_shapes=[VMEM((sources * tall, lanes), F32)],
+        scratch_shapes=[VMEM((rows * PITCH, lanes), F32)],
         compiler_params=pltpu.CompilerParams(
             dimension_semantics=("arbitrary", "arbitrary"), vmem_limit_bytes=56 * MIB
         ),
@@ -444,7 +485,11 @@
     local_experts = gate_proj.shape[0]
     toks, width = residual.shape
 
-    whole_weight = lax.all_gather(out_weight, "exp", axis=0, tiled=True)
+    place = lax.axis_index("exp")
+    place = jnp.stack([place & 1, place >> 1])
+    shift = lambda a, by: lax.ppermute(a, "exp", [(i, (i + 2 * by) % n_exp) for i in range(n_exp)])
+    swap = lambda a: lax.ppermute(a, "exp", [(i, i ^ 1) for i in range(n_exp)])
+    other_weight = swap(out_weight)
     slots = slots_of(expert_ids.T, local_experts * n_dev)
     gates = route_gates.T
 
@@ -456,11 +501,16 @@
     reads, local_out, msg = local_delta(ds, by_head(queries), by_head(key_vectors), by_head(values), parts)
     msg = lax.all_to_all(msg.reshape(n_ctx, dk + wide, dk), "ctx", 0, 0, tiled=True)
     states = lax.all_to_all(prefix_states(msg, wide), "ctx", 0, 0, tiled=True).reshape(heads, dv, dk)
-    gated = gated_rows(reads, local_out, states, by_head(out_gate), head_gain.reshape(1, dv))
-    gated = lax.all_to_all(gated.reshape(n_exp, toks, heads * dv), "exp", 0, 0, tiled=True)
-    summed = project(gated, whole_weight)
+    mine, give = gated_rows(
+        place, reads, local_out, states, by_head(out_gate), head_gain.reshape(1, dv), toks
+    )
+    got = swap(give)
+    first, second = project(place, mine, got, out_weight, other_weight, False)
+    first, second = shift(first, 1), shift(second, -1)
+    near = project(place, mine, got, out_weight, other_weight, True)
+    right, left = relay(near, first, second)
     attended, send = dispatch(
-        summed, residual, post_gain.reshape(1, width), slots, n_dev * local_experts * CAP
+        near, shift(right, 1), shift(left, -1), residual, post_gain.reshape(1, width), slots, n_dev * local_experts * CAP
     )
     tall = CAP * width // 128
     held = lax.all_to_all(

time: 420 us -> 385 us (0.917)
  waiting for transfers between devices: 36.8 us -> 18.7 us
  between operations: 14.1 us -> 0.72 us
  Pallas kernels: 74.8 us -> 68.5 us
    all_to_all x1 -> x0, waiting for transfers between devices: 26.2 us -> none  [shards(): lax.all_to_all(gated.reshape(n_exp, toks, heads * dv), 'exp', 0, 0, tiled...]
    ppermute x0 -> x6, waiting for transfers between devices: none -> 13.7 us  [the longest x4 11.9 us: shards(): lax.ppermute(a, 'exp', [(i, (i + 2 * by) % n_exp) for i in range(n_exp)])]
    ppermute x0 -> x6, starting transfers between devices: none -> 9.48 us  [the longest x4 5.66 us: shards(): lax.ppermute(a, 'exp', [(i, (i + 2 * by) % n_exp) for i in range(n_exp)])]
    all_to_all x1 -> x0, starting transfers between devices: 7.58 us -> none  [shards(): lax.all_to_all(gated.reshape(n_exp, toks, heads * dv), 'exp', 0, 0, tiled...]
    pallas_call x1, Pallas kernels: 29.5 us -> 24.9 us  [run_experts(): pl.pallas_call(expert_kernel, grid=(local, count // sources), in_specs=[t...]
    pallas_call x3 -> x5, Pallas kernels: 19.3 us -> 17.6 us  [the longest x2 7.17 us: project(): pl.pallas_call(near_kernel if near else far_kernel, grid_spec=pltpu.Prefe...]
  transfers between devices with their start and end apart: 3 -> 7, of which waited for: 3 -> 4; matrix products, arithmetic and copies ran while one was open for 2% -> 2% of each run, Pallas kernels for 6% -> 8%
where the time goes in v3:
time: 385 us; the launch traced here: 384 us
  blocking collectives  274 us (71%)
  Pallas kernels  68.5 us (18%)
  waiting for transfers between devices  18.7 us (5%)
  starting transfers between devices  13 us (3%)
  local copies, waits for them, and re-layouts  7.51 us (2%)
    all_to_all x1, blocking collectives, shards(): lax.all_to_all(send.reshape(n_dev, local_experts, tall, 128), ('ctx', 'ex...  128 us
    all_to_all x1, blocking collectives, shards(): back = lax.all_to_all(done, ('ctx', 'exp'), 0, 0, tiled=True)  125 us
    pallas_call x1, Pallas kernels, run_experts(): pl.pallas_call(expert_kernel, grid=(local, count // sources), in_specs=[t...  24.9 us
    all_to_all x1, blocking collectives, shards(): lax.all_to_all(msg.reshape(n_ctx, dk + wide, dk), 'ctx', 0, 0, tiled=True)  20.7 us
    pallas_call x1, Pallas kernels, local_delta(): pl.pallas_call(delta_kernel, grid=(seq // rows,), in_specs=[pl.BlockSpec(...  18.1 us
    ppermute x4, waiting for transfers between devices, shards(): lax.ppermute(a, 'exp', [(i, (i + 2 * by) % n_exp) for i in range(n_exp)])  11.9 us
  transfers between devices with their start and end apart: 7, of which 4 were waited for; matrix products, arithmetic and copies ran while one was open for 2% of the time, Pallas kernels for 8%

profile of v3, /device:TPU:1, one launch (start us, length us, event | category | flops | bytes accessed | tf_op | source)
XLA Modules:
  0.0 384.2 jit_solution(16019106808382565557)
XLA Ops:
  0.6 0.0 copy-start.7
  0.6 1.5 collective-permute-start.1
  2.1 2.4 copy.26
  4.5 1.4 maximum_bitcast_fusion.ds_ref
  5.9 2.3 copy_bitcast_fusion.2
  8.2 18.1 %delta_local.1 = (bf16[4,1024,128]{2,1,0:T(8,128)(2,1)}, f32[4,1024,128]{2,1,0:T(8,128)}, bf16[4,4,160,128]{3,2,1,0:T(8,128)(2,1)}) custom-call(f32[8,8,128]{2,1,0:T(8,128)} %maximum_bitcast_fusion.ds_ref, bf16[2,1024,128]{2,1,0:T(8,128)(2,1)} %get-tuple-element.25.q_ref, bf16[2,1024,128]{2,1,0:T(8,128)(2,1)} %get-tuple-element.24.k_ref, ...), custom_call_target="tpu_custom_call" | custom-call | tf_op jit(solution)/shard_map/delta_local/pallas_call | solution.py:180
  26.2 0.0 copy-start
  26.3 20.7 %all_to_all.20.msg_ref = bf16[16,160,128]{2,1,0:T(8,128)(2,1)S(1)} all-to-all(bf16[16,160,128]{2,1,0:T(8,128)(2,1)} %bitcast.31), channel_id=1, replica_groups=mesh['ctx'=16,'exp'=8] {'ctx'}, dimensions={0} | all-to-all | bytes 1310720 | tf_op jit(solution)/shard_map/all_to_all | solution.py:502
  47.0 2.5 prefix_states.1
  49.5 3.5 all-to-all-start.1
  53.1 0.0 copy-done.7
  53.1 1.1 copy.25
  54.2 0.6 pad_add_fusion.place_ref
  54.8 0.0 copy-start.6
  54.8 5.1 %all-to-all-done.1 = bf16[16,32,128]{2,1,0:T(8,128)(2,1)S(1)} async-done(((bf16[16,32,128]{2,1,0:T(8,128)(2,1)}), bf16[16,32,128]{2,1,0:T(8,128)(2,1)S(1)}, u32[]{:S(2)}, u32[]{:S(2)}) %all-to-all-start.1) | async-done | bytes 131104 | tf_op jit(solution)/shard_map/all_to_all | solution.py:503
  59.9 0.0 copy-start.8
  59.9 0.7 copy-done.8
  60.5 5.8 %gated_rows.1 = (bf16[4,128,512]{2,1,0:T(8,128)(2,1)}, bf16[4,128,512]{2,1,0:T(8,128)(2,1)}) custom-call(s32[2]{0:T(128)} %pad_add_fusion.place_ref, bf16[4,1024,128]{2,1,0:T(8,128)(2,1)} %get-tuple-element.13.r_ref, f32[4,1024,128]{2,1,0:T(8,128)} %get-tuple-element.14.o_ref, bf16[4,128,128]{2,1,0:T(8,128)(2,1)} %bitcast.32, ...), custom_call_target="tpu_custom_call" | custom-call | tf_op jit(solution)/shard_map/gated_rows/pallas_call | solution.py:249
  66.3 2.3 collective-permute-start
  68.7 1.7 collective-permute-done.got_ref
  70.4 0.0 collective-permute-done.1.v_ref
  70.4 0.0 copy-done
  70.4 0.0 copy-done.6
  70.4 0.0 copy-start.1
  70.4 1.0 copy-done.1
  71.5 2.8 project_far.1
  74.3 1.3 collective-permute-start.2
  75.6 0.0 copy-start.4
  75.6 0.0 copy-start.2
  75.6 0.0 copy-start.3
  75.6 1.6 collective-permute-start.3
  77.2 4.3 %project_near.1.near_ref = f32[3,128,2048]{2,1,0:T(8,128)S(1)} custom-call(s32[2]{0:T(128)S(1)} %copy-done.6, bf16[4,128,512]{2,1,0:T(8,128)(2,1)S(1)} %copy-done.1, bf16[4,128,512]{2,1,0:T(8,128)(2,1)S(1)} %collective-permute-done.got_ref, bf16[512,2048]{1,0:T(8,128)(2,1)S(1)} %copy-done, bf16[512,2048]{1,0:T(8,128)(2,1)} %collective-permute-done.1.v_ref), custom_call_target="tpu_custom_call" | custom-call | flops 1610612736 | bytes 7340032 | tf_op jit(solution)/shard_map/project_near/pallas_call | solution.py:288
  81.5 1.6 collective-permute-done.2.a_ref
  83.1 0.0 collective-permute-done.3.b_ref
  83.1 0.2 relay.1
  83.3 1.0 collective-permute-start.4
  84.2 1.8 collective-permute-start.5
  86.1 0.0 copy-done.4
  86.1 0.4 slots.1.slot_ref
  86.4 10.3 %collective-permute-done.4.back_ref = bf16[128,2048]{1,0:T(8,128)(2,1)S(1)} collective-permute-done((bf16[128,2048]{1,0:T(8,128)(2,1)S(1)}, bf16[128,2048]{1,0:T(8,128)(2,1)S(1)}, u32[]{:S(2)}, u32[]{:S(2)}) %collective-permute-start.4) | collective-permute-done | bytes 524320 | tf_op jit(solution)/shard_map/ppermute | solution.py:490
  96.8 0.0 collective-permute-done.5.ahead_ref
  96.8 0.0 copy-done.2
  96.8 0.0 copy-done.3
  96.8 4.4 %dispatch.1 = (bf16[128,2048]{1,0:T(8,128)(2,1)}, bf16[2560,16,128]{2,1,0:T(8,128)(2,1)S(1)}) custom-call(f32[3,128,2048]{2,1,0:T(8,128)S(1)} %project_near.1.near_ref, bf16[128,2048]{1,0:T(8,128)(2,1)S(1)} %collective-permute-done.4.back_ref, bf16[128,2048]{1,0:T(8,128)(2,1)S(1)} %collective-permute-done.5.ahead_ref, bf16[128,2048]{1,0:T(8,128)(2,1)S(1)} %copy-done.2, ...), custom_call_target="tpu_custom_call" | custom-call | tf_op jit(solution)/shard_map/dispatch/pallas_call | solution.py:375
  101.2 127.6 %all_to_all.21.x_ref = bf16[128,2,160,128]{3,2,1,0:T(8,128)(2,1)} all-to-all(bf16[128,2,160,128]{3,2,1,0:T(8,128)(2,1)S(1)} %bitcast.25), channel_id=1, replica_groups=mesh['ctx'=16,'exp'=8] {'ctx','exp'}, dimensions={0} | all-to-all | bytes 20971520 | tf_op jit(solution)/shard_map/all_to_all | solution.py:516
  228.8 24.9 %experts.1 = bf16[128,2,160,128]{3,2,1,0:T(8,128)(2,1)} custom-call(bf16[128,2,160,128]{3,2,1,0:T(8,128)(2,1)} %all_to_all.21.x_ref, bf16[2,2048,512]{2,1,0:T(8,128)(2,1)} %wg_ref.1, bf16[2,2048,512]{2,1,0:T(8,128)(2,1)} %wu_ref.1, bf16[2,512,2048]{2,1,0:T(8,128)(2,1)} %wd_ref.1), custom_call_target="tpu_custom_call" | custom-call | tf_op jit(solution)/shard_map/experts/pallas_call | solution.py:412
  253.8 0.0 copy-start.5
  253.8 125.4 %all_to_all.22 = bf16[128,2,160,128]{3,2,1,0:T(8,128)(2,1)S(1)} all-to-all(bf16[128,2,160,128]{3,2,1,0:T(8,128)(2,1)} %experts.1), channel_id=1, replica_groups=mesh['ctx'=16,'exp'=8] {'ctx','exp'}, dimensions={0} | all-to-all | bytes 20971520 | tf_op jit(solution)/shard_map/all_to_all | solution.py:520
  379.2 0.0 copy-done.5
  379.2 5.0 %combine.1 = bf16[128,2048]{1,0:T(8,128)(2,1)} custom-call(bf16[2560,16,128]{2,1,0:T(8,128)(2,1)S(1)} %bitcast.24, s32[10,128]{1,0:T(8,128)S(1)} %slots.1.slot_ref, f32[10,128]{1,0:T(8,128)S(1)} %bitcast.28), custom_call_target="tpu_custom_call" | custom-call | tf_op jit(solution)/shard_map/combine/pallas_call | solution.py:450
Async XLA Ops:
  0.6 52.4 %copy-start.7 = (bf16[1024,4,128]{2,1,0:T(4,128)(2,1)S(1)}, bf16[1024,4,128]{2,1,0:T(4,128)(2,1)}, u32[]{:S(2)}) copy-start(bf16[1024,4,128]{2,1,0:T(4,128)(2,1)} %param.18) | copy-start | bytes 3145732
  0.6 69.8 %collective-permute-start.1 = (bf16[512,2048]{1,0:T(8,128)(2,1)}, bf16[512,2048]{1,0:T(8,128)(2,1)}, u32[]{:S(2)}, u32[]{:S(2)}) collective-permute-start(bf16[512,2048]{1,0:T(8,128)(2,1)} %w_ref.3), channel_id=1, source_target_pairs={{0,1},{1,0},{2,3},{3,2},{4,5},{5,4},{6,7},{7,6},{8,9},{9,8},{10,11... | collective-permute-start | bytes 6291464 | tf_op jit(solution)/shard_map/ppermute | solution.py:491
  26.2 44.2 %copy-start = (bf16[512,2048]{1,0:T(8,128)(2,1)S(1)}, bf16[512,2048]{1,0:T(8,128)(2,1)}, u32[]{:S(2)}) copy-start(bf16[512,2048]{1,0:T(8,128)(2,1)} %w_ref.3) | copy-start | bytes 6291460
  49.5 10.3 %all-to-all-start.1 = ((bf16[16,32,128]{2,1,0:T(8,128)(2,1)}), bf16[16,32,128]{2,1,0:T(8,128)(2,1)S(1)}, u32[]{:S(2)}, u32[]{:S(2)}) async-start(bf16[16,32,128]{2,1,0:T(8,128)(2,1)} %prefix_states.1), calls=%async_computation.1 | async-start | bytes 262144 | tf_op jit(solution)/shard_map/all_to_all | solution.py:503
  54.8 15.6 %copy-start.6 = (s32[2]{0:T(128)S(1)}, s32[2]{0:T(128)}, u32[]{:S(2)}) copy-start(s32[2]{0:T(128)} %pad_add_fusion.place_ref) | copy-start | bytes 28
  59.9 0.7 copy-start.8
  66.3 4.1 %collective-permute-start = (bf16[4,128,512]{2,1,0:T(8,128)(2,1)}, bf16[4,128,512]{2,1,0:T(8,128)(2,1)S(1)}, u32[]{:S(2)}, u32[]{:S(2)}) collective-permute-start(bf16[4,128,512]{2,1,0:T(8,128)(2,1)} %get-tuple-element.17), channel_id=1, source_target_pairs={{0,1},{1,0},{2,3},{3,2},{4,5},{5,4},{6,7},{7,6},{8,9},{9,8},{10,11... | collective-permute-start | bytes 1572872 | tf_op jit(solution)/shard_map/ppermute | solution.py:491
  70.4 1.0 copy-start.1
  74.3 8.8 %collective-permute-start.2 = (bf16[64,2048]{1,0:T(8,128)(2,1)S(1)}, bf16[64,2048]{1,0:T(8,128)(2,1)S(1)}, u32[]{:S(2)}, u32[]{:S(2)}) collective-permute-start(bf16[64,2048]{1,0:T(8,128)(2,1)S(1)} %get-tuple-element.18), channel_id=1, source_target_pairs={{0,2},{1,3},{2,4},{3,5},{4,6},{5,7},{6,0},{7,1},{8,10},{9,11},{10,... | collective-permute-start | bytes 786440 | tf_op jit(solution)/shard_map/ppermute | solution.py:490
  75.6 10.5 %copy-start.4 = (s32[128,10]{0,1:T(8,128)S(1)}, s32[128,10]{0,1:T(8,128)}, u32[]{:S(2)}) copy-start(s32[128,10]{0,1:T(8,128)} %param.28) | copy-start | bytes 15364
  75.6 21.2 %copy-start.2 = (bf16[128,2048]{1,0:T(8,128)(2,1)S(1)}, bf16[128,2048]{1,0:T(8,128)(2,1)}, u32[]{:S(2)}) copy-start(bf16[128,2048]{1,0:T(8,128)(2,1)} %res_ref.1) | copy-start | bytes 1572868
  75.6 21.2 %copy-start.3 = (f32[2048]{0:T(1024)S(1)}, f32[2048]{0:T(1024)}, u32[]{:S(2)}) copy-start(f32[2048]{0:T(1024)} %param.24) | copy-start | bytes 24580
  75.6 7.5 %collective-permute-start.3 = (bf16[64,2048]{1,0:T(8,128)(2,1)S(1)}, bf16[64,2048]{1,0:T(8,128)(2,1)S(1)}, u32[]{:S(2)}, u32[]{:S(2)}) collective-permute-start(bf16[64,2048]{1,0:T(8,128)(2,1)S(1)} %get-tuple-element.19), channel_id=1, source_target_pairs={{0,6},{1,7},{2,0},{3,1},{4,2},{5,3},{6,4},{7,5},{8,14},{9,15},{10,... | collective-permute-start | bytes 786440 | tf_op jit(solution)/shard_map/ppermute | solution.py:490
  83.3 13.5 %collective-permute-start.4 = (bf16[128,2048]{1,0:T(8,128)(2,1)S(1)}, bf16[128,2048]{1,0:T(8,128)(2,1)S(1)}, u32[]{:S(2)}, u32[]{:S(2)}) collective-permute-start(bf16[128,2048]{1,0:T(8,128)(2,1)S(1)} %get-tuple-element.20), channel_id=1, source_target_pairs={{0,2},{1,3},{2,4},{3,5},{4,6},{5,7},{6,0},{7,1},{8,10},{9,11},{10,... | collective-permute-start | bytes 1572872 | tf_op jit(solution)/shard_map/ppermute | solution.py:490
  84.2 12.5 %collective-permute-start.5 = (bf16[128,2048]{1,0:T(8,128)(2,1)S(1)}, bf16[128,2048]{1,0:T(8,128)(2,1)S(1)}, u32[]{:S(2)}, u32[]{:S(2)}) collective-permute-start(bf16[128,2048]{1,0:T(8,128)(2,1)S(1)} %get-tuple-element.21), channel_id=1, source_target_pairs={{0,6},{1,7},{2,0},{3,1},{4,2},{5,3},{6,4},{7,5},{8,14},{9,15},{10,... | collective-permute-start | bytes 1572872 | tf_op jit(solution)/shard_map/ppermute | solution.py:490
  253.8 125.4 %copy-start.5 = (f32[128,10]{0,1:T(8,128)S(1)}, f32[128,10]{0,1:T(8,128)}, u32[]{:S(2)}) copy-start(f32[128,10]{0,1:T(8,128)} %param.29) | copy-start | bytes 15364

commit v4 on v3

--- a/solution.py
+++ b/solution.py
@@ -52,9 +52,10 @@
     size = 16
     while size < row.shape[0]:
         pick = (row // (2 * size) == col // (2 * size)) & (row // size != col // size)
-        invs = [halves(inv) for inv in inverses]
-        crossed = [halves(product(inv, halves(jnp.where(pick, low, 0.0)))) for inv, low in zip(invs, lowers)]
-        inverses = [full - product(cro, inv) for full, cro, inv in zip(inverses, crossed, invs)]
+        belows = [jnp.where(pick, low, 0.0).astype(BF16) for low in lowers]
+        invs = [inv.astype(BF16) for inv in inverses]
+        crossed = [mxu(inv, below).astype(BF16) for inv, below in zip(invs, belows)]
+        inverses = [full - mxu(cro, inv) for full, cro, inv in zip(inverses, crossed, invs)]
         size = size * 2
     return inverses
 
@@ -155,7 +156,7 @@
                 jnp.concatenate([bases[h], freshes[h]], axis=0),
             )
             r_ref[h, span] = out[:, :d].astype(BF16)
-            o_ref[h, span] = out[:, d:]
+            o_ref[h, span] = out[:, d:].astype(BF16)
     for h in range(heads):
         state_ref[h] = states[h]
 
@@ -192,13 +193,13 @@
             pl.BlockSpec((heads, parts, dk + wide, dk), lambda i: (0, 0, 0, 0)),
         ],
         out_shape=[
-            jax.ShapeDtypeStruct((heads, seq, dk), BF16),
-            jax.ShapeDtypeStruct((heads, seq, dv), F32),
+            pltpu.HBM((heads, seq, dk), BF16),
+            pltpu.HBM((heads, seq, dv), BF16),
             jax.ShapeDtypeStruct((heads, parts, dk + wide, dk), BF16),
         ],
         scratch_shapes=[VMEM((heads, dk, dk + dv), F32)],
         compiler_params=pltpu.CompilerParams(
-            dimension_semantics=("arbitrary",), vmem_limit_bytes=56 * MIB
+            dimension_semantics=("arbitrary",), vmem_limit_bytes=30 * MIB
         ),
         name="delta_local",
     )(ds, q, k, v)
@@ -233,11 +234,11 @@
     for part, out_ref in ((core, keep_ref), (1 - core, give_ref)):
         span = pl.ds(pl.multiple_of(part * rows, rows), rows)
         for h in range(r_ref.shape[0]):
-            value = o_ref[h, span, :] + mxu(r_ref[h, span, :], s_ref[h], ((1,), (1,)))
-            root = jnp.sqrt(jnp.mean(value * value, axis=1, keepdims=True) + 1e-06)
+            value = o_ref[h, span, :].astype(F32) + mxu(r_ref[h, span, :], s_ref[h], ((1,), (1,)))
+            scale = 1.0 / jnp.sqrt(jnp.mean(value * value, axis=1, keepdims=True) + 1e-06)
             gate = g_ref[h, span, :].astype(F32)
-            silu = gate / (1.0 + jnp.exp(-gate))
-            out_ref[0, :, h * d : (h + 1) * d] = (value / root * gain_ref[...] * silu).astype(BF16)
+            silu = gate * lax.logistic(gate)
+            out_ref[0, :, h * d : (h + 1) * d] = (value * scale * gain_ref[...] * silu).astype(BF16)
 
 
 def gated_rows(place, r, o, states, gate, gain, toks):
@@ -273,55 +274,63 @@
     b_ref[...] = part[half:].astype(BF16)
 
 
-def near_kernel(place_ref, mine_ref, got_ref, w_ref, v_ref, out_ref):
-    out_ref[0] = mxu(mine_ref[0], w_ref[...]) + mxu(got_ref[0], v_ref[...])
-
-
-def project(place, mine, got, weight, other, near):
+def near_kernel(place_ref, ahead_ref, ahead_got_ref, behind_ref, behind_got_ref, w_ref, v_ref, right_ref, left_ref):
+    half = right_ref.shape[0]
+    for row_ref, got_ref, first, out_ref in (
+        (ahead_ref, ahead_got_ref, half, right_ref),
+        (behind_ref, behind_got_ref, 0, left_ref),
+    ):
+        rows = pl.ds(first, half)
+        out_ref[...] = (mxu(row_ref[0, rows, :], w_ref[...]) + mxu(got_ref[0, rows, :], v_ref[...])).astype(BF16)
+
+
+def rest_kernel(
+    place_ref, ahead_ref, ahead_got_ref, behind_ref, behind_got_ref, own_ref, own_got_ref, w_ref, v_ref, out_ref
+):
+    half = own_ref.shape[1] // 2
+    rows = jnp.concatenate([ahead_ref[0, :half, :], behind_ref[0, half:, :], own_ref[0]], axis=0)
+    got = jnp.concatenate([ahead_got_ref[0, :half, :], behind_got_ref[0, half:, :], own_got_ref[0]], axis=0)
+    out_ref[...] = mxu(rows, w_ref[...]) + mxu(got, v_ref[...])
+
+
+def project(kernel, steps, out_shape, name, place, mine, got, weight, other):
     count, toks, deep = mine.shape
     width = weight.shape[1]
-    step = (lambda i: lax.rem(1 + 2 * i, 4) * (1 - i // 2)) if near else (lambda i: i + 2)
-    chunk = pl.BlockSpec((1, toks, deep), lambda i, p: (lax.rem(p[1] + step(i), count), 0, 0))
-    whole = pl.BlockSpec(weight.shape, lambda i, p: (0, 0))
-    half = jax.ShapeDtypeStruct((toks // 2, width), BF16)
-    steps = 3 if near else 1
-    return pl.pallas_call(
-        near_kernel if near else far_kernel,
+    chunk = lambda step: pl.BlockSpec((1, toks, deep), lambda i, p: (lax.rem(p[1] + step, count), 0, 0))
+    whole = lambda shape: pl.BlockSpec(shape, lambda i, p: (0, 0))
+    return pl.pallas_call(
+        kernel,
         grid_spec=pltpu.PrefetchScalarGridSpec(
             num_scalar_prefetch=1,
-            grid=(steps,),
-            in_specs=[chunk, chunk, whole, whole],
-            out_specs=pl.BlockSpec((1, toks, width), lambda i, p: (i, 0, 0))
-            if near
-            else [pl.BlockSpec((toks // 2, width), lambda i, p: (0, 0))] * 2,
+            grid=(1,),
+            in_specs=[chunk(step) for step in steps for _ in range(2)] + [whole(weight.shape)] * 2,
+            out_specs=[whole(shape.shape) for shape in out_shape],
         ),
-        out_shape=jax.ShapeDtypeStruct((3, toks, width), F32) if near else [half, half],
+        out_shape=out_shape,
         cost_estimate=pl.CostEstimate(
-            flops=4 * steps * toks * deep * width,
-            bytes_accessed=4 * weight.size + 4 * steps * toks * width,
+            flops=4 * len(steps) * toks * deep * width,
+            bytes_accessed=4 * weight.size + 4 * len(steps) * toks * width,
             transcendentals=0,
         ),
         compiler_params=pltpu.CompilerParams(dimension_semantics=("arbitrary",), vmem_limit_bytes=24 * MIB),
-        name="project_near" if near else "project_far",
-    )(place, mine, got, weight, other)
-
-
-def relay_kernel(near_ref, a_ref, b_ref, right_ref, left_ref):
+        name=name,
+    )(place, *([mine, got] * len(steps)), weight, other)
+
+
+def relay_kernel(rest_ref, a_ref, b_ref, right_ref, left_ref):
     half = a_ref.shape[0]
-    right_ref[:half] = (near_ref[0, :half] + a_ref[...].astype(F32)).astype(BF16)
-    right_ref[half:] = near_ref[0, half:].astype(BF16)
-    left_ref[:half] = near_ref[1, :half].astype(BF16)
-    left_ref[half:] = (near_ref[1, half:] + b_ref[...].astype(F32)).astype(BF16)
-
-
-def relay(near, first, second):
-    shape = jax.ShapeDtypeStruct(near.shape[1:], BF16)
+    right_ref[...] = (rest_ref[:half] + a_ref[...].astype(F32)).astype(BF16)
+    left_ref[...] = (rest_ref[half : 2 * half] + b_ref[...].astype(F32)).astype(BF16)
+
+
+def relay(rest, first, second):
+    shape = jax.ShapeDtypeStruct(first.shape, BF16)
     return pl.pallas_call(
         relay_kernel,
         out_shape=[shape, shape],
         compiler_params=pltpu.CompilerParams(vmem_limit_bytes=16 * MIB),
         name="relay",
-    )(near, first, second)
+    )(rest, first, second)
 
 
 def slot_kernel(experts, ids_ref, out_ref):
@@ -349,10 +358,13 @@
     )(ids)
 
 
-def dispatch_kernel(near_ref, back_ref, ahead_ref, res_ref, gain_ref, slot_ref, att_ref, send_ref, flat_ref):
+def dispatch_kernel(rest_ref, a0_ref, a1_ref, b0_ref, b1_ref, res_ref, gain_ref, slot_ref, att_ref, send_ref, flat_ref):
     toks, width = res_ref.shape
     pieces = width // 128
-    total = near_ref[2] + back_ref[...].astype(F32) + ahead_ref[...].astype(F32)
+    own = rest_ref[toks:]
+    early = own[: toks // 2] + a0_ref[...].astype(F32) + a1_ref[...].astype(F32)
+    late = own[toks // 2 :] + b0_ref[...].astype(F32) + b1_ref[...].astype(F32)
+    total = jnp.concatenate([early, late], axis=0)
     attended = (res_ref[...].astype(F32) + total).astype(BF16)
     att_ref[...] = attended
     settled = attended.astype(F32)
@@ -368,13 +380,13 @@
             send_ref[slot_ref[k, t]] = tile
 
 
-def dispatch(near, back, ahead, residual, gain, slots, count):
+def dispatch(rest, early, late, residual, gain, slots, count):
     toks, width = residual.shape
     pieces = width // 128
     whole = pl.BlockSpec(memory_space=VMEM)
     return pl.pallas_call(
         dispatch_kernel,
-        in_specs=[whole] * 5 + [pl.BlockSpec(memory_space=pltpu.SMEM)],
+        in_specs=[whole] * 7 + [pl.BlockSpec(memory_space=pltpu.SMEM)],
         out_specs=[whole, whole],
         out_shape=[
             jax.ShapeDtypeStruct((toks, width), BF16),
@@ -383,7 +395,7 @@
         scratch_shapes=[VMEM((toks * pieces, 128), F32)],
         compiler_params=pltpu.CompilerParams(vmem_limit_bytes=24 * MIB),
         name="dispatch",
-    )(near, back, ahead, residual, gain, slots)
+    )(rest, *early, *late, residual, gain, slots)
 
 
 def expert_kernel(x_ref, wg_ref, wu_ref, wd_ref, out_ref, flat_ref):
@@ -397,7 +409,7 @@
     )
     gate = mxu(x, wg_ref[0])
     up = mxu(x, wu_ref[0])
-    inner = (gate / (1.0 + jnp.exp(-gate)) * up).astype(BF16)
+    inner = (gate * lax.logistic(gate) * up).astype(BF16)
     y = mxu(inner, wd_ref[0])
     for j in range(pieces):
         flat_ref[pl.ds(j, rows, stride=PITCH), :] = y[:, j * lanes : (j + 1) * lanes]
@@ -505,12 +517,28 @@
         place, reads, local_out, states, by_head(out_gate), head_gain.reshape(1, dv), toks
     )
     got = swap(give)
-    first, second = project(place, mine, got, out_weight, other_weight, False)
+    half = jax.ShapeDtypeStruct((toks // 2, width), BF16)
+    operands = (place, mine, got, out_weight, other_weight)
+    first, second = project(far_kernel, (2,), [half, half], "project_far", *operands)
     first, second = shift(first, 1), shift(second, -1)
-    near = project(place, mine, got, out_weight, other_weight, True)
-    right, left = relay(near, first, second)
+    ahead, behind = project(near_kernel, (1, n_exp // 2 - 1), [half, half], "project_near", *operands)
+    ahead, behind = shift(ahead, 1), shift(behind, -1)
+    [rest] = project(
+        rest_kernel,
+        (1, n_exp // 2 - 1, 0),
+        [jax.ShapeDtypeStruct((2 * toks, width), F32)],
+        "project_rest",
+        *operands,
+    )
+    right, left = relay(rest, first, second)
     attended, send = dispatch(
-        near, shift(right, 1), shift(left, -1), residual, post_gain.reshape(1, width), slots, n_dev * local_experts * CAP
+        rest,
+        (shift(right, 1), behind),
+        (ahead, shift(left, -1)),
+        residual,
+        post_gain.reshape(1, width),
+        slots,
+        n_dev * local_experts * CAP,
     )
     tall = CAP * width // 128
     held = lax.all_to_all(

time: 385 us -> 376 us (0.977)
  waiting for transfers between devices: 18.7 us -> 13.4 us
    ppermute x4 -> x6, waiting for transfers between devices: 11.9 us -> 6.62 us  [shards(): lax.ppermute(a, 'exp', [(i, (i + 2 * by) % n_exp) for i in range(n_exp)])]
    pallas_call x3 -> x4, Pallas kernels: 11.6 us -> 14.4 us  [the longest x3 9.91 us: project(): pl.pallas_call(kernel, grid_spec=pltpu.PrefetchScalarGridSpec(num_scalar_...]
  transfers between devices with their start and end apart: 7 -> 9, of which waited for: 4 -> 4; matrix products, arithmetic and copies ran while one was open for 2% -> 1% of each run, Pallas kernels for 8% -> 8%
where the time goes in v4:
time: 376 us
  blocking collectives  272 us (72%)
  Pallas kernels  67.3 us (18%)
  starting transfers between devices  14.4 us (4%)
  waiting for transfers between devices  13.4 us (4%)
  local copies, waits for them, and re-layouts  6.22 us (2%)
    all_to_all x1, blocking collectives, shards(): lax.all_to_all(send.reshape(n_dev, local_experts, tall, 128), ('ctx', 'ex...  126 us
    all_to_all x1, blocking collectives, shards(): back = lax.all_to_all(done, ('ctx', 'exp'), 0, 0, tiled=True)  125 us
    pallas_call x1, Pallas kernels, run_experts(): pl.pallas_call(expert_kernel, grid=(local, count // sources), in_specs=[t...  25 us
    all_to_all x1, blocking collectives, shards(): lax.all_to_all(msg.reshape(n_ctx, dk + wide, dk), 'ctx', 0, 0, tiled=True)  20.5 us
    pallas_call x1, Pallas kernels, local_delta(): pl.pallas_call(delta_kernel, grid=(seq // rows,), in_specs=[pl.BlockSpec(...  14.5 us
    pallas_call x3, Pallas kernels, project(): pl.pallas_call(kernel, grid_spec=pltpu.PrefetchScalarGridSpec(num_scalar_...  9.91 us
  transfers between devices with their start and end apart: 9, of which 4 were waited for; matrix products, arithmetic and copies ran while one was open for 1% of the time, Pallas kernels for 8%

profile of v4, /device:TPU:1, one launch (start us, length us, event | category | flops | bytes accessed | tf_op | source)
XLA Modules:
  0.0 375.5 jit_solution(13184599422332534091)
XLA Ops:
  0.6 0.0 copy-start.7
  0.6 1.5 collective-permute-start.1
  2.1 1.4 copy.26
  3.5 0.7 maximum_bitcast_fusion.ds_ref
  4.3 1.3 copy_bitcast_fusion.2
  5.6 14.5 %delta_local.1 = (bf16[4,1024,128]{2,1,0:T(8,128)(2,1)}, bf16[4,1024,128]{2,1,0:T(8,128)(2,1)}, bf16[4,4,160,128]{3,2,1,0:T(8,128)(2,1)S(1)}) custom-call(f32[8,8,128]{2,1,0:T(8,128)S(1)} %maximum_bitcast_fusion.ds_ref, bf16[2,1024,128]{2,1,0:T(8,128)(2,1)S(1)} %get-tuple-element.29.q_ref, bf16[2,1024,128]{2,1,0:T(8,128)(2,1)S(1)} %get-tuple-element.28.k_ref, ...), custom_call_target="tpu_custom_call" | custom-call | tf_op jit(solution)/shard_map/delta_local/pallas_call | solution.py:181
  20.1 0.0 copy-start
  20.1 20.5 %all_to_all.20.msg_ref = bf16[16,160,128]{2,1,0:T(8,128)(2,1)S(1)} all-to-all(bf16[16,160,128]{2,1,0:T(8,128)(2,1)S(1)} %bitcast.27), channel_id=1, replica_groups=mesh['ctx'=16,'exp'=8] {'ctx'}, dimensions={0} | all-to-all | bytes 1310720 | tf_op jit(solution)/shard_map/all_to_all | solution.py:514
  40.6 2.5 prefix_states.1
  43.1 3.5 all-to-all-start.1
  46.6 0.0 copy-done.7
  46.6 1.1 copy.25
  47.8 0.6 pad_add_fusion.place_ref
  48.4 5.0 %all-to-all-done.1 = bf16[16,32,128]{2,1,0:T(8,128)(2,1)S(1)} async-done(((bf16[16,32,128]{2,1,0:T(8,128)(2,1)}), bf16[16,32,128]{2,1,0:T(8,128)(2,1)S(1)}, u32[]{:S(2)}, u32[]{:S(2)}) %all-to-all-start.1) | async-done | bytes 131104 | tf_op jit(solution)/shard_map/all_to_all | solution.py:515
  53.4 0.0 copy-start.8
  53.4 0.7 copy-done.8
  54.1 5.5 %gated_rows.1 = (bf16[4,128,512]{2,1,0:T(8,128)(2,1)}, bf16[4,128,512]{2,1,0:T(8,128)(2,1)}) custom-call(s32[2]{0:T(128)} %pad_add_fusion.place_ref, bf16[4,1024,128]{2,1,0:T(8,128)(2,1)} %get-tuple-element.15.r_ref, bf16[4,1024,128]{2,1,0:T(8,128)(2,1)} %get-tuple-element.16.o_ref, bf16[4,128,128]{2,1,0:T(8,128)(2,1)} %bitcast.32, ...), custom_call_target="tpu_custom_call" | custom-call | tf_op jit(solution)/shard_map/gated_rows/pallas_call | solution.py:250
  59.6 2.3 collective-permute-start
  62.0 1.7 collective-permute-done.ahead_got_ref.behind_got_ref.own_got_ref.got_ref
  63.7 0.0 collective-permute-done.1.v_ref
  63.7 0.0 copy-done
  63.7 0.0 copy-start.1
  63.7 1.0 copy-done.1
  64.8 0.0 copy-start.6
  64.8 0.7 copy-done.6
  65.4 2.9 project_far.1
  68.3 1.3 collective-permute-start.2
  69.5 1.5 collective-permute-start.3
  71.0 3.7 project_near.1
  74.7 1.3 collective-permute-start.5
  76.1 0.0 copy-start.4
  76.1 0.0 copy-start.2
  76.1 0.0 copy-start.3
  76.1 0.2 collective-permute-start.6
  76.3 3.4 project_rest.1.rest_ref
  79.6 0.0 collective-permute-done.2.a_ref
  79.6 0.0 collective-permute-done.3.b_ref
  79.7 0.1 relay.1
  79.8 0.1 collective-permute-start.4
  79.9 2.6 collective-permute-start.7
  82.5 0.0 copy-done.4
  82.5 0.4 slots.1.slot_ref
  82.9 0.0 collective-permute-done.5.a1_ref
  82.9 1.0 collective-permute-done.6.b0_ref
  83.9 5.6 %collective-permute-done.4.a0_ref = bf16[64,2048]{1,0:T(8,128)(2,1)S(1)} collective-permute-done((bf16[64,2048]{1,0:T(8,128)(2,1)S(1)}, bf16[64,2048]{1,0:T(8,128)(2,1)S(1)}, u32[]{:S(2)}, u32[]{:S(2)}) %collective-permute-start.4) | collective-permute-done | bytes 262176 | tf_op jit(solution)/shard_map/ppermute | solution.py:502
  89.5 0.0 collective-permute-done.7.b1_ref
  89.5 0.0 copy-done.2
  89.5 0.0 copy-done.3
  89.5 4.4 %dispatch.1 = (bf16[128,2048]{1,0:T(8,128)(2,1)}, bf16[2560,16,128]{2,1,0:T(8,128)(2,1)S(1)}) custom-call(f32[256,2048]{1,0:T(8,128)S(1)} %project_rest.1.rest_ref, bf16[64,2048]{1,0:T(8,128)(2,1)S(1)} %collective-permute-done.4.a0_ref, bf16[64,2048]{1,0:T(8,128)(2,1)S(1)} %collective-permute-done.5.a1_ref, ...), custom_call_target="tpu_custom_call" | custom-call | tf_op jit(solution)/shard_map/dispatch/pallas_call | solution.py:387
  93.9 126.2 %all_to_all.21.x_ref = bf16[128,2,160,128]{3,2,1,0:T(8,128)(2,1)} all-to-all(bf16[128,2,160,128]{3,2,1,0:T(8,128)(2,1)S(1)} %bitcast.25), channel_id=1, replica_groups=mesh['ctx'=16,'exp'=8] {'ctx','exp'}, dimensions={0} | all-to-all | bytes 20971520 | tf_op jit(solution)/shard_map/all_to_all | solution.py:544
  220.1 25.0 %experts.1 = bf16[128,2,160,128]{3,2,1,0:T(8,128)(2,1)} custom-call(bf16[128,2,160,128]{3,2,1,0:T(8,128)(2,1)} %all_to_all.21.x_ref, bf16[2,2048,512]{2,1,0:T(8,128)(2,1)} %wg_ref.1, bf16[2,2048,512]{2,1,0:T(8,128)(2,1)} %wu_ref.1, bf16[2,512,2048]{2,1,0:T(8,128)(2,1)} %wd_ref.1), custom_call_target="tpu_custom_call" | custom-call | tf_op jit(solution)/shard_map/experts/pallas_call | solution.py:424
  245.1 0.0 copy-start.5
  245.1 125.4 %all_to_all.22 = bf16[128,2,160,128]{3,2,1,0:T(8,128)(2,1)S(1)} all-to-all(bf16[128,2,160,128]{3,2,1,0:T(8,128)(2,1)} %experts.1), channel_id=1, replica_groups=mesh['ctx'=16,'exp'=8] {'ctx','exp'}, dimensions={0} | all-to-all | bytes 20971520 | tf_op jit(solution)/shard_map/all_to_all | solution.py:548
  370.5 0.0 copy-done.5
  370.5 5.0 %combine.1 = bf16[128,2048]{1,0:T(8,128)(2,1)} custom-call(bf16[2560,16,128]{2,1,0:T(8,128)(2,1)S(1)} %bitcast.24, s32[10,128]{1,0:T(8,128)S(1)} %slots.1.slot_ref, f32[10,128]{1,0:T(8,128)S(1)} %bitcast.30), custom_call_target="tpu_custom_call" | custom-call | tf_op jit(solution)/shard_map/combine/pallas_call | solution.py:462
Async XLA Ops:
  0.6 46.0 %copy-start.7 = (bf16[1024,4,128]{2,1,0:T(4,128)(2,1)S(1)}, bf16[1024,4,128]{2,1,0:T(4,128)(2,1)}, u32[]{:S(2)}) copy-start(bf16[1024,4,128]{2,1,0:T(4,128)(2,1)} %param.18) | copy-start | bytes 3145732
  0.6 63.1 %collective-permute-start.1 = (bf16[512,2048]{1,0:T(8,128)(2,1)}, bf16[512,2048]{1,0:T(8,128)(2,1)}, u32[]{:S(2)}, u32[]{:S(2)}) collective-permute-start(bf16[512,2048]{1,0:T(8,128)(2,1)} %w_ref.5), channel_id=1, source_target_pairs={{0,1},{1,0},{2,3},{3,2},{4,5},{5,4},{6,7},{7,6},{8,9},{9,8},{10,11... | collective-permute-start | bytes 6291464 | tf_op jit(solution)/shard_map/ppermute | solution.py:503
  20.1 43.7 %copy-start = (bf16[512,2048]{1,0:T(8,128)(2,1)S(1)}, bf16[512,2048]{1,0:T(8,128)(2,1)}, u32[]{:S(2)}) copy-start(bf16[512,2048]{1,0:T(8,128)(2,1)} %w_ref.5) | copy-start | bytes 6291460
  43.1 10.3 %all-to-all-start.1 = ((bf16[16,32,128]{2,1,0:T(8,128)(2,1)}), bf16[16,32,128]{2,1,0:T(8,128)(2,1)S(1)}, u32[]{:S(2)}, u32[]{:S(2)}) async-start(bf16[16,32,128]{2,1,0:T(8,128)(2,1)} %prefix_states.1), calls=%async_computation.1 | async-start | bytes 262144 | tf_op jit(solution)/shard_map/all_to_all | solution.py:515
  53.4 0.7 copy-start.8
  59.6 4.1 %collective-permute-start = (bf16[4,128,512]{2,1,0:T(8,128)(2,1)}, bf16[4,128,512]{2,1,0:T(8,128)(2,1)S(1)}, u32[]{:S(2)}, u32[]{:S(2)}) collective-permute-start(bf16[4,128,512]{2,1,0:T(8,128)(2,1)} %get-tuple-element.19), channel_id=1, source_target_pairs={{0,1},{1,0},{2,3},{3,2},{4,5},{5,4},{6,7},{7,6},{8,9},{9,8},{10,11... | collective-permute-start | bytes 1572872 | tf_op jit(solution)/shard_map/ppermute | solution.py:503
  63.7 1.0 copy-start.1
  64.8 0.7 copy-start.6
  68.3 11.4 %collective-permute-start.2 = (bf16[64,2048]{1,0:T(8,128)(2,1)S(1)}, bf16[64,2048]{1,0:T(8,128)(2,1)S(1)}, u32[]{:S(2)}, u32[]{:S(2)}) collective-permute-start(bf16[64,2048]{1,0:T(8,128)(2,1)S(1)} %get-tuple-element.20), channel_id=1, source_target_pairs={{0,2},{1,3},{2,4},{3,5},{4,6},{5,7},{6,0},{7,1},{8,10},{9,11},{10,... | collective-permute-start | bytes 786440 | tf_op jit(solution)/shard_map/ppermute | solution.py:502
  69.5 10.1 %collective-permute-start.3 = (bf16[64,2048]{1,0:T(8,128)(2,1)S(1)}, bf16[64,2048]{1,0:T(8,128)(2,1)S(1)}, u32[]{:S(2)}, u32[]{:S(2)}) collective-permute-start(bf16[64,2048]{1,0:T(8,128)(2,1)S(1)} %get-tuple-element.21), channel_id=1, source_target_pairs={{0,6},{1,7},{2,0},{3,1},{4,2},{5,3},{6,4},{7,5},{8,14},{9,15},{10,... | collective-permute-start | bytes 786440 | tf_op jit(solution)/shard_map/ppermute | solution.py:502
  74.7 8.2 %collective-permute-start.5 = (bf16[64,2048]{1,0:T(8,128)(2,1)S(1)}, bf16[64,2048]{1,0:T(8,128)(2,1)S(1)}, u32[]{:S(2)}, u32[]{:S(2)}) collective-permute-start(bf16[64,2048]{1,0:T(8,128)(2,1)S(1)} %get-tuple-element.23), channel_id=1, source_target_pairs={{0,6},{1,7},{2,0},{3,1},{4,2},{5,3},{6,4},{7,5},{8,14},{9,15},{10,... | collective-permute-start | bytes 786440 | tf_op jit(solution)/shard_map/ppermute | solution.py:502
  76.1 6.5 %copy-start.4 = (s32[128,10]{0,1:T(8,128)S(1)}, s32[128,10]{0,1:T(8,128)}, u32[]{:S(2)}) copy-start(s32[128,10]{0,1:T(8,128)} %param.28) | copy-start | bytes 15364
  76.1 13.4 %copy-start.2 = (bf16[128,2048]{1,0:T(8,128)(2,1)S(1)}, bf16[128,2048]{1,0:T(8,128)(2,1)}, u32[]{:S(2)}) copy-start(bf16[128,2048]{1,0:T(8,128)(2,1)} %res_ref.1) | copy-start | bytes 1572868
  76.1 13.4 %copy-start.3 = (f32[2048]{0:T(1024)S(1)}, f32[2048]{0:T(1024)}, u32[]{:S(2)}) copy-start(f32[2048]{0:T(1024)} %param.24) | copy-start | bytes 24580
  76.1 7.8 %collective-permute-start.6 = (bf16[64,2048]{1,0:T(8,128)(2,1)S(1)}, bf16[64,2048]{1,0:T(8,128)(2,1)S(1)}, u32[]{:S(2)}, u32[]{:S(2)}) collective-permute-start(bf16[64,2048]{1,0:T(8,128)(2,1)S(1)} %get-tuple-element.24), channel_id=1, source_target_pairs={{0,2},{1,3},{2,4},{3,5},{4,6},{5,7},{6,0},{7,1},{8,10},{9,11},{10,... | collective-permute-start | bytes 786440 | tf_op jit(solution)/shard_map/ppermute | solution.py:502
  79.8 9.7 %collective-permute-start.4 = (bf16[64,2048]{1,0:T(8,128)(2,1)S(1)}, bf16[64,2048]{1,0:T(8,128)(2,1)S(1)}, u32[]{:S(2)}, u32[]{:S(2)}) collective-permute-start(bf16[64,2048]{1,0:T(8,128)(2,1)S(1)} %get-tuple-element.22), channel_id=1, source_target_pairs={{0,2},{1,3},{2,4},{3,5},{4,6},{5,7},{6,0},{7,1},{8,10},{9,11},{10,... | collective-permute-start | bytes 786440 | tf_op jit(solution)/shard_map/ppermute | solution.py:502
  79.9 9.6 %collective-permute-start.7 = (bf16[64,2048]{1,0:T(8,128)(2,1)S(1)}, bf16[64,2048]{1,0:T(8,128)(2,1)S(1)}, u32[]{:S(2)}, u32[]{:S(2)}) collective-permute-start(bf16[64,2048]{1,0:T(8,128)(2,1)S(1)} %get-tuple-element.25), channel_id=1, source_target_pairs={{0,6},{1,7},{2,0},{3,1},{4,2},{5,3},{6,4},{7,5},{8,14},{9,15},{10,... | collective-permute-start | bytes 786440 | tf_op jit(solution)/shard_map/ppermute | solution.py:502
  245.1 125.4 %copy-start.5 = (f32[128,10]{0,1:T(8,128)S(1)}, f32[128,10]{0,1:T(8,128)}, u32[]{:S(2)}) copy-start(f32[128,10]{0,1:T(8,128)} %param.29) | copy-start | bytes 15364

commit v5 on v4

--- a/solution.py
+++ b/solution.py
@@ -227,110 +227,112 @@
     )(msg)
 
 
-def gate_kernel(place_ref, r_ref, o_ref, s_ref, g_ref, gain_ref, keep_ref, give_ref):
-    d = r_ref.shape[2]
+def gate_kernel(r_ref, o_ref, s_ref, g_ref, gain_ref, keep_ref, give_ref):
+    heads, _, d = r_ref.shape
     rows = keep_ref.shape[1]
-    core = place_ref[0]
-    for part, out_ref in ((core, keep_ref), (1 - core, give_ref)):
-        span = pl.ds(pl.multiple_of(part * rows, rows), rows)
-        for h in range(r_ref.shape[0]):
-            value = o_ref[h, span, :].astype(F32) + mxu(r_ref[h, span, :], s_ref[h], ((1,), (1,)))
-            scale = 1.0 / jnp.sqrt(jnp.mean(value * value, axis=1, keepdims=True) + 1e-06)
-            gate = g_ref[h, span, :].astype(F32)
-            silu = gate * lax.logistic(gate)
-            out_ref[0, :, h * d : (h + 1) * d] = (value * scale * gain_ref[...] * silu).astype(BF16)
-
-
-def gated_rows(place, r, o, states, gate, gain, toks):
+    core = lax.axis_index("exp") & 1
+    spans = [pl.ds(pl.multiple_of(part * rows, rows), rows) for part in (core, 1 - core)]
+    each = [(span, h) for span in spans for h in range(heads)]
+    reads = [mxu(r_ref[h, span, :], s_ref[h], ((1,), (1,))) for span, h in each]
+    silus = []
+    for span, h in each:
+        gate = g_ref[h, span, :].astype(F32)
+        silus.append(gate * lax.logistic(gate) * gain_ref[...])
+    values = [o_ref[h, span, :].astype(F32) + read for (span, h), read in zip(each, reads)]
+    scales = [1.0 / jnp.sqrt(jnp.mean(value * value, axis=1, keepdims=True) + 1e-06) for value in values]
+    for n, (value, scale, silu) in enumerate(zip(values, scales, silus)):
+        out_ref, h = (keep_ref, give_ref)[n // heads], n % heads
+        out_ref[0, :, h * d : (h + 1) * d] = (value * scale * silu).astype(BF16)
+
+
+def gated_rows(r, o, states, gate, gain, toks):
     heads, seq, d = r.shape
     rows = 2 * toks
-    by_rows = pl.BlockSpec((heads, rows, d), lambda i, p: (0, i, 0))
-    out = pl.BlockSpec((1, toks, heads * d), lambda i, p: (i, 0, 0))
+    by_rows = pl.BlockSpec((heads, rows, d), lambda i: (0, i, 0))
+    out = pl.BlockSpec((1, toks, heads * d), lambda i: (i, 0, 0))
     shape = jax.ShapeDtypeStruct((seq // rows, toks, heads * d), BF16)
     return pl.pallas_call(
         gate_kernel,
-        grid_spec=pltpu.PrefetchScalarGridSpec(
-            num_scalar_prefetch=1,
-            grid=(seq // rows,),
-            in_specs=[
-                by_rows,
-                by_rows,
-                pl.BlockSpec((heads, d, d), lambda i, p: (0, 0, 0)),
-                by_rows,
-                pl.BlockSpec((1, d), lambda i, p: (0, 0)),
-            ],
-            out_specs=[out, out],
-        ),
+        grid=(seq // rows,),
+        in_specs=[
+            by_rows,
+            by_rows,
+            pl.BlockSpec((heads, d, d), lambda i: (0, 0, 0)),
+            by_rows,
+            pl.BlockSpec((1, d), lambda i: (0, 0)),
+        ],
+        out_specs=[out, out],
         out_shape=[shape, shape],
         compiler_params=pltpu.CompilerParams(dimension_semantics=("arbitrary",), vmem_limit_bytes=56 * MIB),
         name="gated_rows",
-    )(place, r, o, states, gate, gain)
-
-
-def far_kernel(place_ref, mine_ref, got_ref, w_ref, v_ref, a_ref, b_ref):
-    part = mxu(mine_ref[0], w_ref[...]) + mxu(got_ref[0], v_ref[...])
-    half = a_ref.shape[0]
+    )(r, o, states, gate, gain)
+
+
+def chunk_at(step, mine_ref, got_ref):
+    place = lax.rem((lax.axis_index("exp") >> 1) + step, mine_ref.shape[0])
+    return jnp.concatenate([mine_ref[place], got_ref[place]], axis=1)
+
+
+def far_kernel(mine_ref, got_ref, w_ref, v_ref, a_ref, b_ref):
+    rows = chunk_at(2, mine_ref, got_ref)
+    deep, half = w_ref.shape[0], a_ref.shape[0]
+    part = mxu(rows[:, :deep], w_ref[...]) + mxu(rows[:, deep:], v_ref[...])
     a_ref[...] = part[:half].astype(BF16)
     b_ref[...] = part[half:].astype(BF16)
 
 
-def near_kernel(place_ref, ahead_ref, ahead_got_ref, behind_ref, behind_got_ref, w_ref, v_ref, right_ref, left_ref):
+def near_kernel(mine_ref, got_ref, w_ref, v_ref, right_ref, left_ref, held_ref):
     half = right_ref.shape[0]
-    for row_ref, got_ref, first, out_ref in (
-        (ahead_ref, ahead_got_ref, half, right_ref),
-        (behind_ref, behind_got_ref, 0, left_ref),
-    ):
-        rows = pl.ds(first, half)
-        out_ref[...] = (mxu(row_ref[0, rows, :], w_ref[...]) + mxu(got_ref[0, rows, :], v_ref[...])).astype(BF16)
-
-
-def rest_kernel(
-    place_ref, ahead_ref, ahead_got_ref, behind_ref, behind_got_ref, own_ref, own_got_ref, w_ref, v_ref, out_ref
-):
-    half = own_ref.shape[1] // 2
-    rows = jnp.concatenate([ahead_ref[0, :half, :], behind_ref[0, half:, :], own_ref[0]], axis=0)
-    got = jnp.concatenate([ahead_got_ref[0, :half, :], behind_got_ref[0, half:, :], own_got_ref[0]], axis=0)
-    out_ref[...] = mxu(rows, w_ref[...]) + mxu(got, v_ref[...])
-
-
-def project(kernel, steps, out_shape, name, place, mine, got, weight, other):
+    deep = w_ref.shape[0]
+    rows = jnp.concatenate(
+        [chunk_at(1, mine_ref, got_ref), chunk_at(mine_ref.shape[0] - 1, mine_ref, got_ref)], axis=0
+    )
+    part = mxu(rows[:, :deep], w_ref[...]) + mxu(rows[:, deep:], v_ref[...])
+    held_ref[:half] = part[:half]
+    right_ref[...] = part[half : 2 * half].astype(BF16)
+    left_ref[...] = part[2 * half : 3 * half].astype(BF16)
+    held_ref[half:] = part[3 * half :]
+
+
+def own_kernel(mine_ref, got_ref, w_ref, v_ref, out_ref):
+    rows = chunk_at(0, mine_ref, got_ref)
+    deep = w_ref.shape[0]
+    out_ref[...] = mxu(rows[:, :deep], w_ref[...]) + mxu(rows[:, deep:], v_ref[...])
+
+
+def project(kernel, chunks, out_shape, name, mine, got, weight, other):
     count, toks, deep = mine.shape
     width = weight.shape[1]
-    chunk = lambda step: pl.BlockSpec((1, toks, deep), lambda i, p: (lax.rem(p[1] + step, count), 0, 0))
-    whole = lambda shape: pl.BlockSpec(shape, lambda i, p: (0, 0))
+    whole = pl.BlockSpec(memory_space=VMEM)
     return pl.pallas_call(
         kernel,
-        grid_spec=pltpu.PrefetchScalarGridSpec(
-            num_scalar_prefetch=1,
-            grid=(1,),
-            in_specs=[chunk(step) for step in steps for _ in range(2)] + [whole(weight.shape)] * 2,
-            out_specs=[whole(shape.shape) for shape in out_shape],
-        ),
+        in_specs=[whole] * 4,
+        out_specs=[whole] * len(out_shape),
         out_shape=out_shape,
         cost_estimate=pl.CostEstimate(
-            flops=4 * len(steps) * toks * deep * width,
-            bytes_accessed=4 * weight.size + 4 * len(steps) * toks * width,
+            flops=4 * chunks * toks * deep * width,
+            bytes_accessed=4 * weight.size + 4 * chunks * toks * width,
             transcendentals=0,
         ),
-        compiler_params=pltpu.CompilerParams(dimension_semantics=("arbitrary",), vmem_limit_bytes=24 * MIB),
+        compiler_params=pltpu.CompilerParams(vmem_limit_bytes=24 * MIB),
         name=name,
-    )(place, *([mine, got] * len(steps)), weight, other)
-
-
-def relay_kernel(rest_ref, a_ref, b_ref, right_ref, left_ref):
+    )(mine, got, weight, other)
+
+
+def relay_kernel(held_ref, a_ref, b_ref, right_ref, left_ref):
     half = a_ref.shape[0]
-    right_ref[...] = (rest_ref[:half] + a_ref[...].astype(F32)).astype(BF16)
-    left_ref[...] = (rest_ref[half : 2 * half] + b_ref[...].astype(F32)).astype(BF16)
-
-
-def relay(rest, first, second):
+    right_ref[...] = (held_ref[:half] + a_ref[...].astype(F32)).astype(BF16)
+    left_ref[...] = (held_ref[half:] + b_ref[...].astype(F32)).astype(BF16)
+
+
+def relay(held, first, second):
     shape = jax.ShapeDtypeStruct(first.shape, BF16)
     return pl.pallas_call(
         relay_kernel,
         out_shape=[shape, shape],
         compiler_params=pltpu.CompilerParams(vmem_limit_bytes=16 * MIB),
         name="relay",
-    )(rest, first, second)
+    )(held, first, second)
 
 
 def slot_kernel(experts, ids_ref, out_ref):
@@ -358,10 +360,10 @@
     )(ids)
 
 
-def dispatch_kernel(rest_ref, a0_ref, a1_ref, b0_ref, b1_ref, res_ref, gain_ref, slot_ref, att_ref, send_ref, flat_ref):
+def dispatch_kernel(own_ref, a0_ref, a1_ref, b0_ref, b1_ref, res_ref, gain_ref, slot_ref, att_ref, send_ref, flat_ref):
     toks, width = res_ref.shape
     pieces = width // 128
-    own = rest_ref[toks:]
+    own = own_ref[...]
     early = own[: toks // 2] + a0_ref[...].astype(F32) + a1_ref[...].astype(F32)
     late = own[toks // 2 :] + b0_ref[...].astype(F32) + b1_ref[...].astype(F32)
     total = jnp.concatenate([early, late], axis=0)
@@ -371,16 +373,16 @@
     root = jnp.sqrt(jnp.mean(settled * settled, axis=1, keepdims=True) + 1e-06)
     normed = settled / root * gain_ref[...]
     for j in range(pieces):
-        flat_ref[pl.ds(j, toks, stride=pieces), :] = normed[:, j * 128 : (j + 1) * 128]
-
-    @pl.loop(0, toks)
+        flat_ref[pl.ds(j, toks, stride=PITCH), :] = normed[:, j * 128 : (j + 1) * 128]
+
+    @pl.loop(0, toks, unroll=4)
     def _(t):
-        tile = flat_ref[pl.ds(pl.multiple_of(t * pieces, pieces), pieces), :].astype(BF16)
+        tile = flat_ref[pl.ds(pl.multiple_of(t * PITCH, 8), pieces), :].astype(BF16)
         for k in range(slot_ref.shape[0]):
             send_ref[slot_ref[k, t]] = tile
 
 
-def dispatch(rest, early, late, residual, gain, slots, count):
+def dispatch(own, early, late, residual, gain, slots, count):
     toks, width = residual.shape
     pieces = width // 128
     whole = pl.BlockSpec(memory_space=VMEM)
@@ -392,10 +394,10 @@
             jax.ShapeDtypeStruct((toks, width), BF16),
             jax.ShapeDtypeStruct((count, pieces, 128), BF16),
         ],
-        scratch_shapes=[VMEM((toks * pieces, 128), F32)],
+        scratch_shapes=[VMEM((toks * PITCH, 128), F32)],
         compiler_params=pltpu.CompilerParams(vmem_limit_bytes=24 * MIB),
         name="dispatch",
-    )(rest, *early, *late, residual, gain, slots)
+    )(own, *early, *late, residual, gain, slots)
 
 
 def expert_kernel(x_ref, wg_ref, wu_ref, wd_ref, out_ref, flat_ref):
@@ -444,15 +446,15 @@
     toks, width = out_ref.shape
     pieces = width // 128
 
-    @pl.loop(0, toks)
+    @pl.loop(0, toks, unroll=4)
     def _(t):
         total = jnp.zeros((pieces, 128), F32)
         for k in range(slot_ref.shape[0]):
             total = total + gate_ref[k, t] * back_ref[slot_ref[k, t]].astype(F32)
-        flat_ref[pl.ds(pl.multiple_of(t * pieces, pieces), pieces), :] = total
+        flat_ref[pl.ds(pl.multiple_of(t * PITCH, 8), pieces), :] = total
 
     for j in range(pieces):
-        out_ref[:, j * 128 : (j + 1) * 128] = flat_ref[pl.ds(j, toks, stride=pieces), :].astype(BF16)
+        out_ref[:, j * 128 : (j + 1) * 128] = flat_ref[pl.ds(j, toks, stride=PITCH), :].astype(BF16)
 
 
 def combine(back, slots, gates):
@@ -464,7 +466,7 @@
         in_specs=[pl.BlockSpec(memory_space=VMEM), smem, smem],
         out_specs=pl.BlockSpec(memory_space=VMEM),
         out_shape=jax.ShapeDtypeStruct((toks, pieces * lanes), BF16),
-        scratch_shapes=[VMEM((toks * pieces, lanes), F32)],
+        scratch_shapes=[VMEM((toks * PITCH, lanes), F32)],
         compiler_params=pltpu.CompilerParams(vmem_limit_bytes=24 * MIB),
         name="combine",
     )(back, slots, gates)
@@ -497,8 +499,6 @@
     local_experts = gate_proj.shape[0]
     toks, width = residual.shape
 
-    place = lax.axis_index("exp")
-    place = jnp.stack([place & 1, place >> 1])
     shift = lambda a, by: lax.ppermute(a, "exp", [(i, (i + 2 * by) % n_exp) for i in range(n_exp)])
     swap = lambda a: lax.ppermute(a, "exp", [(i, i ^ 1) for i in range(n_exp)])
     other_weight = swap(out_weight)
@@ -514,25 +514,20 @@
     msg = lax.all_to_all(msg.reshape(n_ctx, dk + wide, dk), "ctx", 0, 0, tiled=True)
     states = lax.all_to_all(prefix_states(msg, wide), "ctx", 0, 0, tiled=True).reshape(heads, dv, dk)
     mine, give = gated_rows(
-        place, reads, local_out, states, by_head(out_gate), head_gain.reshape(1, dv), toks
+        reads, local_out, states, by_head(out_gate), head_gain.reshape(1, dv), toks
     )
     got = swap(give)
     half = jax.ShapeDtypeStruct((toks // 2, width), BF16)
-    operands = (place, mine, got, out_weight, other_weight)
-    first, second = project(far_kernel, (2,), [half, half], "project_far", *operands)
+    operands = (mine, got, out_weight, other_weight)
+    first, second = project(far_kernel, 1, [half, half], "project_far", *operands)
     first, second = shift(first, 1), shift(second, -1)
-    ahead, behind = project(near_kernel, (1, n_exp // 2 - 1), [half, half], "project_near", *operands)
+    total = jax.ShapeDtypeStruct((toks, width), F32)
+    ahead, behind, held = project(near_kernel, 2, [half, half, total], "project_near", *operands)
     ahead, behind = shift(ahead, 1), shift(behind, -1)
-    [rest] = project(
-        rest_kernel,
-        (1, n_exp // 2 - 1, 0),
-        [jax.ShapeDtypeStruct((2 * toks, width), F32)],
-        "project_rest",
-        *operands,
-    )
-    right, left = relay(rest, first, second)
+    right, left = relay(held, first, second)
+    [own] = project(own_kernel, 1, [total], "project_own", *operands)
     attended, send = dispatch(
-        rest,
+        own,
         (shift(right, 1), behind),
         (ahead, shift(left, -1)),
         residual,

time: 376 us -> 373 us (level)
  Pallas kernels: 67.3 us -> 63.1 us
  transfers between devices with their start and end apart: 9 -> 9, of which waited for: 4 -> 5; matrix products, arithmetic and copies ran while one was open for 1% -> 1% of each run, Pallas kernels for 8% -> 7%
where the time goes in v5:
time: 373 us; the launch traced here: 372 us
  blocking collectives  272 us (73%)
  Pallas kernels  63.1 us (17%)
  waiting for transfers between devices  15.1 us (4%)
  starting transfers between devices  14.4 us (4%)
  local copies, waits for them, and re-layouts  5.57 us (1%)
    all_to_all x1, blocking collectives, shards(): lax.all_to_all(send.reshape(n_dev, local_experts, tall, 128), ('ctx', 'ex...  126 us
    all_to_all x1, blocking collectives, shards(): back = lax.all_to_all(done, ('ctx', 'exp'), 0, 0, tiled=True)  125 us
    pallas_call x1, Pallas kernels, run_experts(): pl.pallas_call(expert_kernel, grid=(local, count // sources), in_specs=[t...  25 us
    all_to_all x1, blocking collectives, shards(): lax.all_to_all(msg.reshape(n_ctx, dk + wide, dk), 'ctx', 0, 0, tiled=True)  20.5 us
    pallas_call x1, Pallas kernels, local_delta(): pl.pallas_call(delta_kernel, grid=(seq // rows,), in_specs=[pl.BlockSpec(...  14.4 us
    ppermute x6, waiting for transfers between devices, shards(): lax.ppermute(a, 'exp', [(i, (i + 2 * by) % n_exp) for i in range(n_exp)])  7.7 us
  transfers between devices with their start and end apart: 9, of which 5 were waited for; matrix products, arithmetic and copies ran while one was open for 1% of the time, Pallas kernels for 7%

profile of v5, /device:TPU:1, one launch (start us, length us, event | category | flops | bytes accessed | tf_op | source)
XLA Modules:
  0.0 371.9 jit_solution(15206936108839572031)
XLA Ops:
  0.6 0.0 copy-start.6
  0.6 1.5 collective-permute-start.1
  2.1 1.4 copy.26
  3.5 0.7 maximum_bitcast_fusion.ds_ref
  4.3 1.3 copy_bitcast_fusion.2
  5.6 14.4 %delta_local.1 = (bf16[4,1024,128]{2,1,0:T(8,128)(2,1)}, bf16[4,1024,128]{2,1,0:T(8,128)(2,1)}, bf16[4,4,160,128]{3,2,1,0:T(8,128)(2,1)S(1)}) custom-call(f32[8,8,128]{2,1,0:T(8,128)S(1)} %maximum_bitcast_fusion.ds_ref, bf16[2,1024,128]{2,1,0:T(8,128)(2,1)S(1)} %get-tuple-element.31.q_ref, bf16[2,1024,128]{2,1,0:T(8,128)(2,1)S(1)} %get-tuple-element.30.k_ref, ...), custom_call_target="tpu_custom_call" | custom-call | tf_op jit(solution)/shard_map/delta_local/pallas_call | solution.py:181
  20.0 0.0 copy-start
  20.0 20.5 %all_to_all.20.msg_ref = bf16[16,160,128]{2,1,0:T(8,128)(2,1)S(1)} all-to-all(bf16[16,160,128]{2,1,0:T(8,128)(2,1)S(1)} %bitcast.25), channel_id=1, replica_groups=mesh['ctx'=16,'exp'=8] {'ctx'}, dimensions={0} | all-to-all | bytes 1310720 | tf_op jit(solution)/shard_map/all_to_all | solution.py:514
  40.5 2.5 prefix_states.1
  43.1 3.5 all-to-all-start.1
  46.6 0.0 copy-done.6
  46.6 1.1 copy.25
  47.8 5.6 %all-to-all-done.1 = bf16[16,32,128]{2,1,0:T(8,128)(2,1)S(1)} async-done(((bf16[16,32,128]{2,1,0:T(8,128)(2,1)}), bf16[16,32,128]{2,1,0:T(8,128)(2,1)S(1)}, u32[]{:S(2)}, u32[]{:S(2)}) %all-to-all-start.1) | async-done | bytes 131104 | tf_op jit(solution)/shard_map/all_to_all | solution.py:515
  53.4 0.0 copy-start.7
  53.4 0.7 copy-done.7
  54.1 4.8 %gated_rows.1 = (bf16[4,128,512]{2,1,0:T(8,128)(2,1)}, bf16[4,128,512]{2,1,0:T(8,128)(2,1)}) custom-call(bf16[4,1024,128]{2,1,0:T(8,128)(2,1)} %get-tuple-element.16.r_ref, bf16[4,1024,128]{2,1,0:T(8,128)(2,1)} %get-tuple-element.17.o_ref, bf16[4,128,128]{2,1,0:T(8,128)(2,1)} %bitcast.30, bf16[4,1024,128]{2,1,0:T(8,128)(2,1)} %bitcast.29, f32[1,128]{1,0:T(1,128)} %bitcast.31), custom_call_target="tpu_custom_call" | custom-call | tf_op jit(solution)/shard_map/gated_rows/pallas_call | solution.py:254
  58.9 2.3 collective-permute-start
  61.2 1.7 collective-permute-done.got_ref
  63.0 0.0 collective-permute-done.1.v_ref
  63.0 0.0 copy-done
  63.0 0.0 copy-start.1
  63.0 1.0 copy-done.1
  64.0 2.3 project_far.1
  66.4 0.0 copy-start.4
  66.4 1.3 collective-permute-start.2
  67.7 1.5 collective-permute-start.3
  69.1 2.8 project_near.1
  72.0 0.0 copy-start.2
  72.0 0.0 copy-start.3
  72.0 1.3 collective-permute-start.5
  73.3 0.2 collective-permute-start.6
  73.5 1.7 collective-permute-done.2.a_ref
  75.2 0.0 collective-permute-done.3.b_ref
  75.2 0.1 relay.1
  75.3 1.0 collective-permute-start.4
  76.2 1.8 collective-permute-start.7
  78.0 0.0 copy-done.4
  78.0 0.4 slots.1.slot_ref
  78.4 2.3 project_own.1.own_ref
  80.7 0.0 collective-permute-done.5.a1_ref
  80.7 0.4 collective-permute-done.6.b0_ref
  81.1 5.6 %collective-permute-done.4.a0_ref = bf16[64,2048]{1,0:T(8,128)(2,1)S(1)} collective-permute-done((bf16[64,2048]{1,0:T(8,128)(2,1)S(1)}, bf16[64,2048]{1,0:T(8,128)(2,1)S(1)}, u32[]{:S(2)}, u32[]{:S(2)}) %collective-permute-start.4) | collective-permute-done | bytes 262176 | tf_op jit(solution)/shard_map/ppermute | solution.py:502
  86.7 0.0 collective-permute-done.7.b1_ref
  86.7 0.0 copy-done.2
  86.7 0.0 copy-done.3
  86.7 4.3 %dispatch.1 = (bf16[128,2048]{1,0:T(8,128)(2,1)}, bf16[2560,16,128]{2,1,0:T(8,128)(2,1)S(1)}) custom-call(f32[128,2048]{1,0:T(8,128)S(1)} %project_own.1.own_ref, bf16[64,2048]{1,0:T(8,128)(2,1)S(1)} %collective-permute-done.4.a0_ref, bf16[64,2048]{1,0:T(8,128)(2,1)S(1)} %collective-permute-done.5.a1_ref, ...), custom_call_target="tpu_custom_call" | custom-call | tf_op jit(solution)/shard_map/dispatch/pallas_call | solution.py:389
  91.0 126.3 %all_to_all.21.x_ref = bf16[128,2,160,128]{3,2,1,0:T(8,128)(2,1)} all-to-all(bf16[128,2,160,128]{3,2,1,0:T(8,128)(2,1)S(1)} %bitcast.23), channel_id=1, replica_groups=mesh['ctx'=16,'exp'=8] {'ctx','exp'}, dimensions={0} | all-to-all | bytes 20971520 | tf_op jit(solution)/shard_map/all_to_all | solution.py:539
  217.3 25.0 %experts.1 = bf16[128,2,160,128]{3,2,1,0:T(8,128)(2,1)} custom-call(bf16[128,2,160,128]{3,2,1,0:T(8,128)(2,1)} %all_to_all.21.x_ref, bf16[2,2048,512]{2,1,0:T(8,128)(2,1)} %wg_ref.1, bf16[2,2048,512]{2,1,0:T(8,128)(2,1)} %wu_ref.1, bf16[2,512,2048]{2,1,0:T(8,128)(2,1)} %wd_ref.1), custom_call_target="tpu_custom_call" | custom-call | tf_op jit(solution)/shard_map/experts/pallas_call | solution.py:426
  242.3 0.0 copy-start.5
  242.3 125.5 %all_to_all.22 = bf16[128,2,160,128]{3,2,1,0:T(8,128)(2,1)S(1)} all-to-all(bf16[128,2,160,128]{3,2,1,0:T(8,128)(2,1)} %experts.1), channel_id=1, replica_groups=mesh['ctx'=16,'exp'=8] {'ctx','exp'}, dimensions={0} | all-to-all | bytes 20971520 | tf_op jit(solution)/shard_map/all_to_all | solution.py:543
  367.8 0.0 copy-done.5
  367.8 4.1 %combine.1 = bf16[128,2048]{1,0:T(8,128)(2,1)} custom-call(bf16[2560,16,128]{2,1,0:T(8,128)(2,1)S(1)} %bitcast.22, s32[10,128]{1,0:T(8,128)S(1)} %slots.1.slot_ref, f32[10,128]{1,0:T(8,128)S(1)} %bitcast.28), custom_call_target="tpu_custom_call" | custom-call | tf_op jit(solution)/shard_map/combine/pallas_call | solution.py:464
Async XLA Ops:
  0.6 46.0 %copy-start.6 = (bf16[1024,4,128]{2,1,0:T(4,128)(2,1)S(1)}, bf16[1024,4,128]{2,1,0:T(4,128)(2,1)}, u32[]{:S(2)}) copy-start(bf16[1024,4,128]{2,1,0:T(4,128)(2,1)} %param.18) | copy-start | bytes 3145732
  0.6 62.4 %collective-permute-start.1 = (bf16[512,2048]{1,0:T(8,128)(2,1)}, bf16[512,2048]{1,0:T(8,128)(2,1)}, u32[]{:S(2)}, u32[]{:S(2)}) collective-permute-start(bf16[512,2048]{1,0:T(8,128)(2,1)} %w_ref.5), channel_id=1, source_target_pairs={{0,1},{1,0},{2,3},{3,2},{4,5},{5,4},{6,7},{7,6},{8,9},{9,8},{10,11... | collective-permute-start | bytes 6291464 | tf_op jit(solution)/shard_map/ppermute | solution.py:503
  20.0 43.0 %copy-start = (bf16[512,2048]{1,0:T(8,128)(2,1)S(1)}, bf16[512,2048]{1,0:T(8,128)(2,1)}, u32[]{:S(2)}) copy-start(bf16[512,2048]{1,0:T(8,128)(2,1)} %w_ref.5) | copy-start | bytes 6291460
  43.1 10.3 %all-to-all-start.1 = ((bf16[16,32,128]{2,1,0:T(8,128)(2,1)}), bf16[16,32,128]{2,1,0:T(8,128)(2,1)S(1)}, u32[]{:S(2)}, u32[]{:S(2)}) async-start(bf16[16,32,128]{2,1,0:T(8,128)(2,1)} %prefix_states.1), calls=%async_computation.1 | async-start | bytes 262144 | tf_op jit(solution)/shard_map/all_to_all | solution.py:515
  53.4 0.7 copy-start.7
  58.9 4.1 %collective-permute-start = (bf16[4,128,512]{2,1,0:T(8,128)(2,1)}, bf16[4,128,512]{2,1,0:T(8,128)(2,1)S(1)}, u32[]{:S(2)}, u32[]{:S(2)}) collective-permute-start(bf16[4,128,512]{2,1,0:T(8,128)(2,1)} %get-tuple-element.20), channel_id=1, source_target_pairs={{0,1},{1,0},{2,3},{3,2},{4,5},{5,4},{6,7},{7,6},{8,9},{9,8},{10,11... | collective-permute-start | bytes 1572872 | tf_op jit(solution)/shard_map/ppermute | solution.py:503
  63.0 1.0 copy-start.1
  66.4 11.7 %copy-start.4 = (s32[128,10]{0,1:T(8,128)S(1)}, s32[128,10]{0,1:T(8,128)}, u32[]{:S(2)}) copy-start(s32[128,10]{0,1:T(8,128)} %param.28) | copy-start | bytes 15364
  66.4 8.8 %collective-permute-start.2 = (bf16[64,2048]{1,0:T(8,128)(2,1)S(1)}, bf16[64,2048]{1,0:T(8,128)(2,1)S(1)}, u32[]{:S(2)}, u32[]{:S(2)}) collective-permute-start(bf16[64,2048]{1,0:T(8,128)(2,1)S(1)} %get-tuple-element.22), channel_id=1, source_target_pairs={{0,2},{1,3},{2,4},{3,5},{4,6},{5,7},{6,0},{7,1},{8,10},{9,11},{10,... | collective-permute-start | bytes 786440 | tf_op jit(solution)/shard_map/ppermute | solution.py:502
  67.7 7.5 %collective-permute-start.3 = (bf16[64,2048]{1,0:T(8,128)(2,1)S(1)}, bf16[64,2048]{1,0:T(8,128)(2,1)S(1)}, u32[]{:S(2)}, u32[]{:S(2)}) collective-permute-start(bf16[64,2048]{1,0:T(8,128)(2,1)S(1)} %get-tuple-element.23), channel_id=1, source_target_pairs={{0,6},{1,7},{2,0},{3,1},{4,2},{5,3},{6,4},{7,5},{8,14},{9,15},{10,... | collective-permute-start | bytes 786440 | tf_op jit(solution)/shard_map/ppermute | solution.py:502
  72.0 14.8 %copy-start.2 = (bf16[128,2048]{1,0:T(8,128)(2,1)S(1)}, bf16[128,2048]{1,0:T(8,128)(2,1)}, u32[]{:S(2)}) copy-start(bf16[128,2048]{1,0:T(8,128)(2,1)} %res_ref.1) | copy-start | bytes 1572868
  72.0 14.8 %copy-start.3 = (f32[2048]{0:T(1024)S(1)}, f32[2048]{0:T(1024)}, u32[]{:S(2)}) copy-start(f32[2048]{0:T(1024)} %param.24) | copy-start | bytes 24580
  72.0 8.7 %collective-permute-start.5 = (bf16[64,2048]{1,0:T(8,128)(2,1)S(1)}, bf16[64,2048]{1,0:T(8,128)(2,1)S(1)}, u32[]{:S(2)}, u32[]{:S(2)}) collective-permute-start(bf16[64,2048]{1,0:T(8,128)(2,1)S(1)} %get-tuple-element.25), channel_id=1, source_target_pairs={{0,6},{1,7},{2,0},{3,1},{4,2},{5,3},{6,4},{7,5},{8,14},{9,15},{10,... | collective-permute-start | bytes 786440 | tf_op jit(solution)/shard_map/ppermute | solution.py:502
  73.3 7.8 %collective-permute-start.6 = (bf16[64,2048]{1,0:T(8,128)(2,1)S(1)}, bf16[64,2048]{1,0:T(8,128)(2,1)S(1)}, u32[]{:S(2)}, u32[]{:S(2)}) collective-permute-start(bf16[64,2048]{1,0:T(8,128)(2,1)S(1)} %get-tuple-element.26), channel_id=1, source_target_pairs={{0,2},{1,3},{2,4},{3,5},{4,6},{5,7},{6,0},{7,1},{8,10},{9,11},{10,... | collective-permute-start | bytes 786440 | tf_op jit(solution)/shard_map/ppermute | solution.py:502
  75.3 11.5 %collective-permute-start.4 = (bf16[64,2048]{1,0:T(8,128)(2,1)S(1)}, bf16[64,2048]{1,0:T(8,128)(2,1)S(1)}, u32[]{:S(2)}, u32[]{:S(2)}) collective-permute-start(bf16[64,2048]{1,0:T(8,128)(2,1)S(1)} %get-tuple-element.24), channel_id=1, source_target_pairs={{0,2},{1,3},{2,4},{3,5},{4,6},{5,7},{6,0},{7,1},{8,10},{9,11},{10,... | collective-permute-start | bytes 786440 | tf_op jit(solution)/shard_map/ppermute | solution.py:502
  76.2 10.5 %collective-permute-start.7 = (bf16[64,2048]{1,0:T(8,128)(2,1)S(1)}, bf16[64,2048]{1,0:T(8,128)(2,1)S(1)}, u32[]{:S(2)}, u32[]{:S(2)}) collective-permute-start(bf16[64,2048]{1,0:T(8,128)(2,1)S(1)} %get-tuple-element.27), channel_id=1, source_target_pairs={{0,6},{1,7},{2,0},{3,1},{4,2},{5,3},{6,4},{7,5},{8,14},{9,15},{10,... | collective-permute-start | bytes 786440 | tf_op jit(solution)/shard_map/ppermute | solution.py:502
  242.3 125.5 %copy-start.5 = (f32[128,10]{0,1:T(8,128)S(1)}, f32[128,10]{0,1:T(8,128)}, u32[]{:S(2)}) copy-start(f32[128,10]{0,1:T(8,128)} %param.29) | copy-start | bytes 15364

commit v6 on v5

--- a/solution.py
+++ b/solution.py
@@ -60,7 +60,7 @@
     return inverses
 
 
-def delta_kernel(ds_ref, q_ref, k_ref, v_ref, r_ref, o_ref, msg_ref, state_ref):
+def delta_kernel(decay_ref, beta_ref, q_ref, k_ref, v_ref, r_ref, o_ref, msg_ref, state_ref):
     step = pl.program_id(0)
     heads = v_ref.shape[0]
     group = heads // q_ref.shape[0]
@@ -81,7 +81,7 @@
     upto = (row <= col).astype(BF16)
     rows_of, columns_of = [], []
     for n in range(per_step):
-        ds = ds_ref[n]
+        ds = jnp.concatenate([a[:, n * c : (n + 1) * c] for a in (decay_ref, beta_ref)], axis=0)
         d0 = ds.astype(BF16)
         rest = ds - d0.astype(F32)
         d1 = rest.astype(BF16)
@@ -173,7 +173,7 @@
                 msg_ref[h, p, d:, :] = added[p * wide : (p + 1) * wide]
 
 
-def local_delta(ds, q, k, v, parts):
+def local_delta(decay, beta, q, k, v, parts):
     heads, seq, dv = v.shape
     kh, _, dk = q.shape
     wide = dv // parts
@@ -182,7 +182,8 @@
         delta_kernel,
         grid=(seq // rows,),
         in_specs=[
-            pl.BlockSpec((PER_STEP, 2 * heads, CHUNK), lambda i: (i, 0, 0)),
+            pl.BlockSpec((heads, rows), lambda i: (0, i)),
+            pl.BlockSpec((heads, rows), lambda i: (0, i)),
             pl.BlockSpec((kh, rows, dk), lambda i: (0, i, 0)),
             pl.BlockSpec((kh, rows, dk), lambda i: (0, i, 0)),
             pl.BlockSpec((heads, rows, dv), lambda i: (0, i, 0)),
@@ -202,7 +203,7 @@
             dimension_semantics=("arbitrary",), vmem_limit_bytes=30 * MIB
         ),
         name="delta_local",
-    )(ds, q, k, v)
+    )(decay, beta, q, k, v)
 
 
 def prefix_kernel(msg_ref, out_ref):
@@ -263,7 +264,7 @@
         ],
         out_specs=[out, out],
         out_shape=[shape, shape],
-        compiler_params=pltpu.CompilerParams(dimension_semantics=("arbitrary",), vmem_limit_bytes=56 * MIB),
+        compiler_params=pltpu.CompilerParams(dimension_semantics=("arbitrary",), vmem_limit_bytes=44 * MIB),
         name="gated_rows",
     )(r, o, states, gate, gain)
 
@@ -409,10 +410,11 @@
     x = jnp.concatenate(
         [flat_ref[pl.ds(j, rows, stride=PITCH), :].astype(BF16) for j in range(pieces)], axis=1
     )
-    gate = mxu(x, wg_ref[0])
-    up = mxu(x, wu_ref[0])
+    e = pl.program_id(0)
+    gate = mxu(x, wg_ref[e])
+    up = mxu(x, wu_ref[e])
     inner = (gate * lax.logistic(gate) * up).astype(BF16)
-    y = mxu(inner, wd_ref[0])
+    y = mxu(inner, wd_ref[e])
     for j in range(pieces):
         flat_ref[pl.ds(j, rows, stride=PITCH), :] = y[:, j * lanes : (j + 1) * lanes]
     out_ref[...] = tiles_ref[:, :pieces, :].astype(BF16).reshape(sources, 1, tall, lanes)
@@ -428,15 +430,15 @@
         grid=(local, count // sources),
         in_specs=[
             tokens,
-            pl.BlockSpec((1,) + gate_proj.shape[1:], lambda e, i: (e, 0, 0)),
-            pl.BlockSpec((1,) + up_proj.shape[1:], lambda e, i: (e, 0, 0)),
-            pl.BlockSpec((1,) + down_proj.shape[1:], lambda e, i: (e, 0, 0)),
+            pl.BlockSpec(memory_space=VMEM),
+            pl.BlockSpec(memory_space=VMEM),
+            pl.BlockSpec(memory_space=VMEM),
         ],
         out_specs=tokens,
         out_shape=jax.ShapeDtypeStruct(x.shape, BF16),
         scratch_shapes=[VMEM((rows * PITCH, lanes), F32)],
         compiler_params=pltpu.CompilerParams(
-            dimension_semantics=("arbitrary", "arbitrary"), vmem_limit_bytes=56 * MIB
+            dimension_semantics=("arbitrary", "arbitrary"), vmem_limit_bytes=36 * MIB
         ),
         name="experts",
     )(x, gate_proj, up_proj, down_proj)
@@ -506,11 +508,8 @@
     gates = route_gates.T
 
     by_head = lambda a: jnp.transpose(a, (1, 0, 2))
-    ds = jnp.transpose(
-        jnp.concatenate([decay_logarithm, write_strength], axis=0).reshape(2 * heads, seq // CHUNK, CHUNK),
-        (1, 0, 2),
-    )
-    reads, local_out, msg = local_delta(ds, by_head(queries), by_head(key_vectors), by_head(values), parts)
+    reads, local_out, msg = local_delta(
+        decay_logarithm, write_strength, by_head(queries), by_head(key_vectors), by_head(values), parts)
     msg = lax.all_to_all(msg.reshape(n_ctx, dk + wide, dk), "ctx", 0, 0, tiled=True)
     states = lax.all_to_all(prefix_states(msg, wide), "ctx", 0, 0, tiled=True).reshape(heads, dv, dk)
     mine, give = gated_rows(

time: 373 us -> 369 us (0.989)
  Pallas kernels: 63.1 us -> 59.2 us
where the time goes in v6:
time: 369 us; the launch traced here: 368 us
  blocking collectives  272 us (74%)
  Pallas kernels  59.2 us (16%)
  waiting for transfers between devices  14.7 us (4%)
  starting transfers between devices  14.3 us (4%)
  local copies, waits for them, and re-layouts  6.57 us (2%)
    all_to_all x1, blocking collectives, shards(): lax.all_to_all(send.reshape(n_dev, local_experts, tall, 128), ('ctx', 'ex...  126 us
    all_to_all x1, blocking collectives, shards(): back = lax.all_to_all(done, ('ctx', 'exp'), 0, 0, tiled=True)  125 us
    pallas_call x1, Pallas kernels, run_experts(): pl.pallas_call(expert_kernel, grid=(local, count // sources), in_specs=[t...  23.2 us
    all_to_all x1, blocking collectives, shards(): lax.all_to_all(msg.reshape(n_ctx, dk + wide, dk), 'ctx', 0, 0, tiled=True)  20.6 us
    pallas_call x1, Pallas kernels, local_delta(): pl.pallas_call(delta_kernel, grid=(seq // rows,), in_specs=[pl.BlockSpec(...  14.5 us
    ppermute x6, waiting for transfers between devices, shards(): lax.ppermute(a, 'exp', [(i, (i + 2 * by) % n_exp) for i in range(n_exp)])  7.68 us
    pallas_call x3, Pallas kernels, project(): pl.pallas_call(kernel, in_specs=[whole] * 4, out_specs=[whole] * len(out_...  7.45 us
  transfers between devices with their start and end apart: 9, of which 5 were waited for; matrix products, arithmetic and copies ran while one was open for 1% of the time, Pallas kernels for 7%

profile of v6, /device:TPU:1, one launch (start us, length us, event | category | flops | bytes accessed | tf_op | source)
XLA Modules:
  0.0 368.0 jit_solution(4510433829567394394)
XLA Ops:
  0.6 0.0 copy-start.7
  0.6 0.0 copy-start.8
  0.7 1.5 collective-permute-start.1
  2.2 1.4 copy.26
  3.5 0.0 copy-start.12
  3.5 1.3 copy_bitcast_fusion.2
  4.9 0.0 copy-done.7
  4.9 0.0 copy-done.8
  4.9 14.5 %delta_local.1 = (bf16[4,1024,128]{2,1,0:T(8,128)(2,1)}, bf16[4,1024,128]{2,1,0:T(8,128)(2,1)}, bf16[4,4,160,128]{3,2,1,0:T(8,128)(2,1)S(1)}) custom-call(f32[4,1024]{1,0:T(4,128)S(1)} %copy-done.7, f32[4,1024]{1,0:T(4,128)S(1)} %copy-done.8, bf16[2,1024,128]{2,1,0:T(8,128)(2,1)S(1)} %get-tuple-element.31.q_ref, ...), custom_call_target="tpu_custom_call" | custom-call | tf_op jit(solution)/shard_map/delta_local/pallas_call | solution.py:181
  19.4 0.0 copy-start
  19.4 20.6 %all_to_all.20.msg_ref = bf16[16,160,128]{2,1,0:T(8,128)(2,1)S(1)} all-to-all(bf16[16,160,128]{2,1,0:T(8,128)(2,1)S(1)} %bitcast.22), channel_id=1, replica_groups=mesh['ctx'=16,'exp'=8] {'ctx'}, dimensions={0} | all-to-all | bytes 1310720 | tf_op jit(solution)/shard_map/all_to_all | solution.py:513
  40.0 2.5 prefix_states.1
  42.5 3.5 all-to-all-start.1
  46.0 1.4 copy.25
  47.4 5.5 %all-to-all-done.1 = bf16[16,32,128]{2,1,0:T(8,128)(2,1)S(1)} async-done(((bf16[16,32,128]{2,1,0:T(8,128)(2,1)}), bf16[16,32,128]{2,1,0:T(8,128)(2,1)S(1)}, u32[]{:S(2)}, u32[]{:S(2)}) %all-to-all-start.1) | async-done | bytes 131104 | tf_op jit(solution)/shard_map/all_to_all | solution.py:514
  52.9 0.0 copy-done.12
  52.9 0.0 copy-start.4
  52.9 1.2 copy-done.4
  54.1 0.0 copy-start.5
  54.1 1.2 copy-done.5
  55.3 2.6 gated_rows.1
  58.0 2.3 collective-permute-start
  60.3 1.5 collective-permute-done.got_ref
  61.8 0.0 collective-permute-done.1.v_ref
  61.8 0.0 copy-done
  61.8 2.3 project_far.1
  64.1 0.0 copy-start.10
  64.1 1.3 collective-permute-start.2
  65.4 1.5 collective-permute-start.3
  66.9 2.8 project_near.1
  69.7 0.0 copy-start.6
  69.7 0.0 copy-start.9
  69.7 1.3 collective-permute-start.5
  71.1 0.2 collective-permute-start.6
  71.3 1.7 collective-permute-done.2.a_ref
  72.9 0.0 collective-permute-done.3.b_ref
  72.9 0.1 relay.1
  73.0 1.0 collective-permute-start.4
  74.0 1.8 collective-permute-start.7
  75.8 0.0 copy-done.10
  75.8 0.4 slots.1.slot_ref
  76.2 2.3 project_own.1.own_ref
  78.5 0.0 collective-permute-done.5.a1_ref
  78.5 0.4 collective-permute-done.6.b0_ref
  78.9 5.6 %collective-permute-done.4.a0_ref = bf16[64,2048]{1,0:T(8,128)(2,1)S(1)} collective-permute-done((bf16[64,2048]{1,0:T(8,128)(2,1)S(1)}, bf16[64,2048]{1,0:T(8,128)(2,1)S(1)}, u32[]{:S(2)}, u32[]{:S(2)}) %collective-permute-start.4) | collective-permute-done | bytes 262176 | tf_op jit(solution)/shard_map/ppermute | solution.py:504
  84.5 0.0 collective-permute-done.7.b1_ref
  84.5 0.0 copy-done.6
  84.5 0.0 copy-done.9
  84.5 4.3 %dispatch.1 = (bf16[128,2048]{1,0:T(8,128)(2,1)}, bf16[2560,16,128]{2,1,0:T(8,128)(2,1)S(1)}) custom-call(f32[128,2048]{1,0:T(8,128)S(1)} %project_own.1.own_ref, bf16[64,2048]{1,0:T(8,128)(2,1)S(1)} %collective-permute-done.4.a0_ref, bf16[64,2048]{1,0:T(8,128)(2,1)S(1)} %collective-permute-done.5.a1_ref, ...), custom_call_target="tpu_custom_call" | custom-call | tf_op jit(solution)/shard_map/dispatch/pallas_call | solution.py:390
  88.8 0.0 copy-start.1
  88.8 0.0 copy-start.2
  88.8 0.0 copy-start.3
  88.8 126.4 %all_to_all.21.x_ref = bf16[128,2,160,128]{3,2,1,0:T(8,128)(2,1)} all-to-all(bf16[128,2,160,128]{3,2,1,0:T(8,128)(2,1)S(1)} %bitcast.19), channel_id=1, replica_groups=mesh['ctx'=16,'exp'=8] {'ctx','exp'}, dimensions={0} | all-to-all | bytes 20971520 | tf_op jit(solution)/shard_map/all_to_all | solution.py:538
  215.2 0.0 copy-done.1
  215.2 0.0 copy-done.2
  215.2 0.0 copy-done.3
  215.2 23.2 %experts.1 = bf16[128,2,160,128]{3,2,1,0:T(8,128)(2,1)} custom-call(bf16[128,2,160,128]{3,2,1,0:T(8,128)(2,1)} %all_to_all.21.x_ref, bf16[2,2048,512]{2,1,0:T(8,128)(2,1)S(1)} %copy-done.1, bf16[2,2048,512]{2,1,0:T(8,128)(2,1)S(1)} %copy-done.2, bf16[2,512,2048]{2,1,0:T(8,128)(2,1)S(1)} %copy-done.3), custom_call_target="tpu_custom_call" | custom-call | tf_op jit(solution)/shard_map/experts/pallas_call | solution.py:428
  238.4 0.0 copy-start.11
  238.4 125.5 %all_to_all.22 = bf16[128,2,160,128]{3,2,1,0:T(8,128)(2,1)S(1)} all-to-all(bf16[128,2,160,128]{3,2,1,0:T(8,128)(2,1)} %experts.1), channel_id=1, replica_groups=mesh['ctx'=16,'exp'=8] {'ctx','exp'}, dimensions={0} | all-to-all | bytes 20971520 | tf_op jit(solution)/shard_map/all_to_all | solution.py:542
  363.9 0.0 copy-done.11
  363.9 4.1 %combine.1 = bf16[128,2048]{1,0:T(8,128)(2,1)} custom-call(bf16[2560,16,128]{2,1,0:T(8,128)(2,1)S(1)} %bitcast.18, s32[10,128]{1,0:T(8,128)S(1)} %slots.1.slot_ref, f32[10,128]{1,0:T(8,128)S(1)} %bitcast.26), custom_call_target="tpu_custom_call" | custom-call | tf_op jit(solution)/shard_map/combine/pallas_call | solution.py:466
Async XLA Ops:
  0.6 4.2 %copy-start.7 = (f32[4,1024]{1,0:T(4,128)S(1)}, f32[4,1024]{1,0:T(4,128)}, u32[]{:S(2)}) copy-start(f32[4,1024]{1,0:T(4,128)} %decay_ref.1) | copy-start | bytes 49156
  0.6 4.2 %copy-start.8 = (f32[4,1024]{1,0:T(4,128)S(1)}, f32[4,1024]{1,0:T(4,128)}, u32[]{:S(2)}) copy-start(f32[4,1024]{1,0:T(4,128)} %beta_ref.1) | copy-start | bytes 49156
  0.7 61.2 %collective-permute-start.1 = (bf16[512,2048]{1,0:T(8,128)(2,1)}, bf16[512,2048]{1,0:T(8,128)(2,1)}, u32[]{:S(2)}, u32[]{:S(2)}) collective-permute-start(bf16[512,2048]{1,0:T(8,128)(2,1)} %w_ref.5), channel_id=1, source_target_pairs={{0,1},{1,0},{2,3},{3,2},{4,5},{5,4},{6,7},{7,6},{8,9},{9,8},{10,11... | collective-permute-start | bytes 6291464 | tf_op jit(solution)/shard_map/ppermute | solution.py:505
  3.5 49.4 %copy-start.12 = (f32[128]{0:T(128)S(1)}, f32[128]{0:T(128)}, u32[]{:S(2)}) copy-start(f32[128]{0:T(128)} %param.23) | copy-start | bytes 1540
  19.4 42.4 %copy-start = (bf16[512,2048]{1,0:T(8,128)(2,1)S(1)}, bf16[512,2048]{1,0:T(8,128)(2,1)}, u32[]{:S(2)}) copy-start(bf16[512,2048]{1,0:T(8,128)(2,1)} %w_ref.5) | copy-start | bytes 6291460
  42.5 10.4 %all-to-all-start.1 = ((bf16[16,32,128]{2,1,0:T(8,128)(2,1)}), bf16[16,32,128]{2,1,0:T(8,128)(2,1)S(1)}, u32[]{:S(2)}, u32[]{:S(2)}) async-start(bf16[16,32,128]{2,1,0:T(8,128)(2,1)} %prefix_states.1), calls=%async_computation.1 | async-start | bytes 262144 | tf_op jit(solution)/shard_map/all_to_all | solution.py:514
  52.9 1.2 copy-start.4
  54.1 1.2 copy-start.5
  58.0 3.8 %collective-permute-start = (bf16[4,128,512]{2,1,0:T(8,128)(2,1)S(1)}, bf16[4,128,512]{2,1,0:T(8,128)(2,1)S(1)}, u32[]{:S(2)}, u32[]{:S(2)}) collective-permute-start(bf16[4,128,512]{2,1,0:T(8,128)(2,1)S(1)} %get-tuple-element.20), channel_id=1, source_target_pairs={{0,1},{1,0},{2,3},{3,2},{4,5},{5,4},{6,7},{7,6},{8,9},{9,8},{10,11... | collective-permute-start | bytes 1572872 | tf_op jit(solution)/shard_map/ppermute | solution.py:505
  64.1 11.7 %copy-start.10 = (s32[128,10]{0,1:T(8,128)S(1)}, s32[128,10]{0,1:T(8,128)}, u32[]{:S(2)}) copy-start(s32[128,10]{0,1:T(8,128)} %param.28) | copy-start | bytes 15364
  64.1 8.8 %collective-permute-start.2 = (bf16[64,2048]{1,0:T(8,128)(2,1)S(1)}, bf16[64,2048]{1,0:T(8,128)(2,1)S(1)}, u32[]{:S(2)}, u32[]{:S(2)}) collective-permute-start(bf16[64,2048]{1,0:T(8,128)(2,1)S(1)} %get-tuple-element.22), channel_id=1, source_target_pairs={{0,2},{1,3},{2,4},{3,5},{4,6},{5,7},{6,0},{7,1},{8,10},{9,11},{10,... | collective-permute-start | bytes 786440 | tf_op jit(solution)/shard_map/ppermute | solution.py:504
  65.4 7.5 %collective-permute-start.3 = (bf16[64,2048]{1,0:T(8,128)(2,1)S(1)}, bf16[64,2048]{1,0:T(8,128)(2,1)S(1)}, u32[]{:S(2)}, u32[]{:S(2)}) collective-permute-start(bf16[64,2048]{1,0:T(8,128)(2,1)S(1)} %get-tuple-element.23), channel_id=1, source_target_pairs={{0,6},{1,7},{2,0},{3,1},{4,2},{5,3},{6,4},{7,5},{8,14},{9,15},{10,... | collective-permute-start | bytes 786440 | tf_op jit(solution)/shard_map/ppermute | solution.py:504
  69.7 14.8 %copy-start.6 = (bf16[128,2048]{1,0:T(8,128)(2,1)S(1)}, bf16[128,2048]{1,0:T(8,128)(2,1)}, u32[]{:S(2)}) copy-start(bf16[128,2048]{1,0:T(8,128)(2,1)} %res_ref.1) | copy-start | bytes 1572868
  69.7 14.8 %copy-start.9 = (f32[2048]{0:T(1024)S(1)}, f32[2048]{0:T(1024)}, u32[]{:S(2)}) copy-start(f32[2048]{0:T(1024)} %param.24) | copy-start | bytes 24580
  69.7 8.7 %collective-permute-start.5 = (bf16[64,2048]{1,0:T(8,128)(2,1)S(1)}, bf16[64,2048]{1,0:T(8,128)(2,1)S(1)}, u32[]{:S(2)}, u32[]{:S(2)}) collective-permute-start(bf16[64,2048]{1,0:T(8,128)(2,1)S(1)} %get-tuple-element.25), channel_id=1, source_target_pairs={{0,6},{1,7},{2,0},{3,1},{4,2},{5,3},{6,4},{7,5},{8,14},{9,15},{10,... | collective-permute-start | bytes 786440 | tf_op jit(solution)/shard_map/ppermute | solution.py:504
  71.1 7.8 %collective-permute-start.6 = (bf16[64,2048]{1,0:T(8,128)(2,1)S(1)}, bf16[64,2048]{1,0:T(8,128)(2,1)S(1)}, u32[]{:S(2)}, u32[]{:S(2)}) collective-permute-start(bf16[64,2048]{1,0:T(8,128)(2,1)S(1)} %get-tuple-element.26), channel_id=1, source_target_pairs={{0,2},{1,3},{2,4},{3,5},{4,6},{5,7},{6,0},{7,1},{8,10},{9,11},{10,... | collective-permute-start | bytes 786440 | tf_op jit(solution)/shard_map/ppermute | solution.py:504
  73.0 11.4 %collective-permute-start.4 = (bf16[64,2048]{1,0:T(8,128)(2,1)S(1)}, bf16[64,2048]{1,0:T(8,128)(2,1)S(1)}, u32[]{:S(2)}, u32[]{:S(2)}) collective-permute-start(bf16[64,2048]{1,0:T(8,128)(2,1)S(1)} %get-tuple-element.24), channel_id=1, source_target_pairs={{0,2},{1,3},{2,4},{3,5},{4,6},{5,7},{6,0},{7,1},{8,10},{9,11},{10,... | collective-permute-start | bytes 786440 | tf_op jit(solution)/shard_map/ppermute | solution.py:504
  74.0 10.5 %collective-permute-start.7 = (bf16[64,2048]{1,0:T(8,128)(2,1)S(1)}, bf16[64,2048]{1,0:T(8,128)(2,1)S(1)}, u32[]{:S(2)}, u32[]{:S(2)}) collective-permute-start(bf16[64,2048]{1,0:T(8,128)(2,1)S(1)} %get-tuple-element.27), channel_id=1, source_target_pairs={{0,6},{1,7},{2,0},{3,1},{4,2},{5,3},{6,4},{7,5},{8,14},{9,15},{10,... | collective-permute-start | bytes 786440 | tf_op jit(solution)/shard_map/ppermute | solution.py:504
  88.8 126.4 %copy-start.1 = (bf16[2,2048,512]{2,1,0:T(8,128)(2,1)S(1)}, bf16[2,2048,512]{2,1,0:T(8,128)(2,1)}, u32[]{:S(2)}) copy-start(bf16[2,2048,512]{2,1,0:T(8,128)(2,1)} %wg_ref.1) | copy-start | bytes 12582916
  88.8 126.4 %copy-start.2 = (bf16[2,2048,512]{2,1,0:T(8,128)(2,1)S(1)}, bf16[2,2048,512]{2,1,0:T(8,128)(2,1)}, u32[]{:S(2)}) copy-start(bf16[2,2048,512]{2,1,0:T(8,128)(2,1)} %wu_ref.1) | copy-start | bytes 12582916
  88.8 126.4 %copy-start.3 = (bf16[2,512,2048]{2,1,0:T(8,128)(2,1)S(1)}, bf16[2,512,2048]{2,1,0:T(8,128)(2,1)}, u32[]{:S(2)}) copy-start(bf16[2,512,2048]{2,1,0:T(8,128)(2,1)} %wd_ref.1) | copy-start | bytes 12582916
  238.4 125.5 %copy-start.11 = (f32[128,10]{0,1:T(8,128)S(1)}, f32[128,10]{0,1:T(8,128)}, u32[]{:S(2)}) copy-start(f32[128,10]{0,1:T(8,128)} %param.29) | copy-start | bytes 15364

commit v7 on v6

--- a/solution.py
+++ b/solution.py
@@ -60,7 +60,7 @@
     return inverses
 
 
-def delta_kernel(decay_ref, beta_ref, q_ref, k_ref, v_ref, r_ref, o_ref, msg_ref, state_ref):
+def delta_kernel(decay_ref, beta_ref, q_ref, k_ref, v_ref, out_ref, msg_ref, state_ref):
     step = pl.program_id(0)
     heads = v_ref.shape[0]
     group = heads // q_ref.shape[0]
@@ -155,8 +155,7 @@
                 jnp.concatenate([query, mixings[n * heads + h]], axis=1),
                 jnp.concatenate([bases[h], freshes[h]], axis=0),
             )
-            r_ref[h, span] = out[:, :d].astype(BF16)
-            o_ref[h, span] = out[:, d:].astype(BF16)
+            out_ref[h, span] = out.astype(BF16)
     for h in range(heads):
         state_ref[h] = states[h]
 
@@ -189,13 +188,11 @@
             pl.BlockSpec((heads, rows, dv), lambda i: (0, i, 0)),
         ],
         out_specs=[
-            pl.BlockSpec((heads, rows, dk), lambda i: (0, i, 0)),
-            pl.BlockSpec((heads, rows, dv), lambda i: (0, i, 0)),
+            pl.BlockSpec((heads, rows, dk + dv), lambda i: (0, i, 0)),
             pl.BlockSpec((heads, parts, dk + wide, dk), lambda i: (0, 0, 0, 0)),
         ],
         out_shape=[
-            pltpu.HBM((heads, seq, dk), BF16),
-            pltpu.HBM((heads, seq, dv), BF16),
+            pltpu.HBM((heads, seq, dk + dv), BF16),
             jax.ShapeDtypeStruct((heads, parts, dk + wide, dk), BF16),
         ],
         scratch_shapes=[VMEM((heads, dk, dk + dv), F32)],
@@ -228,45 +225,35 @@
     )(msg)
 
 
-def gate_kernel(r_ref, o_ref, s_ref, g_ref, gain_ref, keep_ref, give_ref):
-    heads, _, d = r_ref.shape
-    rows = keep_ref.shape[1]
-    core = lax.axis_index("exp") & 1
-    spans = [pl.ds(pl.multiple_of(part * rows, rows), rows) for part in (core, 1 - core)]
-    each = [(span, h) for span in spans for h in range(heads)]
-    reads = [mxu(r_ref[h, span, :], s_ref[h], ((1,), (1,))) for span, h in each]
-    silus = []
-    for span, h in each:
-        gate = g_ref[h, span, :].astype(F32)
-        silus.append(gate * lax.logistic(gate) * gain_ref[...])
-    values = [o_ref[h, span, :].astype(F32) + read for (span, h), read in zip(each, reads)]
-    scales = [1.0 / jnp.sqrt(jnp.mean(value * value, axis=1, keepdims=True) + 1e-06) for value in values]
-    for n, (value, scale, silu) in enumerate(zip(values, scales, silus)):
-        out_ref, h = (keep_ref, give_ref)[n // heads], n % heads
-        out_ref[0, :, h * d : (h + 1) * d] = (value * scale * silu).astype(BF16)
-
-
-def gated_rows(r, o, states, gate, gain, toks):
-    heads, seq, d = r.shape
-    rows = 2 * toks
-    by_rows = pl.BlockSpec((heads, rows, d), lambda i: (0, i, 0))
-    out = pl.BlockSpec((1, toks, heads * d), lambda i: (i, 0, 0))
-    shape = jax.ShapeDtypeStruct((seq // rows, toks, heads * d), BF16)
-    return pl.pallas_call(
-        gate_kernel,
-        grid=(seq // rows,),
-        in_specs=[
-            by_rows,
-            by_rows,
-            pl.BlockSpec((heads, d, d), lambda i: (0, 0, 0)),
-            by_rows,
-            pl.BlockSpec((1, d), lambda i: (0, 0)),
-        ],
-        out_specs=[out, out],
-        out_shape=[shape, shape],
-        compiler_params=pltpu.CompilerParams(dimension_semantics=("arbitrary",), vmem_limit_bytes=44 * MIB),
-        name="gated_rows",
-    )(r, o, states, gate, gain)
+def gate_kernel(other, ro_ref, s_ref, g_ref, gain_ref, out_ref):
+    heads, d, _ = s_ref.shape
+    chunks, rows, _ = out_ref.shape
+    part = (lax.axis_index("exp") & 1) ^ other
+    for i in range(chunks):
+        span = pl.ds(pl.multiple_of((2 * i + part) * rows, rows), rows)
+        both = [ro_ref[h, span, :] for h in range(heads)]
+        reads = [mxu(both[h][:, :d], s_ref[h], ((1,), (1,))) for h in range(heads)]
+        gates = [g_ref[h, span, :].astype(F32) for h in range(heads)]
+        silus = [gate * lax.logistic(gate) * gain_ref[...] for gate in gates]
+        values = [both[h][:, d:].astype(F32) + reads[h] for h in range(heads)]
+        scales = [1.0 / jnp.sqrt(jnp.mean(value * value, axis=1, keepdims=True) + 1e-06) for value in values]
+        for h in range(heads):
+            out_ref[i, :, h * d : (h + 1) * d] = (values[h] * scales[h] * silus[h]).astype(BF16)
+
+
+def gated_rows(other, ro, states, gate, gain, toks):
+    heads, seq, d = gate.shape
+    whole = pl.BlockSpec(memory_space=VMEM)
+    half = heads * seq * d // 2
+    return pl.pallas_call(
+        functools.partial(gate_kernel, other),
+        in_specs=[whole] * 4,
+        out_specs=whole,
+        out_shape=jax.ShapeDtypeStruct((seq // (2 * toks), toks, heads * d), BF16),
+        cost_estimate=pl.CostEstimate(flops=2 * half * d, bytes_accessed=8 * half, transcendentals=half),
+        compiler_params=pltpu.CompilerParams(vmem_limit_bytes=24 * MIB),
+        name="gated_other" if other else "gated_own",
+    )(ro, states, gate, gain)
 
 
 def chunk_at(step, mine_ref, got_ref):
@@ -508,14 +495,14 @@
     gates = route_gates.T
 
     by_head = lambda a: jnp.transpose(a, (1, 0, 2))
-    reads, local_out, msg = local_delta(
-        decay_logarithm, write_strength, by_head(queries), by_head(key_vectors), by_head(values), parts)
+    local_out, msg = local_delta(
+        decay_logarithm, write_strength, by_head(queries), by_head(key_vectors), by_head(values), parts
+    )
     msg = lax.all_to_all(msg.reshape(n_ctx, dk + wide, dk), "ctx", 0, 0, tiled=True)
     states = lax.all_to_all(prefix_states(msg, wide), "ctx", 0, 0, tiled=True).reshape(heads, dv, dk)
-    mine, give = gated_rows(
-        reads, local_out, states, by_head(out_gate), head_gain.reshape(1, dv), toks
-    )
-    got = swap(give)
+    gating = (local_out, states, by_head(out_gate), head_gain.reshape(1, dv), toks)
+    got = swap(gated_rows(1, *gating))
+    mine = gated_rows(0, *gating)
     half = jax.ShapeDtypeStruct((toks // 2, width), BF16)
     operands = (mine, got, out_weight, other_weight)
     first, second = project(far_kernel, 1, [half, half], "project_far", *operands)

time: 369 us -> 366 us (level)
  no operation moved by 1% of the time
where the time goes in v7:
time: 366 us; the launch traced here: 365 us
  blocking collectives  272 us (74%)
  Pallas kernels  58.5 us (16%)
  waiting for transfers between devices  14.8 us (4%)
  starting transfers between devices  14.5 us (4%)
  local copies, waits for them, and re-layouts  4.49 us (1%)
    all_to_all x1, blocking collectives, shards(): lax.all_to_all(send.reshape(n_dev, local_experts, tall, 128), ('ctx', 'ex...  126 us
    all_to_all x1, blocking collectives, shards(): back = lax.all_to_all(done, ('ctx', 'exp'), 0, 0, tiled=True)  125 us
    pallas_call x1, Pallas kernels, run_experts(): pl.pallas_call(expert_kernel, grid=(local, count // sources), in_specs=[t...  23.2 us
    all_to_all x1, blocking collectives, shards(): lax.all_to_all(msg.reshape(n_ctx, dk + wide, dk), 'ctx', 0, 0, tiled=True)  20.4 us
    pallas_call x1, Pallas kernels, local_delta(): pl.pallas_call(delta_kernel, grid=(seq // rows,), in_specs=[pl.BlockSpec(...  14.5 us
    ppermute x6, waiting for transfers between devices, shards(): lax.ppermute(a, 'exp', [(i, (i + 2 * by) % n_exp) for i in range(n_exp)])  7.63 us
    pallas_call x3, Pallas kernels, project(): pl.pallas_call(kernel, in_specs=[whole] * 4, out_specs=[whole] * len(out_...  7.46 us
  transfers between devices with their start and end apart: 9, of which 5 were waited for; matrix products, arithmetic and copies ran while one was open for 1% of the time, Pallas kernels for 7%

profile of v7, /device:TPU:1, one launch (start us, length us, event | category | flops | bytes accessed | tf_op | source)
XLA Modules:
  0.0 365.3 jit_solution(4936938861530245821)
XLA Ops:
  0.6 0.0 copy-start.6
  0.6 0.0 copy-start.7
  0.7 0.0 copy-start.12
  0.7 1.5 collective-permute-start.1
  2.2 1.4 copy.26
  3.5 0.0 copy-start.11
  3.5 1.3 copy_bitcast_fusion.2
  4.9 0.0 copy-done.6
  4.9 0.0 copy-done.7
  4.9 14.5 %delta_local.1 = (bf16[4,1024,256]{2,1,0:T(8,128)(2,1)}, bf16[4,4,160,128]{3,2,1,0:T(8,128)(2,1)S(1)}) custom-call(f32[4,1024]{1,0:T(4,128)S(1)} %copy-done.6, f32[4,1024]{1,0:T(4,128)S(1)} %copy-done.7, bf16[2,1024,128]{2,1,0:T(8,128)(2,1)S(1)} %get-tuple-element.25.q_ref, bf16[2,1024,128]{2,1,0:T(8,128)(2,1)S(1)} %get-tuple-element.24.k_ref, ...), custom_call_target="tpu_custom_call" | custom-call | tf_op jit(solution)/shard_map/delta_local/pallas_call | solution.py:180
  19.4 20.4 %all_to_all.20.msg_ref = bf16[16,160,128]{2,1,0:T(8,128)(2,1)S(1)} all-to-all(bf16[16,160,128]{2,1,0:T(8,128)(2,1)S(1)} %bitcast.25), channel_id=1, replica_groups=mesh['ctx'=16,'exp'=8] {'ctx'}, dimensions={0} | all-to-all | bytes 1310720 | tf_op jit(solution)/shard_map/all_to_all | solution.py:501
  39.7 2.5 prefix_states.1
  42.3 3.5 all-to-all-start.1
  45.8 0.0 copy-done.12
  45.8 0.1 copy.25
  45.9 0.0 copy-start
  45.9 6.6 %all-to-all-done.1 = bf16[16,32,128]{2,1,0:T(8,128)(2,1)S(1)} async-done(((bf16[16,32,128]{2,1,0:T(8,128)(2,1)}), bf16[16,32,128]{2,1,0:T(8,128)(2,1)S(1)}, u32[]{:S(2)}, u32[]{:S(2)}) %all-to-all-start.1) | async-done | bytes 131104 | tf_op jit(solution)/shard_map/all_to_all | solution.py:502
  52.6 0.0 copy-done.11
  52.6 0.0 copy-start.1
  52.6 1.6 copy-done.1
  54.2 1.0 gated_other.1
  55.2 2.4 collective-permute-start
  57.6 1.0 gated_own.1.mine_ref
  58.6 0.5 collective-permute-done.got_ref
  59.1 0.0 collective-permute-done.1.v_ref
  59.1 0.0 copy-done
  59.1 2.3 project_far.1
  61.5 0.0 copy-start.9
  61.5 1.3 collective-permute-start.2
  62.8 1.5 collective-permute-start.3
  64.3 2.8 project_near.1
  67.1 0.0 copy-start.5
  67.1 0.0 copy-start.8
  67.2 1.3 collective-permute-start.5
  68.4 0.3 collective-permute-start.6
  68.7 1.6 collective-permute-done.2.a_ref
  70.3 0.0 collective-permute-done.3.b_ref
  70.3 0.1 relay.1
  70.4 1.0 collective-permute-start.4
  71.3 1.8 collective-permute-start.7
  73.1 0.0 copy-done.9
  73.1 0.4 slots.1.slot_ref
  73.5 2.3 project_own.1.own_ref
  75.8 0.0 collective-permute-done.5.a1_ref
  75.8 0.4 collective-permute-done.6.b0_ref
  76.2 5.6 %collective-permute-done.4.a0_ref = bf16[64,2048]{1,0:T(8,128)(2,1)S(1)} collective-permute-done((bf16[64,2048]{1,0:T(8,128)(2,1)S(1)}, bf16[64,2048]{1,0:T(8,128)(2,1)S(1)}, u32[]{:S(2)}, u32[]{:S(2)}) %collective-permute-start.4) | collective-permute-done | bytes 262176 | tf_op jit(solution)/shard_map/ppermute | solution.py:491
  81.8 0.0 collective-permute-done.7.b1_ref
  81.8 0.0 copy-done.5
  81.9 0.0 copy-done.8
  81.9 4.3 %dispatch.1 = (bf16[128,2048]{1,0:T(8,128)(2,1)}, bf16[2560,16,128]{2,1,0:T(8,128)(2,1)S(1)}) custom-call(f32[128,2048]{1,0:T(8,128)S(1)} %project_own.1.own_ref, bf16[64,2048]{1,0:T(8,128)(2,1)S(1)} %collective-permute-done.4.a0_ref, bf16[64,2048]{1,0:T(8,128)(2,1)S(1)} %collective-permute-done.5.a1_ref, ...), custom_call_target="tpu_custom_call" | custom-call | tf_op jit(solution)/shard_map/dispatch/pallas_call | solution.py:377
  86.1 0.0 copy-start.2
  86.1 0.0 copy-start.3
  86.1 0.0 copy-start.4
  86.1 126.4 %all_to_all.21.x_ref = bf16[128,2,160,128]{3,2,1,0:T(8,128)(2,1)} all-to-all(bf16[128,2,160,128]{3,2,1,0:T(8,128)(2,1)S(1)} %bitcast.19), channel_id=1, replica_groups=mesh['ctx'=16,'exp'=8] {'ctx','exp'}, dimensions={0} | all-to-all | bytes 20971520 | tf_op jit(solution)/shard_map/all_to_all | solution.py:525
  212.5 0.0 copy-done.2
  212.6 0.0 copy-done.3
  212.6 0.0 copy-done.4
  212.6 23.2 %experts.1 = bf16[128,2,160,128]{3,2,1,0:T(8,128)(2,1)} custom-call(bf16[128,2,160,128]{3,2,1,0:T(8,128)(2,1)} %all_to_all.21.x_ref, bf16[2,2048,512]{2,1,0:T(8,128)(2,1)S(1)} %copy-done.2, bf16[2,2048,512]{2,1,0:T(8,128)(2,1)S(1)} %copy-done.3, bf16[2,512,2048]{2,1,0:T(8,128)(2,1)S(1)} %copy-done.4), custom_call_target="tpu_custom_call" | custom-call | tf_op jit(solution)/shard_map/experts/pallas_call | solution.py:415
  235.7 0.0 copy-start.10
  235.7 125.5 %all_to_all.22 = bf16[128,2,160,128]{3,2,1,0:T(8,128)(2,1)S(1)} all-to-all(bf16[128,2,160,128]{3,2,1,0:T(8,128)(2,1)} %experts.1), channel_id=1, replica_groups=mesh['ctx'=16,'exp'=8] {'ctx','exp'}, dimensions={0} | all-to-all | bytes 20971520 | tf_op jit(solution)/shard_map/all_to_all | solution.py:529
  361.2 0.0 copy-done.10
  361.2 4.1 %combine.1 = bf16[128,2048]{1,0:T(8,128)(2,1)} custom-call(bf16[2560,16,128]{2,1,0:T(8,128)(2,1)S(1)} %bitcast.18, s32[10,128]{1,0:T(8,128)S(1)} %slots.1.slot_ref, f32[10,128]{1,0:T(8,128)S(1)} %bitcast.28), custom_call_target="tpu_custom_call" | custom-call | tf_op jit(solution)/shard_map/combine/pallas_call | solution.py:453
Async XLA Ops:
  0.6 4.3 %copy-start.6 = (f32[4,1024]{1,0:T(4,128)S(1)}, f32[4,1024]{1,0:T(4,128)}, u32[]{:S(2)}) copy-start(f32[4,1024]{1,0:T(4,128)} %decay_ref.1) | copy-start | bytes 49156
  0.6 4.3 %copy-start.7 = (f32[4,1024]{1,0:T(4,128)S(1)}, f32[4,1024]{1,0:T(4,128)}, u32[]{:S(2)}) copy-start(f32[4,1024]{1,0:T(4,128)} %beta_ref.1) | copy-start | bytes 49156
  0.7 45.1 %copy-start.12 = (bf16[1024,4,128]{2,1,0:T(4,128)(2,1)S(1)}, bf16[1024,4,128]{2,1,0:T(4,128)(2,1)}, u32[]{:S(2)}) copy-start(bf16[1024,4,128]{2,1,0:T(4,128)(2,1)} %param.18) | copy-start | bytes 3145732
  0.7 58.5 %collective-permute-start.1 = (bf16[512,2048]{1,0:T(8,128)(2,1)}, bf16[512,2048]{1,0:T(8,128)(2,1)}, u32[]{:S(2)}, u32[]{:S(2)}) collective-permute-start(bf16[512,2048]{1,0:T(8,128)(2,1)} %w_ref.5), channel_id=1, source_target_pairs={{0,1},{1,0},{2,3},{3,2},{4,5},{5,4},{6,7},{7,6},{8,9},{9,8},{10,11... | collective-permute-start | bytes 6291464 | tf_op jit(solution)/shard_map/ppermute | solution.py:492
  3.5 49.1 %copy-start.11 = (f32[128]{0:T(128)S(1)}, f32[128]{0:T(128)}, u32[]{:S(2)}) copy-start(f32[128]{0:T(128)} %param.23) | copy-start | bytes 1540
  42.3 10.3 %all-to-all-start.1 = ((bf16[16,32,128]{2,1,0:T(8,128)(2,1)}), bf16[16,32,128]{2,1,0:T(8,128)(2,1)S(1)}, u32[]{:S(2)}, u32[]{:S(2)}) async-start(bf16[16,32,128]{2,1,0:T(8,128)(2,1)} %prefix_states.1), calls=%async_computation.1 | async-start | bytes 262144 | tf_op jit(solution)/shard_map/all_to_all | solution.py:502
  45.9 13.2 %copy-start = (bf16[512,2048]{1,0:T(8,128)(2,1)S(1)}, bf16[512,2048]{1,0:T(8,128)(2,1)}, u32[]{:S(2)}) copy-start(bf16[512,2048]{1,0:T(8,128)(2,1)} %w_ref.5) | copy-start | bytes 6291460
  52.6 1.6 copy-start.1
  55.2 4.0 %collective-permute-start = (bf16[4,128,512]{2,1,0:T(8,128)(2,1)S(1)}, bf16[4,128,512]{2,1,0:T(8,128)(2,1)S(1)}, u32[]{:S(2)}, u32[]{:S(2)}) collective-permute-start(bf16[4,128,512]{2,1,0:T(8,128)(2,1)S(1)} %gated_other.1), channel_id=1, source_target_pairs={{0,1},{1,0},{2,3},{3,2},{4,5},{5,4},{6,7},{7,6},{8,9},{9,8},{10,11... | collective-permute-start | bytes 1572872 | tf_op jit(solution)/shard_map/ppermute | solution.py:492
  61.5 11.7 %copy-start.9 = (s32[128,10]{0,1:T(8,128)S(1)}, s32[128,10]{0,1:T(8,128)}, u32[]{:S(2)}) copy-start(s32[128,10]{0,1:T(8,128)} %param.28) | copy-start | bytes 15364
  61.5 8.8 %collective-permute-start.2 = (bf16[64,2048]{1,0:T(8,128)(2,1)S(1)}, bf16[64,2048]{1,0:T(8,128)(2,1)S(1)}, u32[]{:S(2)}, u32[]{:S(2)}) collective-permute-start(bf16[64,2048]{1,0:T(8,128)(2,1)S(1)} %get-tuple-element.16), channel_id=1, source_target_pairs={{0,2},{1,3},{2,4},{3,5},{4,6},{5,7},{6,0},{7,1},{8,10},{9,11},{10,... | collective-permute-start | bytes 786440 | tf_op jit(solution)/shard_map/ppermute | solution.py:491
  62.8 7.5 %collective-permute-start.3 = (bf16[64,2048]{1,0:T(8,128)(2,1)S(1)}, bf16[64,2048]{1,0:T(8,128)(2,1)S(1)}, u32[]{:S(2)}, u32[]{:S(2)}) collective-permute-start(bf16[64,2048]{1,0:T(8,128)(2,1)S(1)} %get-tuple-element.17), channel_id=1, source_target_pairs={{0,6},{1,7},{2,0},{3,1},{4,2},{5,3},{6,4},{7,5},{8,14},{9,15},{10,... | collective-permute-start | bytes 786440 | tf_op jit(solution)/shard_map/ppermute | solution.py:491
  67.1 14.7 %copy-start.5 = (bf16[128,2048]{1,0:T(8,128)(2,1)S(1)}, bf16[128,2048]{1,0:T(8,128)(2,1)}, u32[]{:S(2)}) copy-start(bf16[128,2048]{1,0:T(8,128)(2,1)} %res_ref.1) | copy-start | bytes 1572868
  67.1 14.7 %copy-start.8 = (f32[2048]{0:T(1024)S(1)}, f32[2048]{0:T(1024)}, u32[]{:S(2)}) copy-start(f32[2048]{0:T(1024)} %param.24) | copy-start | bytes 24580
  67.2 8.6 %collective-permute-start.5 = (bf16[64,2048]{1,0:T(8,128)(2,1)S(1)}, bf16[64,2048]{1,0:T(8,128)(2,1)S(1)}, u32[]{:S(2)}, u32[]{:S(2)}) collective-permute-start(bf16[64,2048]{1,0:T(8,128)(2,1)S(1)} %get-tuple-element.19), channel_id=1, source_target_pairs={{0,6},{1,7},{2,0},{3,1},{4,2},{5,3},{6,4},{7,5},{8,14},{9,15},{10,... | collective-permute-start | bytes 786440 | tf_op jit(solution)/shard_map/ppermute | solution.py:491
  68.4 7.8 %collective-permute-start.6 = (bf16[64,2048]{1,0:T(8,128)(2,1)S(1)}, bf16[64,2048]{1,0:T(8,128)(2,1)S(1)}, u32[]{:S(2)}, u32[]{:S(2)}) collective-permute-start(bf16[64,2048]{1,0:T(8,128)(2,1)S(1)} %get-tuple-element.20), channel_id=1, source_target_pairs={{0,2},{1,3},{2,4},{3,5},{4,6},{5,7},{6,0},{7,1},{8,10},{9,11},{10,... | collective-permute-start | bytes 786440 | tf_op jit(solution)/shard_map/ppermute | solution.py:491
  70.4 11.5 %collective-permute-start.4 = (bf16[64,2048]{1,0:T(8,128)(2,1)S(1)}, bf16[64,2048]{1,0:T(8,128)(2,1)S(1)}, u32[]{:S(2)}, u32[]{:S(2)}) collective-permute-start(bf16[64,2048]{1,0:T(8,128)(2,1)S(1)} %get-tuple-element.18), channel_id=1, source_target_pairs={{0,2},{1,3},{2,4},{3,5},{4,6},{5,7},{6,0},{7,1},{8,10},{9,11},{10,... | collective-permute-start | bytes 786440 | tf_op jit(solution)/shard_map/ppermute | solution.py:491
  71.3 10.5 %collective-permute-start.7 = (bf16[64,2048]{1,0:T(8,128)(2,1)S(1)}, bf16[64,2048]{1,0:T(8,128)(2,1)S(1)}, u32[]{:S(2)}, u32[]{:S(2)}) collective-permute-start(bf16[64,2048]{1,0:T(8,128)(2,1)S(1)} %get-tuple-element.21), channel_id=1, source_target_pairs={{0,6},{1,7},{2,0},{3,1},{4,2},{5,3},{6,4},{7,5},{8,14},{9,15},{10,... | collective-permute-start | bytes 786440 | tf_op jit(solution)/shard_map/ppermute | solution.py:491
  86.1 126.4 %copy-start.2 = (bf16[2,2048,512]{2,1,0:T(8,128)(2,1)S(1)}, bf16[2,2048,512]{2,1,0:T(8,128)(2,1)}, u32[]{:S(2)}) copy-start(bf16[2,2048,512]{2,1,0:T(8,128)(2,1)} %wg_ref.1) | copy-start | bytes 12582916
  86.1 126.4 %copy-start.3 = (bf16[2,2048,512]{2,1,0:T(8,128)(2,1)S(1)}, bf16[2,2048,512]{2,1,0:T(8,128)(2,1)}, u32[]{:S(2)}) copy-start(bf16[2,2048,512]{2,1,0:T(8,128)(2,1)} %wu_ref.1) | copy-start | bytes 12582916
  86.1 126.4 %copy-start.4 = (bf16[2,512,2048]{2,1,0:T(8,128)(2,1)S(1)}, bf16[2,512,2048]{2,1,0:T(8,128)(2,1)}, u32[]{:S(2)}) copy-start(bf16[2,512,2048]{2,1,0:T(8,128)(2,1)} %wd_ref.1) | copy-start | bytes 12582916
  235.7 125.5 %copy-start.10 = (f32[128,10]{0,1:T(8,128)S(1)}, f32[128,10]{0,1:T(8,128)}, u32[]{:S(2)}) copy-start(f32[128,10]{0,1:T(8,128)} %param.29) | copy-start | bytes 15364

commit v8 on v7

--- a/solution.py
+++ b/solution.py
@@ -60,7 +60,7 @@
     return inverses
 
 
-def delta_kernel(decay_ref, beta_ref, q_ref, k_ref, v_ref, out_ref, msg_ref, state_ref):
+def delta_kernel(decay_ref, beta_ref, q_ref, k_ref, v_ref, left_ref, right_ref, msg_ref, state_ref):
     step = pl.program_id(0)
     heads = v_ref.shape[0]
     group = heads // q_ref.shape[0]
@@ -151,11 +151,9 @@
             qf, q_col = keyed[n * q_ref.shape[0] + h // group][0], keyed[n * q_ref.shape[0] + h // group][2]
             cum_col = columns_of[n][:, h : h + 1]
             query = (qf * (q_col * jnp.exp(cum_col))).astype(BF16)
-            out = mxu(
-                jnp.concatenate([query, mixings[n * heads + h]], axis=1),
-                jnp.concatenate([bases[h], freshes[h]], axis=0),
-            )
-            out_ref[h, span] = out.astype(BF16)
+            left_ref[h, span] = jnp.concatenate([query, mixings[n * heads + h]], axis=1)
+            right_ref[h, pl.ds(2 * n * c, c)] = bases[h]
+            right_ref[h, pl.ds((2 * n + 1) * c, c)] = freshes[h]
     for h in range(heads):
         state_ref[h] = states[h]
 
@@ -188,19 +186,48 @@
             pl.BlockSpec((heads, rows, dv), lambda i: (0, i, 0)),
         ],
         out_specs=[
-            pl.BlockSpec((heads, rows, dk + dv), lambda i: (0, i, 0)),
+            pl.BlockSpec((heads, rows, dk + CHUNK), lambda i: (0, i, 0)),
+            pl.BlockSpec((heads, 2 * rows, dk + dv), lambda i: (0, i, 0)),
             pl.BlockSpec((heads, parts, dk + wide, dk), lambda i: (0, 0, 0, 0)),
         ],
         out_shape=[
-            pltpu.HBM((heads, seq, dk + dv), BF16),
+            pltpu.HBM((heads, seq, dk + CHUNK), BF16),
+            pltpu.HBM((heads, 2 * seq, dk + dv), BF16),
             jax.ShapeDtypeStruct((heads, parts, dk + wide, dk), BF16),
         ],
         scratch_shapes=[VMEM((heads, dk, dk + dv), F32)],
         compiler_params=pltpu.CompilerParams(
-            dimension_semantics=("arbitrary",), vmem_limit_bytes=30 * MIB
+            dimension_semantics=("arbitrary",), vmem_limit_bytes=36 * MIB
         ),
         name="delta_local",
     )(decay, beta, q, k, v)
+
+
+def outputs_kernel(left_ref, right_ref, out_ref):
+    c = CHUNK
+    for n in range(left_ref.shape[1] // c):
+        for h in range(left_ref.shape[0]):
+            span = pl.ds(n * c, c)
+            out_ref[h, span] = mxu(left_ref[h, span], right_ref[h, pl.ds(2 * n * c, 2 * c)]).astype(BF16)
+
+
+def local_outputs(left, right):
+    heads, seq, _ = left.shape
+    width = right.shape[2]
+    rows = 2 * CHUNK
+    by_rows = lambda many, wide: pl.BlockSpec((heads, many, wide), lambda i: (0, i, 0))
+    return pl.pallas_call(
+        outputs_kernel,
+        grid=(seq // rows,),
+        in_specs=[by_rows(rows, left.shape[2]), by_rows(2 * rows, width)],
+        out_specs=by_rows(rows, width),
+        out_shape=pltpu.HBM((heads, seq, width), BF16),
+        cost_estimate=pl.CostEstimate(
+            flops=2 * left.size * width, bytes_accessed=2 * (2 * left.size + right.size), transcendentals=0
+        ),
+        compiler_params=pltpu.CompilerParams(dimension_semantics=("arbitrary",), vmem_limit_bytes=56 * MIB),
+        name="local_outputs",
+    )(left, right)
 
 
 def prefix_kernel(msg_ref, out_ref):
@@ -358,8 +385,8 @@
     attended = (res_ref[...].astype(F32) + total).astype(BF16)
     att_ref[...] = attended
     settled = attended.astype(F32)
-    root = jnp.sqrt(jnp.mean(settled * settled, axis=1, keepdims=True) + 1e-06)
-    normed = settled / root * gain_ref[...]
+    scale = 1.0 / jnp.sqrt(jnp.mean(settled * settled, axis=1, keepdims=True) + 1e-06)
+    normed = settled * scale * gain_ref[...]
     for j in range(pieces):
         flat_ref[pl.ds(j, toks, stride=PITCH), :] = normed[:, j * 128 : (j + 1) * 128]
 
@@ -495,10 +522,11 @@
     gates = route_gates.T
 
     by_head = lambda a: jnp.transpose(a, (1, 0, 2))
-    local_out, msg = local_delta(
+    left_side, right_side, msg = local_delta(
         decay_logarithm, write_strength, by_head(queries), by_head(key_vectors), by_head(values), parts
     )
     msg = lax.all_to_all(msg.reshape(n_ctx, dk + wide, dk), "ctx", 0, 0, tiled=True)
+    local_out = local_outputs(left_side, right_side)
     states = lax.all_to_all(prefix_states(msg, wide), "ctx", 0, 0, tiled=True).reshape(heads, dv, dk)
     gating = (local_out, states, by_head(out_gate), head_gain.reshape(1, dv), toks)
     got = swap(gated_rows(1, *gating))

time: 366 us -> 368 us (level)
  Pallas kernels: 58.5 us -> 64.3 us
  waiting for transfers between devices: 14.8 us -> 9.59 us
    all_to_all x1, waiting for transfers between devices: 6.63 us -> 1.42 us  [shards(): lax.all_to_all(prefix_states(msg, wide), 'ctx', 0, 0, tiled=True)]
    pallas_call x0 -> x1, Pallas kernels: none -> 5.21 us  [local_outputs(): pl.pallas_call(outputs_kernel, grid=(seq // rows,), in_specs=[by_rows(row...]
  transfers between devices with their start and end apart: 9 -> 9, of which waited for: 5 -> 5; matrix products, arithmetic and copies ran while one was open for 1% -> 1% of each run, Pallas kernels for 7% -> 8%
where the time goes in v8:
time: 368 us; the launch traced here: 367 us
  blocking collectives  274 us (74%)
  Pallas kernels  64.3 us (17%)
  starting transfers between devices  14.5 us (4%)
  waiting for transfers between devices  9.59 us (3%)
  local copies, waits for them, and re-layouts  4.49 us (1%)
    all_to_all x1, blocking collectives, shards(): lax.all_to_all(send.reshape(n_dev, local_experts, tall, 128), ('ctx', 'ex...  128 us
    all_to_all x1, blocking collectives, shards(): back = lax.all_to_all(done, ('ctx', 'exp'), 0, 0, tiled=True)  125 us
    pallas_call x1, Pallas kernels, run_experts(): pl.pallas_call(expert_kernel, grid=(local, count // sources), in_specs=[t...  23.2 us
    all_to_all x1, blocking collectives, shards(): lax.all_to_all(msg.reshape(n_ctx, dk + wide, dk), 'ctx', 0, 0, tiled=True)  20.4 us
    pallas_call x1, Pallas kernels, local_delta(): pl.pallas_call(delta_kernel, grid=(seq // rows,), in_specs=[pl.BlockSpec(...  15.1 us
    ppermute x6, waiting for transfers between devices, shards(): lax.ppermute(a, 'exp', [(i, (i + 2 * by) % n_exp) for i in range(n_exp)])  7.63 us
    pallas_call x3, Pallas kernels, project(): pl.pallas_call(kernel, in_specs=[whole] * 4, out_specs=[whole] * len(out_...  7.45 us
  transfers between devices with their start and end apart: 9, of which 5 were waited for; matrix products, arithmetic and copies ran while one was open for 1% of the time, Pallas kernels for 8%

profile of v8, /device:TPU:1, one launch (start us, length us, event | category | flops | bytes accessed | tf_op | source)
XLA Modules:
  0.0 367.4 jit_solution(12477074210136493315)
XLA Ops:
  0.6 0.0 copy-start.6
  0.6 0.0 copy-start.7
  0.7 0.0 copy-start.12
  0.7 1.5 collective-permute-start.1
  2.2 1.4 copy.26
  3.5 1.3 copy_bitcast_fusion.2
  4.9 0.0 copy-done.6
  4.9 0.0 copy-done.7
  4.9 15.1 %delta_local.1 = (bf16[4,1024,256]{2,1,0:T(8,128)(2,1)}, bf16[4,2048,256]{2,1,0:T(8,128)(2,1)}, bf16[4,4,160,128]{3,2,1,0:T(8,128)(2,1)S(1)}) custom-call(f32[4,1024]{1,0:T(4,128)S(1)} %copy-done.6, f32[4,1024]{1,0:T(4,128)S(1)} %copy-done.7, bf16[2,1024,128]{2,1,0:T(8,128)(2,1)S(1)} %get-tuple-element.27.q_ref, ...), custom_call_target="tpu_custom_call" | custom-call | tf_op jit(solution)/shard_map/delta_local/pallas_call | solution.py:178
  20.0 20.4 %all_to_all.20.msg_ref = bf16[16,160,128]{2,1,0:T(8,128)(2,1)S(1)} all-to-all(bf16[16,160,128]{2,1,0:T(8,128)(2,1)S(1)} %bitcast.25), channel_id=1, replica_groups=mesh['ctx'=16,'exp'=8] {'ctx'}, dimensions={0} | all-to-all | bytes 1310720 | tf_op jit(solution)/shard_map/all_to_all | solution.py:528
  40.4 2.5 prefix_states.1
  42.9 3.5 all-to-all-start.1
  46.4 0.0 copy-done.12
  46.4 0.1 copy.25
  46.6 0.0 copy-start.11
  46.6 5.2 %local_outputs.1.ro_ref = bf16[4,1024,256]{2,1,0:T(8,128)(2,1)} custom-call(bf16[4,1024,256]{2,1,0:T(8,128)(2,1)} %get-tuple-element.14.left_ref, bf16[4,2048,256]{2,1,0:T(8,128)(2,1)} %get-tuple-element.15.right_ref), custom_call_target="tpu_custom_call" | custom-call | flops 536870912 | bytes 8388608 | tf_op jit(solution)/shard_map/local_outputs/pallas_call | solution.py:219
  51.8 0.0 copy-start
  51.8 1.4 all-to-all-done.1
  53.2 0.0 copy-done.11
  53.2 0.0 copy-start.1
  53.2 1.6 copy-done.1
  54.8 1.0 gated_other.1
  55.8 2.4 collective-permute-start
  58.2 1.0 gated_own.1.mine_ref
  59.2 0.5 collective-permute-done.got_ref
  59.8 0.0 collective-permute-done.1.v_ref
  59.8 0.0 copy-done
  59.8 2.3 project_far.1
  62.1 0.0 copy-start.9
  62.1 1.3 collective-permute-start.2
  63.4 1.5 collective-permute-start.3
  64.9 2.8 project_near.1
  67.8 0.0 copy-start.5
  67.8 0.0 copy-start.8
  67.8 1.3 collective-permute-start.5
  69.1 0.3 collective-permute-start.6
  69.3 1.6 collective-permute-done.2.a_ref
  70.9 0.0 collective-permute-done.3.b_ref
  70.9 0.1 relay.1
  71.0 0.9 collective-permute-start.4
  71.9 1.8 collective-permute-start.7
  73.7 0.0 copy-done.9
  73.7 0.4 slots.1.slot_ref
  74.1 2.3 project_own.1.own_ref
  76.4 0.0 collective-permute-done.5.a1_ref
  76.4 0.4 collective-permute-done.6.b0_ref
  76.8 5.6 %collective-permute-done.4.a0_ref = bf16[64,2048]{1,0:T(8,128)(2,1)S(1)} collective-permute-done((bf16[64,2048]{1,0:T(8,128)(2,1)S(1)}, bf16[64,2048]{1,0:T(8,128)(2,1)S(1)}, u32[]{:S(2)}, u32[]{:S(2)}) %collective-permute-start.4) | collective-permute-done | bytes 262176 | tf_op jit(solution)/shard_map/ppermute | solution.py:518
  82.5 0.0 collective-permute-done.7.b1_ref
  82.5 0.0 copy-done.5
  82.5 0.0 copy-done.8
  82.5 4.3 %dispatch.1 = (bf16[128,2048]{1,0:T(8,128)(2,1)}, bf16[2560,16,128]{2,1,0:T(8,128)(2,1)S(1)}) custom-call(f32[128,2048]{1,0:T(8,128)S(1)} %project_own.1.own_ref, bf16[64,2048]{1,0:T(8,128)(2,1)S(1)} %collective-permute-done.4.a0_ref, bf16[64,2048]{1,0:T(8,128)(2,1)S(1)} %collective-permute-done.5.a1_ref, ...), custom_call_target="tpu_custom_call" | custom-call | tf_op jit(solution)/shard_map/dispatch/pallas_call | solution.py:404
  86.7 0.0 copy-start.2
  86.7 0.0 copy-start.3
  86.7 0.0 copy-start.4
  86.8 127.8 %all_to_all.21.x_ref = bf16[128,2,160,128]{3,2,1,0:T(8,128)(2,1)} all-to-all(bf16[128,2,160,128]{3,2,1,0:T(8,128)(2,1)S(1)} %bitcast.19), channel_id=1, replica_groups=mesh['ctx'=16,'exp'=8] {'ctx','exp'}, dimensions={0} | all-to-all | bytes 20971520 | tf_op jit(solution)/shard_map/all_to_all | solution.py:553
  214.6 0.0 copy-done.2
  214.6 0.0 copy-done.3
  214.6 0.0 copy-done.4
  214.6 23.2 %experts.1 = bf16[128,2,160,128]{3,2,1,0:T(8,128)(2,1)} custom-call(bf16[128,2,160,128]{3,2,1,0:T(8,128)(2,1)} %all_to_all.21.x_ref, bf16[2,2048,512]{2,1,0:T(8,128)(2,1)S(1)} %copy-done.2, bf16[2,2048,512]{2,1,0:T(8,128)(2,1)S(1)} %copy-done.3, bf16[2,512,2048]{2,1,0:T(8,128)(2,1)S(1)} %copy-done.4), custom_call_target="tpu_custom_call" | custom-call | tf_op jit(solution)/shard_map/experts/pallas_call | solution.py:442
  237.8 0.0 copy-start.10
  237.8 125.5 %all_to_all.22 = bf16[128,2,160,128]{3,2,1,0:T(8,128)(2,1)S(1)} all-to-all(bf16[128,2,160,128]{3,2,1,0:T(8,128)(2,1)} %experts.1), channel_id=1, replica_groups=mesh['ctx'=16,'exp'=8] {'ctx','exp'}, dimensions={0} | all-to-all | bytes 20971520 | tf_op jit(solution)/shard_map/all_to_all | solution.py:557
  363.2 0.0 copy-done.10
  363.3 4.1 %combine.1 = bf16[128,2048]{1,0:T(8,128)(2,1)} custom-call(bf16[2560,16,128]{2,1,0:T(8,128)(2,1)S(1)} %bitcast.18, s32[10,128]{1,0:T(8,128)S(1)} %slots.1.slot_ref, f32[10,128]{1,0:T(8,128)S(1)} %bitcast.28), custom_call_target="tpu_custom_call" | custom-call | tf_op jit(solution)/shard_map/combine/pallas_call | solution.py:480
Async XLA Ops:
  0.6 4.2 %copy-start.6 = (f32[4,1024]{1,0:T(4,128)S(1)}, f32[4,1024]{1,0:T(4,128)}, u32[]{:S(2)}) copy-start(f32[4,1024]{1,0:T(4,128)} %decay_ref.1) | copy-start | bytes 49156
  0.6 4.2 %copy-start.7 = (f32[4,1024]{1,0:T(4,128)S(1)}, f32[4,1024]{1,0:T(4,128)}, u32[]{:S(2)}) copy-start(f32[4,1024]{1,0:T(4,128)} %beta_ref.1) | copy-start | bytes 49156
  0.7 45.8 %copy-start.12 = (bf16[1024,4,128]{2,1,0:T(4,128)(2,1)S(1)}, bf16[1024,4,128]{2,1,0:T(4,128)(2,1)}, u32[]{:S(2)}) copy-start(bf16[1024,4,128]{2,1,0:T(4,128)(2,1)} %param.18) | copy-start | bytes 3145732
  0.7 59.1 %collective-permute-start.1 = (bf16[512,2048]{1,0:T(8,128)(2,1)}, bf16[512,2048]{1,0:T(8,128)(2,1)}, u32[]{:S(2)}, u32[]{:S(2)}) collective-permute-start(bf16[512,2048]{1,0:T(8,128)(2,1)} %w_ref.5), channel_id=1, source_target_pairs={{0,1},{1,0},{2,3},{3,2},{4,5},{5,4},{6,7},{7,6},{8,9},{9,8},{10,11... | collective-permute-start | bytes 6291464 | tf_op jit(solution)/shard_map/ppermute | solution.py:519
  42.9 10.3 %all-to-all-start.1 = ((bf16[16,32,128]{2,1,0:T(8,128)(2,1)}), bf16[16,32,128]{2,1,0:T(8,128)(2,1)S(1)}, u32[]{:S(2)}, u32[]{:S(2)}) async-start(bf16[16,32,128]{2,1,0:T(8,128)(2,1)} %prefix_states.1), calls=%async_computation.1 | async-start | bytes 262144 | tf_op jit(solution)/shard_map/all_to_all | solution.py:530
  46.6 6.6 %copy-start.11 = (f32[128]{0:T(128)S(1)}, f32[128]{0:T(128)}, u32[]{:S(2)}) copy-start(f32[128]{0:T(128)} %param.23) | copy-start | bytes 1540
  51.8 8.0 %copy-start = (bf16[512,2048]{1,0:T(8,128)(2,1)S(1)}, bf16[512,2048]{1,0:T(8,128)(2,1)}, u32[]{:S(2)}) copy-start(bf16[512,2048]{1,0:T(8,128)(2,1)} %w_ref.5) | copy-start | bytes 6291460
  53.2 1.6 copy-start.1
  55.8 3.9 %collective-permute-start = (bf16[4,128,512]{2,1,0:T(8,128)(2,1)S(1)}, bf16[4,128,512]{2,1,0:T(8,128)(2,1)S(1)}, u32[]{:S(2)}, u32[]{:S(2)}) collective-permute-start(bf16[4,128,512]{2,1,0:T(8,128)(2,1)S(1)} %gated_other.1), channel_id=1, source_target_pairs={{0,1},{1,0},{2,3},{3,2},{4,5},{5,4},{6,7},{7,6},{8,9},{9,8},{10,11... | collective-permute-start | bytes 1572872 | tf_op jit(solution)/shard_map/ppermute | solution.py:519
  62.1 11.7 %copy-start.9 = (s32[128,10]{0,1:T(8,128)S(1)}, s32[128,10]{0,1:T(8,128)}, u32[]{:S(2)}) copy-start(s32[128,10]{0,1:T(8,128)} %param.28) | copy-start | bytes 15364
  62.1 8.8 %collective-permute-start.2 = (bf16[64,2048]{1,0:T(8,128)(2,1)S(1)}, bf16[64,2048]{1,0:T(8,128)(2,1)S(1)}, u32[]{:S(2)}, u32[]{:S(2)}) collective-permute-start(bf16[64,2048]{1,0:T(8,128)(2,1)S(1)} %get-tuple-element.18), channel_id=1, source_target_pairs={{0,2},{1,3},{2,4},{3,5},{4,6},{5,7},{6,0},{7,1},{8,10},{9,11},{10,... | collective-permute-start | bytes 786440 | tf_op jit(solution)/shard_map/ppermute | solution.py:518
  63.4 7.5 %collective-permute-start.3 = (bf16[64,2048]{1,0:T(8,128)(2,1)S(1)}, bf16[64,2048]{1,0:T(8,128)(2,1)S(1)}, u32[]{:S(2)}, u32[]{:S(2)}) collective-permute-start(bf16[64,2048]{1,0:T(8,128)(2,1)S(1)} %get-tuple-element.19), channel_id=1, source_target_pairs={{0,6},{1,7},{2,0},{3,1},{4,2},{5,3},{6,4},{7,5},{8,14},{9,15},{10,... | collective-permute-start | bytes 786440 | tf_op jit(solution)/shard_map/ppermute | solution.py:518
  67.8 14.7 %copy-start.5 = (bf16[128,2048]{1,0:T(8,128)(2,1)S(1)}, bf16[128,2048]{1,0:T(8,128)(2,1)}, u32[]{:S(2)}) copy-start(bf16[128,2048]{1,0:T(8,128)(2,1)} %res_ref.1) | copy-start | bytes 1572868
  67.8 14.7 %copy-start.8 = (f32[2048]{0:T(1024)S(1)}, f32[2048]{0:T(1024)}, u32[]{:S(2)}) copy-start(f32[2048]{0:T(1024)} %param.24) | copy-start | bytes 24580
  67.8 8.6 %collective-permute-start.5 = (bf16[64,2048]{1,0:T(8,128)(2,1)S(1)}, bf16[64,2048]{1,0:T(8,128)(2,1)S(1)}, u32[]{:S(2)}, u32[]{:S(2)}) collective-permute-start(bf16[64,2048]{1,0:T(8,128)(2,1)S(1)} %get-tuple-element.21), channel_id=1, source_target_pairs={{0,6},{1,7},{2,0},{3,1},{4,2},{5,3},{6,4},{7,5},{8,14},{9,15},{10,... | collective-permute-start | bytes 786440 | tf_op jit(solution)/shard_map/ppermute | solution.py:518
  69.1 7.8 %collective-permute-start.6 = (bf16[64,2048]{1,0:T(8,128)(2,1)S(1)}, bf16[64,2048]{1,0:T(8,128)(2,1)S(1)}, u32[]{:S(2)}, u32[]{:S(2)}) collective-permute-start(bf16[64,2048]{1,0:T(8,128)(2,1)S(1)} %get-tuple-element.22), channel_id=1, source_target_pairs={{0,2},{1,3},{2,4},{3,5},{4,6},{5,7},{6,0},{7,1},{8,10},{9,11},{10,... | collective-permute-start | bytes 786440 | tf_op jit(solution)/shard_map/ppermute | solution.py:518
  71.0 11.5 %collective-permute-start.4 = (bf16[64,2048]{1,0:T(8,128)(2,1)S(1)}, bf16[64,2048]{1,0:T(8,128)(2,1)S(1)}, u32[]{:S(2)}, u32[]{:S(2)}) collective-permute-start(bf16[64,2048]{1,0:T(8,128)(2,1)S(1)} %get-tuple-element.20), channel_id=1, source_target_pairs={{0,2},{1,3},{2,4},{3,5},{4,6},{5,7},{6,0},{7,1},{8,10},{9,11},{10,... | collective-permute-start | bytes 786440 | tf_op jit(solution)/shard_map/ppermute | solution.py:518
  71.9 10.5 %collective-permute-start.7 = (bf16[64,2048]{1,0:T(8,128)(2,1)S(1)}, bf16[64,2048]{1,0:T(8,128)(2,1)S(1)}, u32[]{:S(2)}, u32[]{:S(2)}) collective-permute-start(bf16[64,2048]{1,0:T(8,128)(2,1)S(1)} %get-tuple-element.23), channel_id=1, source_target_pairs={{0,6},{1,7},{2,0},{3,1},{4,2},{5,3},{6,4},{7,5},{8,14},{9,15},{10,... | collective-permute-start | bytes 786440 | tf_op jit(solution)/shard_map/ppermute | solution.py:518
  86.7 127.9 %copy-start.2 = (bf16[2,2048,512]{2,1,0:T(8,128)(2,1)S(1)}, bf16[2,2048,512]{2,1,0:T(8,128)(2,1)}, u32[]{:S(2)}) copy-start(bf16[2,2048,512]{2,1,0:T(8,128)(2,1)} %wg_ref.1) | copy-start | bytes 12582916
  86.7 127.9 %copy-start.3 = (bf16[2,2048,512]{2,1,0:T(8,128)(2,1)S(1)}, bf16[2,2048,512]{2,1,0:T(8,128)(2,1)}, u32[]{:S(2)}) copy-start(bf16[2,2048,512]{2,1,0:T(8,128)(2,1)} %wu_ref.1) | copy-start | bytes 12582916
  86.7 127.9 %copy-start.4 = (bf16[2,512,2048]{2,1,0:T(8,128)(2,1)S(1)}, bf16[2,512,2048]{2,1,0:T(8,128)(2,1)}, u32[]{:S(2)}) copy-start(bf16[2,512,2048]{2,1,0:T(8,128)(2,1)} %wd_ref.1) | copy-start | bytes 12582916
  237.8 125.5 %copy-start.10 = (f32[128,10]{0,1:T(8,128)S(1)}, f32[128,10]{0,1:T(8,128)}, u32[]{:S(2)}) copy-start(f32[128,10]{0,1:T(8,128)} %param.29) | copy-start | bytes 15364

commit v9 on v7

--- a/solution.py
+++ b/solution.py
@@ -358,8 +358,8 @@
     attended = (res_ref[...].astype(F32) + total).astype(BF16)
     att_ref[...] = attended
     settled = attended.astype(F32)
-    root = jnp.sqrt(jnp.mean(settled * settled, axis=1, keepdims=True) + 1e-06)
-    normed = settled / root * gain_ref[...]
+    scale = 1.0 / jnp.sqrt(jnp.mean(settled * settled, axis=1, keepdims=True) + 1e-06)
+    normed = settled * scale * gain_ref[...]
     for j in range(pieces):
         flat_ref[pl.ds(j, toks, stride=PITCH), :] = normed[:, j * 128 : (j + 1) * 128]
 
@@ -435,7 +435,7 @@
     toks, width = out_ref.shape
     pieces = width // 128
 
-    @pl.loop(0, toks, unroll=4)
+    @pl.loop(0, toks, unroll=16)
     def _(t):
         total = jnp.zeros((pieces, 128), F32)
         for k in range(slot_ref.shape[0]):

time: 366 us -> 366 us (level)
  no operation moved by 1% of the time
where the time goes in v9:
time: 366 us; the launch traced here: 365 us
  blocking collectives  272 us (74%)
  Pallas kernels  58.3 us (16%)
  waiting for transfers between devices  14.8 us (4%)
  starting transfers between devices  14.5 us (4%)
  local copies, waits for them, and re-layouts  4.49 us (1%)
    all_to_all x1, blocking collectives, shards(): lax.all_to_all(send.reshape(n_dev, local_experts, tall, 128), ('ctx', 'ex...  126 us
    all_to_all x1, blocking collectives, shards(): back = lax.all_to_all(done, ('ctx', 'exp'), 0, 0, tiled=True)  125 us
    pallas_call x1, Pallas kernels, run_experts(): pl.pallas_call(expert_kernel, grid=(local, count // sources), in_specs=[t...  23.2 us
    all_to_all x1, blocking collectives, shards(): lax.all_to_all(msg.reshape(n_ctx, dk + wide, dk), 'ctx', 0, 0, tiled=True)  20.4 us
    pallas_call x1, Pallas kernels, local_delta(): pl.pallas_call(delta_kernel, grid=(seq // rows,), in_specs=[pl.BlockSpec(...  14.5 us
    ppermute x6, waiting for transfers between devices, shards(): lax.ppermute(a, 'exp', [(i, (i + 2 * by) % n_exp) for i in range(n_exp)])  7.63 us
    pallas_call x3, Pallas kernels, project(): pl.pallas_call(kernel, in_specs=[whole] * 4, out_specs=[whole] * len(out_...  7.46 us
  transfers between devices with their start and end apart: 9, of which 5 were waited for; matrix products, arithmetic and copies ran while one was open for 1% of the time, Pallas kernels for 7%

profile of v9, /device:TPU:1, one launch (start us, length us, event | category | flops | bytes accessed | tf_op | source)
XLA Modules:
  0.0 365.1 jit_solution(3823902469203819299)
XLA Ops:
  0.6 0.0 copy-start.6
  0.6 0.0 copy-start.7
  0.7 0.0 copy-start.12
  0.7 1.5 collective-permute-start.1
  2.2 1.4 copy.26
  3.5 0.0 copy-start.11
  3.5 1.3 copy_bitcast_fusion.2
  4.9 0.0 copy-done.6
  4.9 0.0 copy-done.7
  4.9 14.5 %delta_local.1 = (bf16[4,1024,256]{2,1,0:T(8,128)(2,1)}, bf16[4,4,160,128]{3,2,1,0:T(8,128)(2,1)S(1)}) custom-call(f32[4,1024]{1,0:T(4,128)S(1)} %copy-done.6, f32[4,1024]{1,0:T(4,128)S(1)} %copy-done.7, bf16[2,1024,128]{2,1,0:T(8,128)(2,1)S(1)} %get-tuple-element.25.q_ref, bf16[2,1024,128]{2,1,0:T(8,128)(2,1)S(1)} %get-tuple-element.24.k_ref, ...), custom_call_target="tpu_custom_call" | custom-call | tf_op jit(solution)/shard_map/delta_local/pallas_call | solution.py:180
  19.4 20.4 %all_to_all.20.msg_ref = bf16[16,160,128]{2,1,0:T(8,128)(2,1)S(1)} all-to-all(bf16[16,160,128]{2,1,0:T(8,128)(2,1)S(1)} %bitcast.25), channel_id=1, replica_groups=mesh['ctx'=16,'exp'=8] {'ctx'}, dimensions={0} | all-to-all | bytes 1310720 | tf_op jit(solution)/shard_map/all_to_all | solution.py:501
  39.7 2.5 prefix_states.1
  42.3 3.5 all-to-all-start.1
  45.8 0.0 copy-done.12
  45.8 0.1 copy.25
  45.9 0.0 copy-start
  45.9 6.6 %all-to-all-done.1 = bf16[16,32,128]{2,1,0:T(8,128)(2,1)S(1)} async-done(((bf16[16,32,128]{2,1,0:T(8,128)(2,1)}), bf16[16,32,128]{2,1,0:T(8,128)(2,1)S(1)}, u32[]{:S(2)}, u32[]{:S(2)}) %all-to-all-start.1) | async-done | bytes 131104 | tf_op jit(solution)/shard_map/all_to_all | solution.py:502
  52.6 0.0 copy-done.11
  52.6 0.0 copy-start.1
  52.6 1.6 copy-done.1
  54.2 1.0 gated_other.1
  55.2 2.4 collective-permute-start
  57.6 1.0 gated_own.1.mine_ref
  58.6 0.5 collective-permute-done.got_ref
  59.1 0.0 collective-permute-done.1.v_ref
  59.1 0.0 copy-done
  59.1 2.3 project_far.1
  61.5 0.0 copy-start.9
  61.5 1.3 collective-permute-start.2
  62.8 1.5 collective-permute-start.3
  64.3 2.8 project_near.1
  67.1 0.0 copy-start.5
  67.1 0.0 copy-start.8
  67.2 1.3 collective-permute-start.5
  68.4 0.3 collective-permute-start.6
  68.7 1.6 collective-permute-done.2.a_ref
  70.3 0.0 collective-permute-done.3.b_ref
  70.3 0.1 relay.1
  70.4 1.0 collective-permute-start.4
  71.3 1.8 collective-permute-start.7
  73.1 0.0 copy-done.9
  73.1 0.4 slots.1.slot_ref
  73.5 2.3 project_own.1.own_ref
  75.8 0.0 collective-permute-done.5.a1_ref
  75.8 0.4 collective-permute-done.6.b0_ref
  76.2 5.6 %collective-permute-done.4.a0_ref = bf16[64,2048]{1,0:T(8,128)(2,1)S(1)} collective-permute-done((bf16[64,2048]{1,0:T(8,128)(2,1)S(1)}, bf16[64,2048]{1,0:T(8,128)(2,1)S(1)}, u32[]{:S(2)}, u32[]{:S(2)}) %collective-permute-start.4) | collective-permute-done | bytes 262176 | tf_op jit(solution)/shard_map/ppermute | solution.py:491
  81.8 0.0 collective-permute-done.7.b1_ref
  81.8 0.0 copy-done.5
  81.9 0.0 copy-done.8
  81.9 4.3 %dispatch.1 = (bf16[128,2048]{1,0:T(8,128)(2,1)}, bf16[2560,16,128]{2,1,0:T(8,128)(2,1)S(1)}) custom-call(f32[128,2048]{1,0:T(8,128)S(1)} %project_own.1.own_ref, bf16[64,2048]{1,0:T(8,128)(2,1)S(1)} %collective-permute-done.4.a0_ref, bf16[64,2048]{1,0:T(8,128)(2,1)S(1)} %collective-permute-done.5.a1_ref, ...), custom_call_target="tpu_custom_call" | custom-call | tf_op jit(solution)/shard_map/dispatch/pallas_call | solution.py:377
  86.1 0.0 copy-start.2
  86.1 0.0 copy-start.3
  86.1 0.0 copy-start.4
  86.1 126.4 %all_to_all.21.x_ref = bf16[128,2,160,128]{3,2,1,0:T(8,128)(2,1)} all-to-all(bf16[128,2,160,128]{3,2,1,0:T(8,128)(2,1)S(1)} %bitcast.19), channel_id=1, replica_groups=mesh['ctx'=16,'exp'=8] {'ctx','exp'}, dimensions={0} | all-to-all | bytes 20971520 | tf_op jit(solution)/shard_map/all_to_all | solution.py:525
  212.5 0.0 copy-done.2
  212.6 0.0 copy-done.3
  212.6 0.0 copy-done.4
  212.6 23.2 %experts.1 = bf16[128,2,160,128]{3,2,1,0:T(8,128)(2,1)} custom-call(bf16[128,2,160,128]{3,2,1,0:T(8,128)(2,1)} %all_to_all.21.x_ref, bf16[2,2048,512]{2,1,0:T(8,128)(2,1)S(1)} %copy-done.2, bf16[2,2048,512]{2,1,0:T(8,128)(2,1)S(1)} %copy-done.3, bf16[2,512,2048]{2,1,0:T(8,128)(2,1)S(1)} %copy-done.4), custom_call_target="tpu_custom_call" | custom-call | tf_op jit(solution)/shard_map/experts/pallas_call | solution.py:415
  235.7 0.0 copy-start.10
  235.7 125.5 %all_to_all.22 = bf16[128,2,160,128]{3,2,1,0:T(8,128)(2,1)S(1)} all-to-all(bf16[128,2,160,128]{3,2,1,0:T(8,128)(2,1)} %experts.1), channel_id=1, replica_groups=mesh['ctx'=16,'exp'=8] {'ctx','exp'}, dimensions={0} | all-to-all | bytes 20971520 | tf_op jit(solution)/shard_map/all_to_all | solution.py:529
  361.2 0.0 copy-done.10
  361.2 3.9 %combine.1 = bf16[128,2048]{1,0:T(8,128)(2,1)} custom-call(bf16[2560,16,128]{2,1,0:T(8,128)(2,1)S(1)} %bitcast.18, s32[10,128]{1,0:T(8,128)S(1)} %slots.1.slot_ref, f32[10,128]{1,0:T(8,128)S(1)} %bitcast.28), custom_call_target="tpu_custom_call" | custom-call | tf_op jit(solution)/shard_map/combine/pallas_call | solution.py:453
Async XLA Ops:
  0.6 4.3 %copy-start.6 = (f32[4,1024]{1,0:T(4,128)S(1)}, f32[4,1024]{1,0:T(4,128)}, u32[]{:S(2)}) copy-start(f32[4,1024]{1,0:T(4,128)} %decay_ref.1) | copy-start | bytes 49156
  0.6 4.3 %copy-start.7 = (f32[4,1024]{1,0:T(4,128)S(1)}, f32[4,1024]{1,0:T(4,128)}, u32[]{:S(2)}) copy-start(f32[4,1024]{1,0:T(4,128)} %beta_ref.1) | copy-start | bytes 49156
  0.7 45.1 %copy-start.12 = (bf16[1024,4,128]{2,1,0:T(4,128)(2,1)S(1)}, bf16[1024,4,128]{2,1,0:T(4,128)(2,1)}, u32[]{:S(2)}) copy-start(bf16[1024,4,128]{2,1,0:T(4,128)(2,1)} %param.18) | copy-start | bytes 3145732
  0.7 58.5 %collective-permute-start.1 = (bf16[512,2048]{1,0:T(8,128)(2,1)}, bf16[512,2048]{1,0:T(8,128)(2,1)}, u32[]{:S(2)}, u32[]{:S(2)}) collective-permute-start(bf16[512,2048]{1,0:T(8,128)(2,1)} %w_ref.5), channel_id=1, source_target_pairs={{0,1},{1,0},{2,3},{3,2},{4,5},{5,4},{6,7},{7,6},{8,9},{9,8},{10,11... | collective-permute-start | bytes 6291464 | tf_op jit(solution)/shard_map/ppermute | solution.py:492
  3.5 49.1 %copy-start.11 = (f32[128]{0:T(128)S(1)}, f32[128]{0:T(128)}, u32[]{:S(2)}) copy-start(f32[128]{0:T(128)} %param.23) | copy-start | bytes 1540
  42.3 10.3 %all-to-all-start.1 = ((bf16[16,32,128]{2,1,0:T(8,128)(2,1)}), bf16[16,32,128]{2,1,0:T(8,128)(2,1)S(1)}, u32[]{:S(2)}, u32[]{:S(2)}) async-start(bf16[16,32,128]{2,1,0:T(8,128)(2,1)} %prefix_states.1), calls=%async_computation.1 | async-start | bytes 262144 | tf_op jit(solution)/shard_map/all_to_all | solution.py:502
  45.9 13.2 %copy-start = (bf16[512,2048]{1,0:T(8,128)(2,1)S(1)}, bf16[512,2048]{1,0:T(8,128)(2,1)}, u32[]{:S(2)}) copy-start(bf16[512,2048]{1,0:T(8,128)(2,1)} %w_ref.5) | copy-start | bytes 6291460
  52.6 1.6 copy-start.1
  55.2 4.0 %collective-permute-start = (bf16[4,128,512]{2,1,0:T(8,128)(2,1)S(1)}, bf16[4,128,512]{2,1,0:T(8,128)(2,1)S(1)}, u32[]{:S(2)}, u32[]{:S(2)}) collective-permute-start(bf16[4,128,512]{2,1,0:T(8,128)(2,1)S(1)} %gated_other.1), channel_id=1, source_target_pairs={{0,1},{1,0},{2,3},{3,2},{4,5},{5,4},{6,7},{7,6},{8,9},{9,8},{10,11... | collective-permute-start | bytes 1572872 | tf_op jit(solution)/shard_map/ppermute | solution.py:492
  61.5 11.7 %copy-start.9 = (s32[128,10]{0,1:T(8,128)S(1)}, s32[128,10]{0,1:T(8,128)}, u32[]{:S(2)}) copy-start(s32[128,10]{0,1:T(8,128)} %param.28) | copy-start | bytes 15364
  61.5 8.8 %collective-permute-start.2 = (bf16[64,2048]{1,0:T(8,128)(2,1)S(1)}, bf16[64,2048]{1,0:T(8,128)(2,1)S(1)}, u32[]{:S(2)}, u32[]{:S(2)}) collective-permute-start(bf16[64,2048]{1,0:T(8,128)(2,1)S(1)} %get-tuple-element.16), channel_id=1, source_target_pairs={{0,2},{1,3},{2,4},{3,5},{4,6},{5,7},{6,0},{7,1},{8,10},{9,11},{10,... | collective-permute-start | bytes 786440 | tf_op jit(solution)/shard_map/ppermute | solution.py:491
  62.8 7.5 %collective-permute-start.3 = (bf16[64,2048]{1,0:T(8,128)(2,1)S(1)}, bf16[64,2048]{1,0:T(8,128)(2,1)S(1)}, u32[]{:S(2)}, u32[]{:S(2)}) collective-permute-start(bf16[64,2048]{1,0:T(8,128)(2,1)S(1)} %get-tuple-element.17), channel_id=1, source_target_pairs={{0,6},{1,7},{2,0},{3,1},{4,2},{5,3},{6,4},{7,5},{8,14},{9,15},{10,... | collective-permute-start | bytes 786440 | tf_op jit(solution)/shard_map/ppermute | solution.py:491
  67.1 14.7 %copy-start.5 = (bf16[128,2048]{1,0:T(8,128)(2,1)S(1)}, bf16[128,2048]{1,0:T(8,128)(2,1)}, u32[]{:S(2)}) copy-start(bf16[128,2048]{1,0:T(8,128)(2,1)} %res_ref.1) | copy-start | bytes 1572868
  67.1 14.7 %copy-start.8 = (f32[2048]{0:T(1024)S(1)}, f32[2048]{0:T(1024)}, u32[]{:S(2)}) copy-start(f32[2048]{0:T(1024)} %param.24) | copy-start | bytes 24580
  67.2 8.6 %collective-permute-start.5 = (bf16[64,2048]{1,0:T(8,128)(2,1)S(1)}, bf16[64,2048]{1,0:T(8,128)(2,1)S(1)}, u32[]{:S(2)}, u32[]{:S(2)}) collective-permute-start(bf16[64,2048]{1,0:T(8,128)(2,1)S(1)} %get-tuple-element.19), channel_id=1, source_target_pairs={{0,6},{1,7},{2,0},{3,1},{4,2},{5,3},{6,4},{7,5},{8,14},{9,15},{10,... | collective-permute-start | bytes 786440 | tf_op jit(solution)/shard_map/ppermute | solution.py:491
  68.4 7.8 %collective-permute-start.6 = (bf16[64,2048]{1,0:T(8,128)(2,1)S(1)}, bf16[64,2048]{1,0:T(8,128)(2,1)S(1)}, u32[]{:S(2)}, u32[]{:S(2)}) collective-permute-start(bf16[64,2048]{1,0:T(8,128)(2,1)S(1)} %get-tuple-element.20), channel_id=1, source_target_pairs={{0,2},{1,3},{2,4},{3,5},{4,6},{5,7},{6,0},{7,1},{8,10},{9,11},{10,... | collective-permute-start | bytes 786440 | tf_op jit(solution)/shard_map/ppermute | solution.py:491
  70.4 11.5 %collective-permute-start.4 = (bf16[64,2048]{1,0:T(8,128)(2,1)S(1)}, bf16[64,2048]{1,0:T(8,128)(2,1)S(1)}, u32[]{:S(2)}, u32[]{:S(2)}) collective-permute-start(bf16[64,2048]{1,0:T(8,128)(2,1)S(1)} %get-tuple-element.18), channel_id=1, source_target_pairs={{0,2},{1,3},{2,4},{3,5},{4,6},{5,7},{6,0},{7,1},{8,10},{9,11},{10,... | collective-permute-start | bytes 786440 | tf_op jit(solution)/shard_map/ppermute | solution.py:491
  71.3 10.5 %collective-permute-start.7 = (bf16[64,2048]{1,0:T(8,128)(2,1)S(1)}, bf16[64,2048]{1,0:T(8,128)(2,1)S(1)}, u32[]{:S(2)}, u32[]{:S(2)}) collective-permute-start(bf16[64,2048]{1,0:T(8,128)(2,1)S(1)} %get-tuple-element.21), channel_id=1, source_target_pairs={{0,6},{1,7},{2,0},{3,1},{4,2},{5,3},{6,4},{7,5},{8,14},{9,15},{10,... | collective-permute-start | bytes 786440 | tf_op jit(solution)/shard_map/ppermute | solution.py:491
  86.1 126.4 %copy-start.2 = (bf16[2,2048,512]{2,1,0:T(8,128)(2,1)S(1)}, bf16[2,2048,512]{2,1,0:T(8,128)(2,1)}, u32[]{:S(2)}) copy-start(bf16[2,2048,512]{2,1,0:T(8,128)(2,1)} %wg_ref.1) | copy-start | bytes 12582916
  86.1 126.4 %copy-start.3 = (bf16[2,2048,512]{2,1,0:T(8,128)(2,1)S(1)}, bf16[2,2048,512]{2,1,0:T(8,128)(2,1)}, u32[]{:S(2)}) copy-start(bf16[2,2048,512]{2,1,0:T(8,128)(2,1)} %wu_ref.1) | copy-start | bytes 12582916
  86.1 126.4 %copy-start.4 = (bf16[2,512,2048]{2,1,0:T(8,128)(2,1)S(1)}, bf16[2,512,2048]{2,1,0:T(8,128)(2,1)}, u32[]{:S(2)}) copy-start(bf16[2,512,2048]{2,1,0:T(8,128)(2,1)} %wd_ref.1) | copy-start | bytes 12582916
  235.7 125.5 %copy-start.10 = (f32[128,10]{0,1:T(8,128)S(1)}, f32[128,10]{0,1:T(8,128)}, u32[]{:S(2)}) copy-start(f32[128,10]{0,1:T(8,128)} %param.29) | copy-start | bytes 15364
